TPU v7x, 256 devices: a whole 4x4x8 slice. The times are simulated.
256 devices in a mesh: row: 8 (over z_hi, x), col: 32 (over z_lo, y, core).
Axes of the slice: x: 4, y: 4, z: 8 (z_hi: 2, z_lo: 4; z = z_hi * 4 + z_lo), core: 2. Of those that a mesh axis runs over, the one named last changes fastest.
Arguments:
- contexts: bfloat16 [32768, 128], P(('row', 'col')), may hold values from -8 to 8
- logged_actions: int32 [32768], P(('row', 'col')), may hold values from 0 to 131041
- policy_actions: int32 [32768, 8], P(('row', 'col')), may hold values from 0 to 131041
- rewards: float32 [32768], P(('row', 'col')), may hold values from 0.2 to 2
Outputs:
- weights: float32 [32768, 8], P(('row', 'col'))
- residual: float32 [32768, 8], P(('row', 'col'))
- values: float32 [8], replicated
All inputs are finite; a program needn't handle non-finite values.
Results may differ from a plain program's by a relative error of at most 0.0056.
Values may be sent and summed in bfloat16 or wider, within the bound.
No kernel may reach another device: no remote copies, remote signals or barrier semaphores. Data moves between devices by JAX's collectives and lax.ppermute only.
A program may use at most 64 MiB of HBM per device.

v0:
```python
import math

import jax
import jax.numpy as jnp
from jax import lax
from jax.sharding import PartitionSpec as P

NPOL = 8
NACT = 16
CATALOG = 131042


ridge = 0.1
group_size = 16
stride_base = 1009
phase_step = 0.37
two_pi = 2.0 * math.pi


def action_features(chosen, width):
    levels = jnp.arange(width, dtype=jnp.int32)
    multipliers = 1 + stride_base * levels
    turned = chosen[..., None] * multipliers % CATALOG
    angles = turned.astype(jnp.float32) * (two_pi / CATALOG) + phase_step * levels.astype(
        jnp.float32
    )
    wave_terms = math.sqrt(2.0 / width) * jnp.cos(angles)
    constant_term = jnp.full(wave_terms.shape, 1.0 / math.sqrt(width), jnp.float32)
    return jnp.where(levels == 0, constant_term, wave_terms).astype(jnp.bfloat16)


def select_actions(products, onehot):
    shaped = products.reshape(
        products.shape[:-1] + (products.shape[-1] // onehot.shape[-1], onehot.shape[-1])
    )
    return jnp.sum(shaped * jnp.expand_dims(onehot.astype(jnp.float32), -2), axis=-1)


def kernel_tiles(left_tiles, right_tiles, left_squares, right_squares):
    inner = jnp.einsum("grd,gsd->grs", left_tiles, right_tiles, preferred_element_type=jnp.float32)
    expo = (2.0 * inner - left_squares[:, :, None] - right_squares[:, None, :]) / left_tiles.shape[
        -1
    ]
    return jnp.exp(expo).astype(jnp.bfloat16)


def tile_terms(kernel, left_matrix, right_matrix, left_onehot, right_onehot):
    toward_left = jnp.einsum(
        "grs,gsm->grm", kernel, right_matrix, preferred_element_type=jnp.float32
    )
    toward_right = jnp.einsum(
        "grs,grm->gsm", kernel, left_matrix, preferred_element_type=jnp.float32
    )
    return (select_actions(toward_left, left_onehot), select_actions(toward_right, right_onehot))


def listed_pass(
    left_ctx,
    left_squares,
    left_matrix,
    left_onehot,
    right_ctx,
    right_squares,
    right_matrix,
    right_onehot,
    placed,
    diagonal,
):
    left_count = left_ctx.shape[0]
    tile_rows = left_ctx.shape[1]
    right_count = right_ctx.shape[0]
    policies = left_matrix.shape[-1] // left_onehot.shape[-1]
    flat_placed = placed.reshape(-1)
    flat_diagonal = diagonal.reshape(-1)
    plan = jnp.argsort(1 - flat_placed, stable=True)
    active_count = jnp.sum(flat_placed)
    rounds = (active_count + group_size - 1) // group_size

    def advance(round_index, carried):
        row_sums, column_sums = carried
        picked = lax.dynamic_slice_in_dim(plan, round_index * group_size, group_size)
        left_pick = picked // right_count
        right_pick = picked % right_count
        live_flags = jnp.take(flat_placed, picked).astype(jnp.float32)
        mirror_flags = live_flags * (1 - jnp.take(flat_diagonal, picked)).astype(jnp.float32)
        kernel = kernel_tiles(
            left_ctx[left_pick],
            right_ctx[right_pick],
            left_squares[left_pick],
            right_squares[right_pick],
        )
        toward_left, toward_right = tile_terms(
            kernel,
            left_matrix[left_pick],
            right_matrix[right_pick],
            left_onehot[left_pick],
            right_onehot[right_pick],
        )
        row_sums = row_sums.at[left_pick].add(toward_left * live_flags[:, None, None])
        column_sums = column_sums.at[right_pick].add(toward_right * mirror_flags[:, None, None])
        return (row_sums, column_sums)

    start_rows = jnp.zeros((left_count, tile_rows, policies), jnp.float32)
    start_columns = jnp.zeros((right_count, tile_rows, policies), jnp.float32)
    return lax.fori_loop(0, rounds, advance, (start_rows, start_columns))


def on_device(contexts, logged_actions, policy_actions, rewards):
    tile_rows, feature_count = contexts.shape
    left_count = lax.axis_size("col")
    right_count = lax.axis_size("row")
    factor = NACT / (tile_rows * left_count * right_count)
    own_column = lax.axis_index("col")
    own_row = lax.axis_index("row")
    left_ids = jnp.arange(left_count, dtype=jnp.int32)[:, None]
    right_ids = jnp.arange(right_count, dtype=jnp.int32)[None, :]
    first_owner = own_row * left_count + left_ids
    second_owner = right_ids * left_count + own_column
    parity = (first_owner + second_owner) % 2
    placed = jnp.where(
        first_owner == second_owner, 1, jnp.where(first_owner < second_owner, parity, 1 - parity)
    )
    diagonal = ((left_ids == own_column) & (right_ids == own_row)).astype(jnp.int32)
    left_logged, left_policy = (
        lax.all_gather(logged_actions, "col", axis=0, tiled=True),
        lax.all_gather(policy_actions, "col", axis=0, tiled=True),
    )
    right_logged, right_policy = (
        lax.all_gather(logged_actions, "row", axis=0, tiled=True),
        lax.all_gather(policy_actions, "row", axis=0, tiled=True),
    )
    left_onehot = action_features(left_logged, NACT).reshape(left_count, tile_rows, NACT)
    right_onehot = action_features(right_logged, NACT).reshape(right_count, tile_rows, NACT)
    left_first = action_features(left_policy, NACT).reshape(left_count, tile_rows, NPOL * NACT)
    right_first = action_features(right_policy, NACT).reshape(right_count, tile_rows, NPOL * NACT)
    right_ctx = lax.all_gather(contexts, "row", axis=0, tiled=True).reshape(
        right_count, tile_rows, feature_count
    )
    right_squares = jnp.sum(right_ctx.astype(jnp.float32) ** 2, axis=2)
    left_ctx = lax.all_gather(contexts, "col", axis=0, tiled=True).reshape(
        left_count, tile_rows, feature_count
    )
    left_squares = jnp.sum(left_ctx.astype(jnp.float32) ** 2, axis=2)

    def sweep(left_matrix, right_matrix):
        return listed_pass(
            left_ctx,
            left_squares,
            left_matrix,
            left_onehot,
            right_ctx,
            right_squares,
            right_matrix,
            right_onehot,
            placed,
            diagonal,
        )

    def reduce_terms(toward_left, toward_right):
        mine_left = lax.psum_scatter(toward_left, "col", scatter_dimension=0, tiled=True)
        mine_right = lax.psum_scatter(toward_right, "row", scatter_dimension=0, tiled=True)
        return factor * (mine_left[0] + mine_right[0])

    first_left, first_right = sweep(left_first, right_first)
    right_side = reduce_terms(first_left, first_right)
    right_low = right_side.astype(jnp.bfloat16)
    left_rhs = lax.all_gather(right_low, "col", axis=0, tiled=True).reshape(
        left_count, tile_rows, NPOL
    )
    right_rhs = lax.all_gather(right_low, "row", axis=0, tiled=True).reshape(
        right_count, tile_rows, NPOL
    )
    left_second = (left_onehot[:, :, None, :] * left_rhs[:, :, :, None]).reshape(
        left_count, tile_rows, NPOL * NACT
    )
    right_second = (right_onehot[:, :, None, :] * right_rhs[:, :, :, None]).reshape(
        right_count, tile_rows, NPOL * NACT
    )
    second_left, second_right = sweep(left_second, right_second)
    image = reduce_terms(second_left, second_right) + ridge * right_side
    norm_sums, curvature, reward_sums = lax.psum(
        (
            jnp.sum(right_side * right_side, axis=0),
            jnp.sum(right_side * image, axis=0),
            jnp.sum(rewards[:, None] * right_side, axis=0),
        ),
        ("row", "col"),
    )
    alpha = norm_sums / curvature
    weights = alpha[None, :] * right_side
    residual = right_side - alpha[None, :] * image
    values = alpha * reward_sums / (tile_rows * left_count * right_count)
    return (weights, residual, values)


def solution(mesh):
    placed = (
        P(("row", "col"), None),
        P(("row", "col")),
        P(("row", "col"), None),
        P(("row", "col")),
    )
    return jax.shard_map(
        on_device,
        mesh=mesh,
        in_specs=placed,
        out_specs=(P(("row", "col"), None), P(("row", "col"), None), P()),
        check_vma=False,
    )
```

profile of v0, /device:TPU:1, one launch (start us, length us, event | category | flops | bytes accessed | tf_op | source)
XLA Modules:
  0.0 1289.7 jit_solution(7908967299347687956)
XLA Ops:
  11.6 3.2 sort.19
  14.8 29.4 %all-gather.1 = s32[8,1,128]{2,1,0:T(1,128)S(1)} all-gather(s32[1,1,128]{2,1,0:T(1,128)} %bitcast.113), channel_id=1, replica_groups=mesh['row'=8,'col'=32] {'row'}, dimensions={0}, use_global_device_ids=true | all-gather | bytes 4608 | tf_op jit(solution)/shard_map/all_gather | solution.py:129
  44.2 46.1 %all-gather = s32[32,1,128]{2,1,0:T(1,128)S(1)} all-gather(s32[1,1,128]{2,1,0:T(1,128)} %bitcast.114), channel_id=1, replica_groups=mesh['row'=8,'col'=32] {'col'}, dimensions={0}, use_global_device_ids=true | all-gather | bytes 16896 | tf_op jit(solution)/shard_map/all_gather | solution.py:125
  90.3 37.4 %all_gather.26 = s32[1024,8]{0,1:T(8,128)S(1)} all-gather(s32[128,8]{0,1:T(8,128)} %param.12), channel_id=1, replica_groups=mesh['row'=8,'col'=32] {'row'}, dimensions={0}, use_global_device_ids=true | all-gather | bytes 36864 | tf_op jit(solution)/shard_map/all_gather | solution.py:130
  127.8 44.6 %all_gather.28 = s32[4096,8]{0,1:T(8,128)S(1)} all-gather(s32[128,8]{0,1:T(8,128)} %param.12), channel_id=1, replica_groups=mesh['row'=8,'col'=32] {'col'}, dimensions={0}, use_global_device_ids=true | all-gather | bytes 135168 | tf_op jit(solution)/shard_map/all_gather | solution.py:126
  173.5 37.9 %all_gather.25 = bf16[1024,128]{1,0:T(8,128)(2,1)S(1)} all-gather(bf16[128,128]{1,0:T(8,128)(2,1)} %param.10), channel_id=1, replica_groups=mesh['row'=8,'col'=32] {'row'}, dimensions={0}, use_global_device_ids=true | all-gather | bytes 294912 | tf_op jit(solution)/shard_map/all_gather | solution.py:136
  214.6 266.5 %while.32 = (s32[]{:T(128)}, f32[32,128,8]{1,2,0:T(8,128)S(1)}, f32[8,128,8]{1,2,0:T(8,128)S(1)}, s32[]{:T(128)}, s32[256]{0:T(256)}, /*index=5*/bf16[32,128,128...) while((s32[]{:T(128)}, f32[32,128,8]{1,2,0:T(8,128)S(1)}, ...), condition=%wide.region_9.11_spmd.clone.clone, body=%wide.region_4.10_spmd.clone.clone.sunk | while | flops 213377504 | bytes 27038416 | solution.py:105
  224.0 9.3 fusion.174
  238.1 2.1 fusion.171
  253.6 9.3 fusion.174
  267.7 2.1 fusion.171
  283.2 9.3 fusion.174
  297.3 2.1 fusion.171
  312.8 9.3 fusion.174
  326.9 2.1 fusion.171
  342.3 9.3 fusion.174
  371.9 9.3 fusion.174
  386.1 2.1 fusion.171
  401.5 9.3 fusion.174
  431.1 9.3 fusion.174
  460.7 9.3 fusion.174
  484.7 39.5 %all-reduce.1 = f32[8,128,8]{1,2,0:T(8,128)S(1)} all-reduce(f32[8,128,8]{1,2,0:T(8,128)S(1)} %get-tuple-element.391), channel_id=3, replica_groups=mesh['row'=8,'col'=32] {'row'}, use_global_device_ids=true, to_apply=%region_11.13.clone | all-reduce | flops 8192 | bytes 65536
  524.3 203.3 %all-reduce.8.cloned.1.call-done = f32[32,128,8]{1,2,0:T(8,128)} async-done(((f32[32,128,8]{1,2,0:T(8,128)}), f32[32,128,8]{1,2,0:T(8,128)}) %all-reduce.8.cloned.1.call-update) | async-done | bytes 131088
  727.5 2.5 multiply_convert_fusion
  730.1 39.7 %all_gather.31 = bf16[4096,8]{0,1:T(8,128)(2,1)S(1)} all-gather(bf16[128,8]{0,1:T(8,128)(2,1)S(1)} %get-tuple-element.780), channel_id=1, replica_groups=mesh['row'=8,'col'=32] {'col'}, dimensions={0}, use_global_device_ids=true | all-gather | bytes 67584 | tf_op jit(solution)/shard_map/all_gather | solution.py:167
  769.7 35.1 %all_gather.30 = bf16[1024,8]{0,1:T(8,128)(2,1)S(1)} all-gather(bf16[128,8]{0,1:T(8,128)(2,1)S(1)} %get-tuple-element.780), channel_id=1, replica_groups=mesh['row'=8,'col'=32] {'row'}, dimensions={0}, use_global_device_ids=true | all-gather | bytes 18432 | tf_op jit(solution)/shard_map/all_gather | solution.py:170
  804.8 144.6 %while.33 = (s32[]{:T(128)}, f32[32,128,8]{1,2,0:T(8,128)S(1)}, f32[8,128,8]{1,2,0:T(8,128)S(1)}, s32[]{:T(128)}, s32[256]{0:T(256)}, /*index=5*/bf16[32,128,128...) while((s32[]{:T(128)}, f32[32,128,8]{1,2,0:T(8,128)S(1)}, ...), condition=%wide.region_19.21_spmd.clone.clone, body=%wide.region_14.20_spmd.clone.clone.sunk | while | flops 205513184 | bytes 14005563 | solution.py:105
  950.7 45.4 %all-reduce.3 = f32[8,128,8]{1,2,0:T(8,128)S(1)} all-reduce(f32[8,128,8]{1,2,0:T(8,128)S(1)} %get-tuple-element.393), channel_id=5, replica_groups=mesh['row'=8,'col'=32] {'row'}, use_global_device_ids=true, to_apply=%region_21.23.clone | all-reduce | flops 8192 | bytes 65536
  996.1 204.5 %all-reduce.10.cloned.1.call-done = f32[32,128,8]{1,2,0:T(8,128)} async-done(((f32[32,128,8]{1,2,0:T(8,128)}), f32[32,128,8]{1,2,0:T(8,128)}) %all-reduce.10.cloned.1.call-update) | async-done | bytes 131088
  1200.6 2.1 multiply_reduce_fusion.6
  1202.7 77.4 %all-reduce.4 = (f32[8]{0:T(128)S(1)}, f32[8]{0:T(128)S(1)}, f32[8]{0:T(128)S(1)}) all-reduce(f32[8]{0:T(128)S(1)} %get-tuple-element.680, f32[8]{0:T(128)S(1)} %get-tuple-element.679, f32[8]{0:T(128)S(1)} %get-tuple-element.678), channel_id=1, replica_groups=mesh['row'=8,'col'=32] {'row','col'}, use_global_device_ids=true, to_apply=%region_13.15 | all-reduce | flops 24 | bytes 192 | tf_op jit(solution)/shard_map/psum | solution.py:181
  1280.6 2.6 multiply_subtract_fusion
  (912 shorter events, 325.6 us)
Async XLA Ops:
  7.2 205.5 %all-gather.4.cloned.1.call-start = ((), (), s32[]{:S(2)}) async-start(), calls=%async_computation | async-start | bytes 1081344 | tf_op jit(solution)/shard_map/all_gather | solution.py:140
  7.9 719.6 %all-reduce.8.cloned.1.call-start = ((), (), s32[]{:S(2)}) async-start(), calls=%async_computation.1 | async-start | bytes 262144
  217.5 1.9 copy-start.2
  224.0 10.3 copy-start.6
  224.0 10.4 copy-start.8
  240.2 3.0 copy-start.3
  253.6 10.3 copy-start.6
  253.6 10.4 copy-start.8
  269.8 3.0 copy-start.3
  283.2 10.3 copy-start.6
  283.2 10.4 copy-start.8
  299.4 3.0 copy-start.3
  312.8 10.3 copy-start.6
  312.8 10.4 copy-start.8
  329.0 3.0 copy-start.3
  342.3 10.3 copy-start.6
  342.3 10.4 copy-start.8
  358.6 3.0 copy-start.3
  371.9 10.3 copy-start.6
  371.9 10.4 copy-start.8
  388.2 3.0 copy-start.3
  395.1 1.9 copy-start.2
  401.5 10.3 copy-start.6
  401.5 10.4 copy-start.8
  417.7 3.0 copy-start.3
  431.1 10.3 copy-start.6
  431.1 10.4 copy-start.8
  447.3 3.0 copy-start.3
  460.7 10.3 copy-start.6
  460.7 10.4 copy-start.8
  476.9 3.0 copy-start.3
  481.7 718.9 %all-reduce.10.cloned.1.call-start = ((), (), s32[]{:S(2)}) async-start(), calls=%async_computation.2 | async-start | bytes 262144
  (54 other events, 63.1 us)
Sparse Core Ops, SparseCore 0:
  9.9 63.0 all-gather.3
  481.9 245.6 all-reduce.7
  950.2 250.3 all-reduce.9
where the time goes:
time: 1290 us
  blocking collectives  432 us (33%)
  waiting for transfers between devices  409 us (32%)
  other arithmetic  221 us (17%)
  local copies, waits for them, and re-layouts  183 us (14%)
  matrix products  25.4 us (2%)
  between operations  14.6 us (1%)
    unnamed x5, waiting for transfers between devices  408 us
    convert_element_type x56, other arithmetic, action_features(): jnp.where(levels == 0, constant_term, wave_terms).astype(jnp.bfloat16)  130 us
    unnamed x2, blocking collectives  84.9 us
    psum x1, blocking collectives, on_device(): lax.psum((jnp.sum(right_side * right_side, axis=0), jnp.sum(right_side *...  77.4 us
    all_gather x1, blocking collectives, on_device(): lax.all_gather(logged_actions, 'col', axis=0, tiled=True)  46.1 us
    all_gather x1, blocking collectives, on_device(): lax.all_gather(policy_actions, 'col', axis=0, tiled=True)  44.6 us
    all_gather x1, blocking collectives, on_device(): lax.all_gather(right_low, 'col', axis=0, tiled=True)  39.7 us
    all_gather x1, blocking collectives, on_device(): lax.all_gather(contexts, 'row', axis=0, tiled=True)  37.9 us
  transfers between devices with their start and end apart: 3, of which 2 were waited for; matrix products, arithmetic and copies ran while one was open for 1% of the time, Pallas kernels for 0%

commit v1 on v0

v1 whole, which is shorter than its diff:
```python
import math

import jax
import jax.numpy as jnp
from jax import lax
from jax.experimental import pallas as pl
from jax.experimental.pallas import tpu as pltpu
from jax.sharding import Mesh
from jax.sharding import PartitionSpec as P

NPOL = 8
NACT = 16
CATALOG = 131042
D = 128
TILE = 128

ridge = 0.1
stride_base = 1009
phase_step = 0.37
two_pi = 2.0 * math.pi

SIZES = (("z_hi", 2), ("x", 4), ("z_lo", 4), ("y", 4), ("core", 2))
EVERY = tuple(name for name, _ in SIZES)
PLANE = ("x", "y")
COLUMN = ("z_hi", "z_lo")
PLANES = 16
COLUMNS = 8
LEFT = 2 * PLANES
ROWS = 176
FEAT_AT, CODE_AT = 128, 144
RIGHT_ROWS = 144

f32, bf16, i32 = jnp.float32, jnp.bfloat16, jnp.int32
MIB = 1 << 20


def wrap(product):
    guess = (product.astype(f32) * (1.0 / CATALOG)).astype(i32)
    left = product - guess * CATALOG
    left = jnp.where(left < 0, left + CATALOG, left)
    return jnp.where(left >= CATALOG, left - CATALOG, left)


def cos_sin(turn):
    eighth = (turn.astype(f32) * (4.0 / CATALOG) + 0.5).astype(i32)
    rest = 4 * turn - eighth * CATALOG
    t = rest.astype(f32) * (two_pi / 4 / CATALOG)
    u = t * t
    s = t * (1.0 + u * (-1.0 / 6 + u * (1.0 / 120 + u * (-1.0 / 5040 + u * (1.0 / 362880)))))
    c = 1.0 + u * (-0.5 + u * (1.0 / 24 + u * (-1.0 / 720 + u * (1.0 / 40320))))
    swap = (eighth == 1) | (eighth == 3)
    a = jnp.where(swap, s, c)
    b = jnp.where(swap, c, s)
    a = jnp.where((eighth == 1) | (eighth == 2), -a, a)
    b = jnp.where((eighth == 2) | (eighth == 3), -b, b)
    return a, b


def features(chosen):
    amp = math.sqrt(2.0 / NACT)
    c0, s0 = cos_sin(chosen)
    cz, sz = cos_sin(wrap(chosen * stride_base))
    pc, ps = math.cos(phase_step), math.sin(phase_step)
    zr = cz * pc - sz * ps
    zi = cz * ps + sz * pc
    wr, wi = c0 * amp, s0 * amp
    out = [jnp.full(chosen.shape, 1.0 / math.sqrt(NACT), f32)]
    for _ in range(1, NACT):
        wr, wi = wr * zr - wi * zi, wr * zi + wi * zr
        out.append(wr)
    return out


def prepare(ctx_ref, logged_ref, policy_ref, plane_ref, column_ref):
    feats = features(logged_ref[...])
    logged = jnp.concatenate(feats, axis=0)
    acts = policy_ref[...]
    high = acts >> 16
    middle = (acts >> 8) & 255
    low = acts & 255
    codes = jnp.concatenate([high, middle, low, jnp.zeros_like(low)], axis=0).astype(f32)
    small = jnp.concatenate([logged, codes], axis=0).astype(bf16)
    ctx = ctx_ref[...]
    for i in range(PLANES):
        plane_ref[i, :TILE, :] = ctx
        plane_ref[i, TILE:, :] = small
    for i in range(COLUMNS):
        column_ref[i, :TILE, :] = ctx
        column_ref[i, TILE:, :] = small[:NACT]


SCALE = math.log2(math.e) / D


def first_kernel(own_ref, other_ref, right_ref, kernel_ref, sums_ref, policy, squares, acc):
    step = pl.program_id(0)

    @pl.when(step == 0)
    def _():
        for half, ref in enumerate((own_ref, other_ref)):
            def decode(j, carry):
                codes = ref[j, CODE_AT : CODE_AT + 32, :].astype(f32).astype(i32)
                acts = (codes[0:8] << 16) + (codes[8:16] << 8) + codes[16:24]
                feats = jnp.concatenate(features(acts), axis=0).astype(bf16)
                policy[j, :, half * TILE : (half + 1) * TILE] = feats
                return carry
            lax.fori_loop(0, PLANES, decode, 0, unroll=4)
        for b in range(COLUMNS):
            x = right_ref[b, :TILE, :].astype(f32)
            total = jnp.sum(x * x, axis=1, keepdims=True) * SCALE
            squares[:, b * TILE : (b + 1) * TILE] = jnp.transpose(jnp.broadcast_to(total, (TILE, TILE)))[:8]
        acc[...] = jnp.zeros_like(acc)

    for half, ref in enumerate((own_ref, other_ref)):
        rows = ref[step, :TILE, :]
        wide = rows.astype(f32)
        row_sq = jnp.sum(wide * wide, axis=1, keepdims=True) * SCALE
        for b in range(0, COLUMNS, 2):
            cols = right_ref[b : b + 2, :TILE, :].reshape(2 * TILE, D)
            inner = lax.dot_general(rows, cols, (((1,), (1,)), ((), ())), preferred_element_type=f32)
            span = slice(b * TILE, (b + 2) * TILE)
            expo = (2.0 * SCALE) * inner - row_sq - squares[0:1, span]
            kernel_ref[half * TILE : (half + 1) * TILE, span] = jnp.exp2(expo).astype(bf16)
    acc[...] += jnp.dot(policy[step], kernel_ref[...], preferred_element_type=f32)

    @pl.when(step == pl.num_programs(0) - 1)
    def _():
        for b in range(COLUMNS):
            chosen = right_ref[b, FEAT_AT : FEAT_AT + NACT, :].astype(f32)
            total = jnp.zeros((NPOL, TILE), f32)
            for c in range(NACT):
                total += acc[c * NPOL : (c + 1) * NPOL, b * TILE : (b + 1) * TILE] * chosen[c : c + 1]
            for peer in range(COLUMNS):
                sums_ref[peer, b] = total


def second_kernel(place_ref, kernel_ref, parts_ref, right_ref, own_ref, other_ref, image_ref, side_ref, matched):
    step = pl.program_id(0)
    factor = NACT / (TILE * LEFT * COLUMNS)

    @pl.when(step == 0)
    def _():
        for b in range(COLUMNS):
            total = parts_ref[0, b]
            for peer in range(1, COLUMNS):
                total += parts_ref[peer, b]
            total = total * factor
            side_ref[b] = total
            low = total.astype(bf16).astype(f32)
            chosen = right_ref[b, FEAT_AT : FEAT_AT + NACT, :].astype(f32)
            made = jnp.concatenate([chosen[c : c + 1] * low for c in range(NACT)], axis=0)
            matched[:, b * TILE : (b + 1) * TILE] = made.astype(bf16)

    out = lax.dot_general(matched[...], kernel_ref[...], (((1,), (1,)), ((), ())), preferred_element_type=f32)
    core = place_ref[0]
    for half, ref in enumerate((own_ref, other_ref)):
        chosen = ref[step, FEAT_AT : FEAT_AT + NACT, :].astype(f32)
        total = jnp.zeros((NPOL, TILE), f32)
        for c in range(NACT):
            total += out[c * NPOL : (c + 1) * NPOL, half * TILE : (half + 1) * TILE] * chosen[c : c + 1]
        image_ref[0, jnp.where(core == half, 0, 1)] = total * factor


def third_kernel(place_ref, parts_ref, side_ref, rewards_ref, image_ref, own_ref, sums_ref):
    total = parts_ref[0]
    for i in range(1, LEFT):
        total += parts_ref[i]
    side = side_ref[place_ref[1]]
    image = total + ridge * side
    image_ref[...] = image
    own_ref[...] = side
    lane = lax.broadcasted_iota(i32, (NPOL, TILE), 1)
    row = lax.broadcasted_iota(i32, (NPOL, TILE), 0)
    spread = jnp.zeros((NPOL, TILE), f32)
    for k, value in enumerate((side * side, side * image, rewards_ref[...] * side)):
        spread = jnp.where(lane == row + k * NPOL, jnp.sum(value, axis=1, keepdims=True), spread)
    flat = jnp.sum(spread, axis=0, keepdims=True)
    sums_ref[...] = jnp.broadcast_to(flat, sums_ref.shape)


def last_kernel(sums_ref, image_ref, side_ref, weights_ref, residual_ref, values_ref):
    count = sums_ref.shape[0]
    total = jnp.sum(sums_ref[...], axis=0, keepdims=True)
    lane = lax.broadcasted_iota(i32, (NPOL, TILE), 1)
    row = lax.broadcasted_iota(i32, (NPOL, TILE), 0)
    wide = jnp.broadcast_to(total, (NPOL, TILE))

    def pick(k):
        return jnp.sum(jnp.where(lane == row + k * NPOL, wide, 0.0), axis=1, keepdims=True)

    alpha = pick(0) / pick(1)
    side = side_ref[...]
    weights_ref[...] = alpha * side
    residual_ref[...] = side - alpha * image_ref[...]
    values = alpha * pick(2) / (TILE * count)
    values_ref[...] = jnp.sum(jnp.where(lane == row, values, 0.0), axis=0, keepdims=True)


def params(limit=48 * MIB, grid=False):
    return pltpu.CompilerParams(
        vmem_limit_bytes=limit, dimension_semantics=("arbitrary",) if grid else None
    )


def exchange(value, axes):
    return lax.all_to_all(value, axes, 0, 0)


def on_device(contexts, logged_actions, policy_actions, rewards):
    core = lax.axis_index("core")
    column = lax.axis_index(COLUMN)
    place = jnp.stack([core, column]).astype(i32)
    sds = jax.ShapeDtypeStruct

    plane_send, column_send = pl.pallas_call(
        prepare,
        out_shape=(sds((PLANES, ROWS, D), bf16), sds((COLUMNS, RIGHT_ROWS, D), bf16)),
        compiler_params=params(),
    )(contexts, logged_actions.reshape(1, TILE), policy_actions.T)
    own = exchange(plane_send, PLANE)
    other = lax.ppermute(own, "core", [(0, 1), (1, 0)])
    right = exchange(column_send, COLUMN)

    whole = lambda shape: pl.BlockSpec(shape, lambda i, *_: (0,) * len(shape), pipeline_mode=pl.Buffered(1))
    left_spec, right_spec = whole((PLANES, ROWS, D)), whole((COLUMNS, RIGHT_ROWS, D))
    part_shape = (COLUMNS, COLUMNS, NPOL, TILE)
    width = COLUMNS * TILE
    kernel_spec = pl.BlockSpec((2 * TILE, width), lambda i, *_: (i, 0))
    kernel, first = pl.pallas_call(
        first_kernel,
        grid=(PLANES,),
        in_specs=[left_spec, left_spec, right_spec],
        out_specs=(kernel_spec, pl.BlockSpec(part_shape, lambda i: (0, 0, 0, 0))),
        out_shape=(sds((LEFT * TILE, width), bf16), sds(part_shape, f32)),
        scratch_shapes=[
            pltpu.VMEM((PLANES, TILE, 2 * TILE), bf16),
            pltpu.VMEM((8, width), f32),
            pltpu.VMEM((TILE, width), f32),
        ],
        compiler_params=params(grid=True),
    )(own, other, right)
    parts = exchange(first, COLUMN)

    image_parts, side = pl.pallas_call(
        second_kernel,
        grid_spec=pltpu.PrefetchScalarGridSpec(
            num_scalar_prefetch=1,
            grid=(PLANES,),
            in_specs=[kernel_spec, whole(part_shape), right_spec, left_spec, left_spec],
            out_specs=(
                pl.BlockSpec((1, 2, NPOL, TILE), lambda i, *_: (i, 0, 0, 0)),
                pl.BlockSpec((COLUMNS, NPOL, TILE), lambda i, *_: (0, 0, 0)),
            ),
            scratch_shapes=[pltpu.VMEM((TILE, width), bf16)],
        ),
        out_shape=(sds((PLANES, 2, NPOL, TILE), f32), sds((COLUMNS, NPOL, TILE), f32)),
        compiler_params=params(grid=True),
    )(place, kernel, parts, right, own, other)
    image_parts = exchange(image_parts.reshape(LEFT, NPOL, TILE), PLANE + ("core",))

    count = LEFT * COLUMNS
    vmem = pl.BlockSpec(memory_space=pltpu.VMEM)
    image, own_side, sums = pl.pallas_call(
        third_kernel,
        in_specs=[pl.BlockSpec(memory_space=pltpu.SMEM), vmem, vmem, vmem],
        out_shape=(sds((NPOL, TILE), f32), sds((NPOL, TILE), f32), sds((count, TILE), f32)),
        compiler_params=params(),
    )(place, image_parts, side, rewards.reshape(1, TILE))
    sums = exchange(sums.reshape(count, 1, TILE), EVERY).reshape(count, TILE)
    weights, residual, values = pl.pallas_call(
        last_kernel,
        out_shape=(sds((NPOL, TILE), f32), sds((NPOL, TILE), f32), sds((1, TILE), f32)),
        compiler_params=params(),
    )(sums, image, own_side)
    return weights.T, residual.T, values[0, :NPOL]


def solution(mesh):
    fine = Mesh(mesh.devices.reshape([size for _, size in SIZES]), EVERY)
    return jax.shard_map(
        on_device,
        mesh=fine,
        in_specs=(P(EVERY, None), P(EVERY), P(EVERY, None), P(EVERY)),
        out_specs=(P(EVERY, None), P(EVERY, None), P()),
        check_vma=False,
    )
```

time: 1290 us -> 119 us (0.09)
  waiting for transfers between devices: 409 us -> 10.4 us
  blocking collectives: 432 us -> 71.6 us
  other arithmetic: 221 us -> 0.08 us
  local copies, waits for them, and re-layouts: 183 us -> 2.61 us
  Pallas kernels: 0 us -> 26.9 us
  matrix products: 25.4 us -> 0 us
  between operations: 14.6 us -> 0.68 us
    unnamed x5 -> x0, waiting for transfers between devices: 408 us -> none
    all_gather x7 -> x0, blocking collectives: 270 us -> none  [the longest x1 46.1 us: on_device(): lax.all_gather(logged_actions, 'col', axis=0, tiled=True)]
    gather x180 -> x0, local copies, waits for them, and re-layouts: 134 us -> none  [the longest x18 33.7 us: advance(): left_ctx[left_pick]]
    convert_element_type x111 -> x0, other arithmetic: 133 us -> none  [the longest x56 130 us: action_features(): jnp.where(levels == 0, constant_term, wave_terms).astype(jnp.bfloat16)]
    unnamed x2 -> x0, blocking collectives: 84.9 us -> none
    psum x1 -> x0, blocking collectives: 77.4 us -> none  [on_device(): lax.psum((jnp.sum(right_side * right_side, axis=0), jnp.sum(right_side *...]
    all_to_all x0 -> x4, blocking collectives: none -> 71.6 us  [exchange(): return lax.all_to_all(value, axes, 0, 0)]
    scatter-add x36 -> x0, other arithmetic: 40.1 us -> none  [the longest x18 20.2 us: advance(): row_sums.at[left_pick].add(toward_left * live_flags[:, None, None])]
  transfers between devices with their start and end apart: 3 -> 2, of which waited for: 2 -> 1; matrix products, arithmetic and copies ran while one was open for 1% -> 0% of each run, Pallas kernels for 0% -> 0%
where the time goes in v1:
time: 119 us; the launch traced here: 118 us
  blocking collectives  71.6 us (60%)
  Pallas kernels  26.9 us (23%)
  waiting for transfers between devices  10.4 us (9%)
  starting transfers between devices  5.64 us (5%)
  local copies, waits for them, and re-layouts  2.61 us (2%)
    all_to_all x4, blocking collectives, exchange(): return lax.all_to_all(value, axes, 0, 0)  71.6 us
    pallas_call x1, Pallas kernels, on_device(): pl.pallas_call(first_kernel, grid=(PLANES,), in_specs=[left_spec, left_sp...  13.3 us
    pallas_call x1, Pallas kernels, on_device(): pl.pallas_call(second_kernel, grid_spec=pltpu.PrefetchScalarGridSpec(num_...  12.1 us
    all_to_all x1, waiting for transfers between devices, exchange(): return lax.all_to_all(value, axes, 0, 0)  10.4 us
    all_to_all x1, starting transfers between devices, exchange(): return lax.all_to_all(value, axes, 0, 0)  3.41 us
  transfers between devices with their start and end apart: 2, of which 1 were waited for; matrix products, arithmetic and copies ran while one was open for 0% of the time, Pallas kernels for 0%

profile of v1, /device:TPU:1, one launch (start us, length us, event | category | flops | bytes accessed | tf_op | source)
XLA Modules:
  0.0 117.9 jit_solution(6032197896149580825)
XLA Ops:
  0.6 0.0 copy-start.3
  0.6 0.0 copy-start
  0.7 0.8 copy-done
  1.4 0.0 copy-start.1
  1.4 0.7 copy-done.1
  2.1 0.0 copy-start.2
  2.1 0.7 copy-done.2
  2.7 0.2 shard_map.67
  2.9 19.5 %all_to_all.25.own_ref = bf16[16,176,128]{2,1,0:T(8,128)(2,1)S(1)} all-to-all(bf16[16,176,128]{2,1,0:T(8,128)(2,1)S(1)} %get-tuple-element.15), channel_id=1, replica_groups=mesh['z_hi'=2,'x'=4,'z_lo'=4,'y'=4,'core'=2] {'x','y'}, dimensions={0} | all-to-all | bytes 1441792 | tf_op jit(solution)/shard_map/all_to_all | solution.py:206
  22.5 2.2 %collective-permute-start = (bf16[16,176,128]{2,1,0:T(8,128)(2,1)S(1)}, bf16[16,176,128]{2,1,0:T(8,128)(2,1)S(1)}, u32[]{:S(2)}, u32[]{:S(2)}) collective-permute-start(bf16[16,176,128]{2,1,0:T(8,128)(2,1)S(1)} %all_to_all.25.own_ref), channel_id=1, source_target_pairs={{0,1},{1,0},{2,3},{3,2},{4,5},{5,4},{6,7},{7,6},{8,9},{9,8},{10,11... | collective-permute-start | bytes 2162696 | tf_op jit(solution)/shard_map/ppermute | solution.py:221
  24.7 20.7 %all_to_all.26.right_ref = bf16[8,144,128]{2,1,0:T(8,128)(2,1)S(1)} all-to-all(bf16[8,144,128]{2,1,0:T(8,128)(2,1)S(1)} %get-tuple-element.16), channel_id=1, replica_groups=mesh['z_hi'=2,'x'=4,'z_lo'=4,'y'=4,'core'=2] {'z_hi','z_lo'}, dimensions={0} | all-to-all | bytes 589824 | tf_op jit(solution)/shard_map/all_to_all | solution.py:206
  45.3 0.0 collective-permute-done.other_ref
  45.3 13.3 %shard_map.68 = (bf16[4096,1024]{1,0:T(8,128)(2,1)}, f32[8,8,8,128]{3,2,1,0:T(8,128)}) custom-call(bf16[16,176,128]{2,1,0:T(8,128)(2,1)S(1)} %all_to_all.25.own_ref, bf16[16,176,128]{2,1,0:T(8,128)(2,1)S(1)} %collective-permute-done.other_ref, bf16[8,144,128]{2,1,0:T(8,128)(2,1)S(1)} %all_to_all.26.right_ref), custom_call_target="tpu_custom_call" | custom-call | tf_op jit(solution)/shard_map/pallas_call | solution.py:229
  58.6 3.4 %all-to-all-start.2 = ((f32[8,8,8,128]{3,2,1,0:T(8,128)}), f32[8,8,8,128]{3,2,1,0:T(8,128)S(1)}, u32[]{:S(2)}, u32[]{:S(2)}) async-start(f32[8,8,8,128]{3,2,1,0:T(8,128)} %get-tuple-element.18), calls=%async_computation.2 | async-start | bytes 524288 | tf_op jit(solution)/shard_map/all_to_all | solution.py:206
  62.0 0.1 pad_add_fusion.place_ref
  62.1 10.4 %all-to-all-done.2.parts_ref = f32[8,8,8,128]{3,2,1,0:T(8,128)S(1)} async-done(((f32[8,8,8,128]{3,2,1,0:T(8,128)}), f32[8,8,8,128]{3,2,1,0:T(8,128)S(1)}, u32[]{:S(2)}, u32[]{:S(2)}) %all-to-all-start.2) | async-done | bytes 262176 | tf_op jit(solution)/shard_map/all_to_all | solution.py:206
  72.5 12.1 %shard_map.69 = (f32[16,2,8,128]{3,2,1,0:T(8,128)S(1)}, f32[8,8,128]{2,1,0:T(8,128)S(1)}) custom-call(s32[2]{0:T(128)S(1)} %pad_add_fusion.place_ref, bf16[4096,1024]{1,0:T(8,128)(2,1)} %get-tuple-element.17.kernel_ref, f32[8,8,8,128]{3,2,1,0:T(8,128)S(1)} %all-to-all-done.2.parts_ref, bf16[8,144,128]{2,1,0:T(8,128)(2,1)S(1)} %all_to_all.26.right_ref, ...), custom_call_target="tpu_custom_call" | custom-call | tf_op jit(solution)/shard_map/pallas_call | solution.py:244
  84.6 13.5 %all_to_all.27.parts_ref = f32[32,8,128]{2,1,0:T(8,128)S(1)} all-to-all(f32[32,8,128]{2,1,0:T(8,128)S(1)} %bitcast.15), channel_id=1, replica_groups=mesh['z_hi'=2,'x'=4,'z_lo'=4,'y'=4,'core'=2] {'x','y','core'}, dimensions={0} | all-to-all | bytes 262144 | tf_op jit(solution)/shard_map/all_to_all | solution.py:206
  98.1 0.0 copy-done.3
  98.1 0.7 shard_map.70
  98.8 17.9 %all_to_all.28 = f32[256,1,128]{2,1,0:T(1,128)S(1)} all-to-all(f32[256,1,128]{2,1,0:T(1,128)S(1)} %bitcast.16), channel_id=1, replica_groups=mesh['z_hi'=2,'x'=4,'z_lo'=4,'y'=4,'core'=2] {'z_hi','x','z_lo','y','core'}, dimensions={0} | all-to-all | bytes 262144 | tf_op jit(solution)/shard_map/all_to_all | solution.py:206
  116.7 0.7 shard_map.71
  117.4 0.5 slice_bitcast_fusion
Async XLA Ops:
  0.6 97.5 %copy-start.3 = (f32[128]{0:T(128)S(1)}, f32[128]{0:T(128)}, u32[]{:S(2)}) copy-start(f32[128]{0:T(128)} %param.7) | copy-start | bytes 1540
  0.6 0.8 copy-start
  1.4 0.7 copy-start.1
  2.1 0.7 copy-start.2
  22.5 22.9 %collective-permute-start = (bf16[16,176,128]{2,1,0:T(8,128)(2,1)S(1)}, bf16[16,176,128]{2,1,0:T(8,128)(2,1)S(1)}, u32[]{:S(2)}, u32[]{:S(2)}) collective-permute-start(bf16[16,176,128]{2,1,0:T(8,128)(2,1)S(1)} %all_to_all.25.own_ref), channel_id=1, source_target_pairs={{0,1},{1,0},{2,3},{3,2},{4,5},{5,4},{6,7},{7,6},{8,9},{9,8},{10,11... | collective-permute-start | bytes 2162696 | tf_op jit(solution)/shard_map/ppermute | solution.py:221
  58.6 13.9 %all-to-all-start.2 = ((f32[8,8,8,128]{3,2,1,0:T(8,128)}), f32[8,8,8,128]{3,2,1,0:T(8,128)S(1)}, u32[]{:S(2)}, u32[]{:S(2)}) async-start(f32[8,8,8,128]{3,2,1,0:T(8,128)} %get-tuple-element.18), calls=%async_computation.2 | async-start | bytes 524288 | tf_op jit(solution)/shard_map/all_to_all | solution.py:206

commit v2 on v1

v2 whole, which is shorter than its diff:
```python
import math

import jax
import jax.numpy as jnp
from jax import lax
from jax.experimental import pallas as pl
from jax.experimental.pallas import tpu as pltpu
from jax.sharding import Mesh
from jax.sharding import PartitionSpec as P

NPOL = 8
NACT = 16
CATALOG = 131042
D = 128
TILE = 128

ridge = 0.1
stride_base = 1009
phase_step = 0.37
two_pi = 2.0 * math.pi

SIZES = (("z_hi", 2), ("x", 4), ("z_lo", 4), ("y", 4), ("core", 2))
EVERY = tuple(name for name, _ in SIZES)
PLANE = ("x", "y")
COLUMN = ("z_hi", "z_lo")
PLANES = 16
COLUMNS = 8
LEFT = 2 * PLANES
ROWS = 160
FEAT_AT, CODE_AT = 128, 144
RIGHT_ROWS = 144

f32, bf16, i32 = jnp.float32, jnp.bfloat16, jnp.int32
MIB = 1 << 20


def wrap(product):
    guess = (product.astype(f32) * (1.0 / CATALOG)).astype(i32)
    left = product - guess * CATALOG
    left = jnp.where(left < 0, left + CATALOG, left)
    return jnp.where(left >= CATALOG, left - CATALOG, left)


def cos_sin(turn):
    eighth = (turn.astype(f32) * (4.0 / CATALOG) + 0.5).astype(i32)
    rest = 4 * turn - eighth * CATALOG
    t = rest.astype(f32) * (two_pi / 4 / CATALOG)
    u = t * t
    s = t * (1.0 + u * (-1.0 / 6 + u * (1.0 / 120 + u * (-1.0 / 5040 + u * (1.0 / 362880)))))
    c = 1.0 + u * (-0.5 + u * (1.0 / 24 + u * (-1.0 / 720 + u * (1.0 / 40320))))
    swap = (eighth == 1) | (eighth == 3)
    a = jnp.where(swap, s, c)
    b = jnp.where(swap, c, s)
    a = jnp.where((eighth == 1) | (eighth == 2), -a, a)
    b = jnp.where((eighth == 2) | (eighth == 3), -b, b)
    return a, b


def features(chosen):
    amp = math.sqrt(2.0 / NACT)
    c0, s0 = cos_sin(chosen)
    cz, sz = cos_sin(wrap(chosen * stride_base))
    pc, ps = math.cos(phase_step), math.sin(phase_step)
    zr = cz * pc - sz * ps
    zi = cz * ps + sz * pc
    wr, wi = c0 * amp, s0 * amp
    out = [jnp.full(chosen.shape, 1.0 / math.sqrt(NACT), f32)]
    for _ in range(1, NACT):
        wr, wi = wr * zr - wi * zi, wr * zi + wi * zr
        out.append(wr)
    return out


def prepare(ctx_hbm, logged_hbm, policy_hbm, plane_ref, column_ref, ctx_ref, logged_ref, policy_ref, sems):
    moves = [
        pltpu.make_async_copy(source, target, sems.at[i])
        for i, (source, target) in enumerate(
            ((ctx_hbm, ctx_ref), (logged_hbm, logged_ref), (policy_hbm, policy_ref))
        )
    ]
    for move in moves:
        move.start()
    for move in moves:
        move.wait()
    logged = jnp.concatenate(features(logged_ref[...]), axis=0)
    acts = policy_ref[...]
    codes = jnp.concatenate([acts >> 9, (acts & 511) - 256], axis=0).astype(f32)
    small = jnp.concatenate([logged, codes], axis=0).astype(bf16)
    ctx = ctx_ref[...]
    for i in range(PLANES):
        plane_ref[i, :TILE, :] = ctx
        plane_ref[i, TILE:, :] = small
    for i in range(COLUMNS):
        column_ref[i, :TILE, :] = ctx
        column_ref[i, TILE:, :] = small[:NACT]


def policy_kernel(own_ref, other_ref, policy_ref):
    for half, ref in enumerate((own_ref, other_ref)):
        for j in range(PLANES):
            codes = ref[j, CODE_AT:ROWS, :].astype(f32).astype(i32)
            acts = (codes[:NPOL] << 9) + codes[NPOL:] + 256
            feats = jnp.concatenate(features(acts), axis=0).astype(bf16)
            policy_ref[:, (2 * j + half) * TILE : (2 * j + half + 1) * TILE] = feats


SCALE = math.log2(math.e) / D
CHUNK = 2


def first_kernel(place_ref, own_ref, other_ref, right_ref, policy_ref, kernel_ref, sums_ref, squares, acc):
    for b in range(COLUMNS):
        x = right_ref[b, :TILE, :].astype(f32)
        total = jnp.sum(x * x, axis=1, keepdims=True) * SCALE
        squares[:, b * TILE : (b + 1) * TILE] = jnp.transpose(jnp.broadcast_to(total, (TILE, TILE)))[:8]
    acc[...] = jnp.zeros_like(acc)

    def rows_of(step, carry):
        for piece in range(CHUNK):
            for half, ref in enumerate((own_ref, other_ref)):
                j = step * CHUNK + piece
                rows = ref[j, :TILE, :]
                wide = rows.astype(f32)
                row_sq = jnp.sum(wide * wide, axis=1, keepdims=True) * SCALE
                at = pl.multiple_of(step * (2 * CHUNK * TILE), 2 * CHUNK * TILE) + (2 * piece + half) * TILE
                for b in range(0, COLUMNS, 2):
                    cols = right_ref[b : b + 2, :TILE, :].reshape(2 * TILE, D)
                    inner = lax.dot_general(rows, cols, (((1,), (1,)), ((), ())), preferred_element_type=f32)
                    span = slice(b * TILE, (b + 2) * TILE)
                    expo = (2.0 * SCALE) * inner - row_sq - squares[0:1, span]
                    kernel_ref[pl.ds(at, TILE), span] = jnp.exp2(expo).astype(bf16)
        start = pl.multiple_of(step * (2 * CHUNK * TILE), 2 * CHUNK * TILE)
        whole = pl.ds(start, 2 * CHUNK * TILE)
        acc[...] += jnp.dot(policy_ref[:, whole], kernel_ref[whole, :], preferred_element_type=f32)
        return carry

    lax.fori_loop(0, PLANES // CHUNK, rows_of, 0)
    for b in range(COLUMNS):
        chosen = right_ref[b, FEAT_AT : FEAT_AT + NACT, :].astype(f32)
        total = jnp.zeros((NPOL, TILE), f32)
        for c in range(NACT):
            total += acc[c * NPOL : (c + 1) * NPOL, b * TILE : (b + 1) * TILE] * chosen[c : c + 1]
        for peer in range(COLUMNS):
            sums_ref[peer, b] = total


def second_kernel(place_ref, kernel_ref, parts_ref, right_ref, own_ref, other_ref, image_ref, side_ref, matched):
    factor = NACT / (TILE * LEFT * COLUMNS)
    for b in range(COLUMNS):
        total = parts_ref[0, b]
        for peer in range(1, COLUMNS):
            total += parts_ref[peer, b]
        total = total * factor
        side_ref[b] = total
        low = total.astype(bf16).astype(f32)
        chosen = right_ref[b, FEAT_AT : FEAT_AT + NACT, :].astype(f32)
        made = jnp.concatenate([chosen[c : c + 1] * low for c in range(NACT)], axis=0)
        matched[:, b * TILE : (b + 1) * TILE] = made.astype(bf16)
    core = place_ref[0]

    def rows_of(step, carry):
        start = pl.multiple_of(step * (2 * CHUNK * TILE), 2 * CHUNK * TILE)
        block = kernel_ref[pl.ds(start, 2 * CHUNK * TILE), :]
        out = lax.dot_general(matched[...], block, (((1,), (1,)), ((), ())), preferred_element_type=f32)
        for piece in range(CHUNK):
            j = step * CHUNK + piece
            for half, ref in enumerate((own_ref, other_ref)):
                chosen = ref[j, FEAT_AT : FEAT_AT + NACT, :].astype(f32)
                at = (2 * piece + half) * TILE
                total = jnp.zeros((NPOL, TILE), f32)
                for c in range(NACT):
                    total += out[c * NPOL : (c + 1) * NPOL, at : at + TILE] * chosen[c : c + 1]
                image_ref[2 * j + jnp.where(core == half, 0, 1)] = total * factor
        return carry

    lax.fori_loop(0, PLANES // CHUNK, rows_of, 0)


def third_kernel(place_ref, parts_ref, side_ref, rewards_ref, image_ref, own_ref, sums_ref):
    total = parts_ref[0]
    for i in range(1, LEFT):
        total += parts_ref[i]
    side = side_ref[place_ref[1]]
    image = total + ridge * side
    image_ref[...] = image
    own_ref[...] = side
    lane = lax.broadcasted_iota(i32, (NPOL, TILE), 1)
    row = lax.broadcasted_iota(i32, (NPOL, TILE), 0)
    spread = jnp.zeros((NPOL, TILE), f32)
    for k, value in enumerate((side * side, side * image, rewards_ref[...] * side)):
        spread = jnp.where(lane == row + k * NPOL, jnp.sum(value, axis=1, keepdims=True), spread)
    flat = jnp.sum(spread, axis=0, keepdims=True)
    sums_ref[...] = jnp.broadcast_to(flat, sums_ref.shape)


def last_kernel(sums_ref, image_ref, side_ref, weights_ref, residual_ref, values_ref):
    count = sums_ref.shape[0]
    total = jnp.sum(sums_ref[...], axis=0, keepdims=True)
    lane = lax.broadcasted_iota(i32, (NPOL, TILE), 1)
    row = lax.broadcasted_iota(i32, (NPOL, TILE), 0)
    wide = jnp.broadcast_to(total, (NPOL, TILE))

    def pick(k):
        return jnp.sum(jnp.where(lane == row + k * NPOL, wide, 0.0), axis=1, keepdims=True)

    alpha = pick(0) / pick(1)
    side = side_ref[...]
    weights_ref[...] = alpha * side
    residual_ref[...] = side - alpha * image_ref[...]
    values = alpha * pick(2) / (TILE * count)
    values_ref[...] = jnp.sum(jnp.where(lane == row, values, 0.0), axis=0, keepdims=True)[:, :NPOL]


def params(limit=32 * MIB):
    return pltpu.CompilerParams(vmem_limit_bytes=limit)


def exchange(value, axes):
    return lax.all_to_all(value, axes, 0, 0)


def on_device(contexts, logged_actions, policy_actions, rewards):
    core = lax.axis_index("core")
    column = lax.axis_index(COLUMN)
    place = jnp.stack([core, column]).astype(i32)
    sds = jax.ShapeDtypeStruct
    vmem = pl.BlockSpec(memory_space=pltpu.VMEM)
    smem = pl.BlockSpec(memory_space=pltpu.SMEM)

    plane_send, column_send = pl.pallas_call(
        prepare,
        in_specs=[pl.BlockSpec(memory_space=pl.ANY)] * 3,
        out_shape=(sds((PLANES, ROWS, D), bf16), sds((COLUMNS, RIGHT_ROWS, D), bf16)),
        scratch_shapes=[
            pltpu.VMEM((TILE, D), bf16),
            pltpu.VMEM((1, TILE), i32),
            pltpu.VMEM((NPOL, TILE), i32),
            pltpu.SemaphoreType.DMA((3,)),
        ],
        compiler_params=params(60 * MIB),
    )(contexts, logged_actions.reshape(1, TILE), policy_actions.T)
    own = exchange(plane_send, PLANE)
    other = lax.ppermute(own, "core", [(0, 1), (1, 0)])
    right = exchange(column_send, COLUMN)

    width = COLUMNS * TILE
    policy = pl.pallas_call(
        policy_kernel,
        out_shape=sds((TILE, LEFT * TILE), bf16),
        cost_estimate=pl.CostEstimate(flops=60_000_000, bytes_accessed=2_000_000, transcendentals=0),
        compiler_params=params(),
    )(own, other)
    kernel, first = pl.pallas_call(
        first_kernel,
        in_specs=[smem] + [vmem] * 4,
        out_shape=(sds((LEFT * TILE, width), bf16), sds((COLUMNS, COLUMNS, NPOL, TILE), f32)),
        scratch_shapes=[pltpu.VMEM((8, width), f32), pltpu.VMEM((TILE, width), f32)],
        compiler_params=params(),
    )(place, own, other, right, policy)
    parts = exchange(first, COLUMN)
    image_parts, side = pl.pallas_call(
        second_kernel,
        in_specs=[smem] + [vmem] * 5,
        out_shape=(sds((LEFT, NPOL, TILE), f32), sds((COLUMNS, NPOL, TILE), f32)),
        scratch_shapes=[pltpu.VMEM((TILE, width), bf16)],
        compiler_params=params(),
    )(place, kernel, parts, right, own, other)
    image_parts = exchange(image_parts, PLANE + ("core",))

    count = LEFT * COLUMNS
    image, own_side, sums = pl.pallas_call(
        third_kernel,
        in_specs=[smem, vmem, vmem, vmem],
        out_shape=(sds((NPOL, TILE), f32), sds((NPOL, TILE), f32), sds((count, TILE), f32)),
        compiler_params=params(),
    )(place, image_parts, side, rewards.reshape(1, TILE))
    sums = exchange(sums.reshape(count, 1, TILE), EVERY).reshape(count, TILE)
    weights, residual, values = pl.pallas_call(
        last_kernel,
        out_shape=(sds((NPOL, TILE), f32), sds((NPOL, TILE), f32), sds((1, NPOL), f32)),
        compiler_params=params(),
    )(sums, image, own_side)
    return weights.T, residual.T, values.reshape(NPOL)


def solution(mesh):
    fine = Mesh(mesh.devices.reshape([size for _, size in SIZES]), EVERY)
    return jax.shard_map(
        on_device,
        mesh=fine,
        in_specs=(P(EVERY, None), P(EVERY), P(EVERY, None), P(EVERY)),
        out_specs=(P(EVERY, None), P(EVERY, None), P()),
        check_vma=False,
    )
```

time: 119 us -> 104 us (0.87)
  Pallas kernels: 26.9 us -> 16.8 us
  blocking collectives: 71.6 us -> 63.6 us
  starting transfers between devices: 5.64 us -> 10.3 us
  local copies, waits for them, and re-layouts: 2.61 us -> 0.01 us
  waiting for transfers between devices: 10.4 us -> 12.1 us
    pallas_call x4 -> x5, Pallas kernels: 26.2 us -> 16.1 us  [the longest x1 8.06 us: on_device(): pl.pallas_call(first_kernel, in_specs=[smem] + [vmem] * 4, out_shape=(sds...]
    all_to_all x4, blocking collectives: 71.6 us -> 63.6 us  [exchange(): return lax.all_to_all(value, axes, 0, 0)]
    all_to_all x1, starting transfers between devices: 3.41 us -> 8.19 us  [exchange(): return lax.all_to_all(value, axes, 0, 0)]
    unnamed x8 -> x2, local copies, waits for them, and re-layouts: 2.1 us -> 0.01 us
    all_to_all x1, waiting for transfers between devices: 10.4 us -> 12.1 us  [exchange(): return lax.all_to_all(value, axes, 0, 0)]
  transfers between devices with their start and end apart: 2 -> 2, of which waited for: 1 -> 1; matrix products, arithmetic and copies ran while one was open for 0% -> 0% of each run, Pallas kernels for 0% -> 1%
where the time goes in v2:
time: 104 us; the launch traced here: 103 us
  blocking collectives  63.6 us (61%)
  Pallas kernels  16.8 us (16%)
  waiting for transfers between devices  12.1 us (12%)
  starting transfers between devices  10.3 us (10%)
    all_to_all x4, blocking collectives, exchange(): return lax.all_to_all(value, axes, 0, 0)  63.6 us
    all_to_all x1, waiting for transfers between devices, exchange(): return lax.all_to_all(value, axes, 0, 0)  12.1 us
    all_to_all x1, starting transfers between devices, exchange(): return lax.all_to_all(value, axes, 0, 0)  8.19 us
    pallas_call x1, Pallas kernels, on_device(): pl.pallas_call(first_kernel, in_specs=[smem] + [vmem] * 4, out_shape=(sds...  8.06 us
    pallas_call x1, Pallas kernels, on_device(): pl.pallas_call(second_kernel, in_specs=[smem] + [vmem] * 5, out_shape=(sd...  4.59 us
  transfers between devices with their start and end apart: 2, of which 1 were waited for; matrix products, arithmetic and copies ran while one was open for 0% of the time, Pallas kernels for 1%

profile of v2, /device:TPU:1, one launch (start us, length us, event | category | flops | bytes accessed | tf_op | source)
XLA Modules:
  0.0 103.4 jit_solution(15699465489694407959)
XLA Ops:
  0.6 1.9 %shard_map.67 = (bf16[16,160,128]{2,1,0:T(8,128)(2,1)}, bf16[8,144,128]{2,1,0:T(8,128)(2,1)}) custom-call(bf16[128,128]{1,0:T(8,128)(2,1)} %ctx_hbm.1, s32[1,128]{1,0:T(1,128)} %bitcast.16, s32[8,128]{1,0:T(8,128)} %bitcast.15), custom_call_target="tpu_custom_call" | custom-call | tf_op jit(solution)/shard_map/pallas_call | solution.py:230
  2.5 19.2 %all_to_all.25.own_ref = bf16[16,160,128]{2,1,0:T(8,128)(2,1)S(1)} all-to-all(bf16[16,160,128]{2,1,0:T(8,128)(2,1)} %get-tuple-element.15), channel_id=1, replica_groups=mesh['z_hi'=2,'x'=4,'z_lo'=4,'y'=4,'core'=2] {'x','y'}, dimensions={0} | all-to-all | bytes 1310720 | tf_op jit(solution)/shard_map/all_to_all | solution.py:219
  21.7 0.0 copy-start
  21.7 2.1 %collective-permute-start = (bf16[16,160,128]{2,1,0:T(8,128)(2,1)S(1)}, bf16[16,160,128]{2,1,0:T(8,128)(2,1)S(1)}, u32[]{:S(2)}, u32[]{:S(2)}) collective-permute-start(bf16[16,160,128]{2,1,0:T(8,128)(2,1)S(1)} %all_to_all.25.own_ref), channel_id=1, source_target_pairs={{0,1},{1,0},{2,3},{3,2},{4,5},{5,4},{6,7},{7,6},{8,9},{9,8},{10,11... | collective-permute-start | bytes 1966088 | tf_op jit(solution)/shard_map/ppermute | solution.py:243
  23.8 8.2 %all-to-all-start.1 = ((bf16[8,144,128]{2,1,0:T(8,128)(2,1)}), bf16[8,144,128]{2,1,0:T(8,128)(2,1)S(1)}, u32[]{:S(2)}, u32[]{:S(2)}) async-start(bf16[8,144,128]{2,1,0:T(8,128)(2,1)} %get-tuple-element.16), calls=%async_computation.1 | async-start | bytes 589824 | tf_op jit(solution)/shard_map/all_to_all | solution.py:219
  32.0 0.1 pad_add_fusion.place_ref
  32.1 0.0 collective-permute-done.other_ref
  32.1 0.9 shard_map.68.policy_ref
  33.0 12.1 %all-to-all-done.1.right_ref = bf16[8,144,128]{2,1,0:T(8,128)(2,1)S(1)} async-done(((bf16[8,144,128]{2,1,0:T(8,128)(2,1)}), bf16[8,144,128]{2,1,0:T(8,128)(2,1)S(1)}, u32[]{:S(2)}, u32[]{:S(2)}) %all-to-all-start.1) | async-done | bytes 294944 | tf_op jit(solution)/shard_map/all_to_all | solution.py:219
  45.1 8.1 %shard_map.69 = (bf16[4096,1024]{1,0:T(8,128)(2,1)S(1)}, f32[8,8,8,128]{3,2,1,0:T(8,128)S(1)}) custom-call(s32[2]{0:T(128)S(1)} %pad_add_fusion.place_ref, bf16[16,160,128]{2,1,0:T(8,128)(2,1)S(1)} %all_to_all.25.own_ref, bf16[16,160,128]{2,1,0:T(8,128)(2,1)S(1)} %collective-permute-done.other_ref, bf16[8,144,128]{2,1,0:T(8,128)(2,1)S(1)} %all-to-all-done.1.right_ref, ...), custom_call_target="tpu_custom_call" | custom-call | tf_op jit(solution)/shard_map/pallas_call | solution.py:253
  53.1 14.6 %all_to_all.26.parts_ref = f32[8,8,8,128]{3,2,1,0:T(8,128)S(1)} all-to-all(f32[8,8,8,128]{3,2,1,0:T(8,128)S(1)} %get-tuple-element.18), channel_id=1, replica_groups=mesh['z_hi'=2,'x'=4,'z_lo'=4,'y'=4,'core'=2] {'z_hi','z_lo'}, dimensions={0} | all-to-all | bytes 524288 | tf_op jit(solution)/shard_map/all_to_all | solution.py:219
  67.8 4.6 %shard_map.70 = (f32[32,8,128]{2,1,0:T(8,128)S(1)}, f32[8,8,128]{2,1,0:T(8,128)S(1)}) custom-call(s32[2]{0:T(128)S(1)} %pad_add_fusion.place_ref, bf16[4096,1024]{1,0:T(8,128)(2,1)S(1)} %get-tuple-element.17.kernel_ref, f32[8,8,8,128]{3,2,1,0:T(8,128)S(1)} %all_to_all.26.parts_ref, bf16[8,144,128]{2,1,0:T(8,128)(2,1)S(1)} %all-to-all-done.1.right_ref, ...), custom_call_target="tpu_custom_call" | custom-call | tf_op jit(solution)/shard_map/pallas_call | solution.py:261
  72.4 11.8 %all_to_all.27.parts_ref = f32[32,8,128]{2,1,0:T(8,128)S(1)} all-to-all(f32[32,8,128]{2,1,0:T(8,128)S(1)} %get-tuple-element.19), channel_id=1, replica_groups=mesh['z_hi'=2,'x'=4,'z_lo'=4,'y'=4,'core'=2] {'x','y','core'}, dimensions={0} | all-to-all | bytes 262144 | tf_op jit(solution)/shard_map/all_to_all | solution.py:219
  84.1 0.0 copy-done
  84.1 0.7 shard_map.71
  84.8 17.9 %all_to_all.28 = f32[256,1,128]{2,1,0:T(1,128)S(1)} all-to-all(f32[256,1,128]{2,1,0:T(1,128)S(1)} %bitcast.13), channel_id=1, replica_groups=mesh['z_hi'=2,'x'=4,'z_lo'=4,'y'=4,'core'=2] {'z_hi','x','z_lo','y','core'}, dimensions={0} | all-to-all | bytes 262144 | tf_op jit(solution)/shard_map/all_to_all | solution.py:219
  102.7 0.7 shard_map.72
Async XLA Ops:
  21.7 62.4 %copy-start = (f32[128]{0:T(128)S(1)}, f32[128]{0:T(128)}, u32[]{:S(2)}) copy-start(f32[128]{0:T(128)} %param.7) | copy-start | bytes 1540
  21.7 10.3 %collective-permute-start = (bf16[16,160,128]{2,1,0:T(8,128)(2,1)S(1)}, bf16[16,160,128]{2,1,0:T(8,128)(2,1)S(1)}, u32[]{:S(2)}, u32[]{:S(2)}) collective-permute-start(bf16[16,160,128]{2,1,0:T(8,128)(2,1)S(1)} %all_to_all.25.own_ref), channel_id=1, source_target_pairs={{0,1},{1,0},{2,3},{3,2},{4,5},{5,4},{6,7},{7,6},{8,9},{9,8},{10,11... | collective-permute-start | bytes 1966088 | tf_op jit(solution)/shard_map/ppermute | solution.py:243
  23.8 21.2 %all-to-all-start.1 = ((bf16[8,144,128]{2,1,0:T(8,128)(2,1)}), bf16[8,144,128]{2,1,0:T(8,128)(2,1)S(1)}, u32[]{:S(2)}, u32[]{:S(2)}) async-start(bf16[8,144,128]{2,1,0:T(8,128)(2,1)} %get-tuple-element.16), calls=%async_computation.1 | async-start | bytes 589824 | tf_op jit(solution)/shard_map/all_to_all | solution.py:219

commit v3 on v2

--- a/solution.py
+++ b/solution.py
@@ -71,7 +71,7 @@
     return out
 
 
-def prepare(ctx_hbm, logged_hbm, policy_hbm, plane_ref, column_ref, ctx_ref, logged_ref, policy_ref, sems):
+def prepare(ctx_hbm, logged_hbm, policy_hbm, plane_ref, mine_ref, ctx_ref, logged_ref, policy_ref, sems):
     moves = [
         pltpu.make_async_copy(source, target, sems.at[i])
         for i, (source, target) in enumerate(
@@ -90,9 +90,8 @@
     for i in range(PLANES):
         plane_ref[i, :TILE, :] = ctx
         plane_ref[i, TILE:, :] = small
-    for i in range(COLUMNS):
-        column_ref[i, :TILE, :] = ctx
-        column_ref[i, TILE:, :] = small[:NACT]
+    mine_ref[:TILE, :] = ctx
+    mine_ref[TILE:, :] = small[:NACT]
 
 
 def policy_kernel(own_ref, other_ref, policy_ref):
@@ -105,85 +104,84 @@
 
 
 SCALE = math.log2(math.e) / D
-CHUNK = 2
-
-
-def first_kernel(place_ref, own_ref, other_ref, right_ref, policy_ref, kernel_ref, sums_ref, squares, acc):
-    for b in range(COLUMNS):
-        x = right_ref[b, :TILE, :].astype(f32)
+CHUNK = 8
+BESIDE = 5
+SPAN = 2 * CHUNK * TILE
+
+
+def home(place_ref, shift):
+    return lax.rem(place_ref[1] + (COLUMNS - shift), COLUMNS)
+
+
+def first_kernel(place_ref, own_ref, other_ref, policy_ref, *refs):
+    right_refs = (own_ref.at[place_ref[2]], *refs[: COLUMNS - 1])
+    kernel_ref, sums_ref, squares, acc, cols = refs[COLUMNS - 1 :]
+    for b, right_ref in enumerate(right_refs):
+        x = right_ref[:TILE, :]
+        cols[b * TILE : (b + 1) * TILE, :] = x
+        x = x.astype(f32)
         total = jnp.sum(x * x, axis=1, keepdims=True) * SCALE
         squares[:, b * TILE : (b + 1) * TILE] = jnp.transpose(jnp.broadcast_to(total, (TILE, TILE)))[:8]
     acc[...] = jnp.zeros_like(acc)
-
-    def rows_of(step, carry):
-        for piece in range(CHUNK):
-            for half, ref in enumerate((own_ref, other_ref)):
-                j = step * CHUNK + piece
-                rows = ref[j, :TILE, :]
-                wide = rows.astype(f32)
-                row_sq = jnp.sum(wide * wide, axis=1, keepdims=True) * SCALE
-                at = pl.multiple_of(step * (2 * CHUNK * TILE), 2 * CHUNK * TILE) + (2 * piece + half) * TILE
-                for b in range(0, COLUMNS, 2):
-                    cols = right_ref[b : b + 2, :TILE, :].reshape(2 * TILE, D)
-                    inner = lax.dot_general(rows, cols, (((1,), (1,)), ((), ())), preferred_element_type=f32)
-                    span = slice(b * TILE, (b + 2) * TILE)
-                    expo = (2.0 * SCALE) * inner - row_sq - squares[0:1, span]
-                    kernel_ref[pl.ds(at, TILE), span] = jnp.exp2(expo).astype(bf16)
-        start = pl.multiple_of(step * (2 * CHUNK * TILE), 2 * CHUNK * TILE)
-        whole = pl.ds(start, 2 * CHUNK * TILE)
+    for step in range(PLANES // CHUNK):
+        tiles = [ref[j, :TILE, :] for j in range(step * CHUNK, (step + 1) * CHUNK) for ref in (own_ref, other_ref)]
+        rows = jnp.concatenate(tiles, axis=0)
+        wide = rows.astype(f32)
+        row_sq = jnp.sum(wide * wide, axis=1, keepdims=True) * SCALE
+        whole = slice(step * SPAN, (step + 1) * SPAN)
+        for b in range(0, COLUMNS, 2):
+            span = slice(b * TILE, (b + 2) * TILE)
+            inner = lax.dot_general(rows, cols[span, :], (((1,), (1,)), ((), ())), preferred_element_type=f32)
+            expo = (2.0 * SCALE) * inner - row_sq - squares[0:1, span]
+            kernel_ref[whole, span] = jnp.exp2(expo).astype(bf16)
         acc[...] += jnp.dot(policy_ref[:, whole], kernel_ref[whole, :], preferred_element_type=f32)
-        return carry
-
-    lax.fori_loop(0, PLANES // CHUNK, rows_of, 0)
-    for b in range(COLUMNS):
-        chosen = right_ref[b, FEAT_AT : FEAT_AT + NACT, :].astype(f32)
+    for b, right_ref in enumerate(right_refs):
+        chosen = right_ref[FEAT_AT : FEAT_AT + NACT, :].astype(f32)
         total = jnp.zeros((NPOL, TILE), f32)
         for c in range(NACT):
             total += acc[c * NPOL : (c + 1) * NPOL, b * TILE : (b + 1) * TILE] * chosen[c : c + 1]
+        at = home(place_ref, b)
         for peer in range(COLUMNS):
-            sums_ref[peer, b] = total
-
-
-def second_kernel(place_ref, kernel_ref, parts_ref, right_ref, own_ref, other_ref, image_ref, side_ref, matched):
+            sums_ref[peer, at] = total
+
+
+def second_kernel(place_ref, kernel_ref, parts_ref, own_ref, other_ref, *refs):
+    right_refs = (own_ref.at[place_ref[2]], *refs[: COLUMNS - 1])
+    image_ref, side_ref, matched = refs[COLUMNS - 1 :]
     factor = NACT / (TILE * LEFT * COLUMNS)
-    for b in range(COLUMNS):
-        total = parts_ref[0, b]
+    for b, right_ref in enumerate(right_refs):
+        at = home(place_ref, b)
+        total = parts_ref[0, at]
         for peer in range(1, COLUMNS):
-            total += parts_ref[peer, b]
+            total += parts_ref[peer, at]
         total = total * factor
-        side_ref[b] = total
+        if b == 0:
+            side_ref[...] = total
         low = total.astype(bf16).astype(f32)
-        chosen = right_ref[b, FEAT_AT : FEAT_AT + NACT, :].astype(f32)
+        chosen = right_ref[FEAT_AT : FEAT_AT + NACT, :].astype(f32)
         made = jnp.concatenate([chosen[c : c + 1] * low for c in range(NACT)], axis=0)
-        matched[:, b * TILE : (b + 1) * TILE] = made.astype(bf16)
+        matched[b * TILE : (b + 1) * TILE, :] = jnp.transpose(made).astype(bf16)
     core = place_ref[0]
-
-    def rows_of(step, carry):
-        start = pl.multiple_of(step * (2 * CHUNK * TILE), 2 * CHUNK * TILE)
-        block = kernel_ref[pl.ds(start, 2 * CHUNK * TILE), :]
-        out = lax.dot_general(matched[...], block, (((1,), (1,)), ((), ())), preferred_element_type=f32)
-        for piece in range(CHUNK):
-            j = step * CHUNK + piece
+    for step in range(PLANES // CHUNK):
+        block = kernel_ref[step * SPAN : (step + 1) * SPAN, :]
+        out = jnp.transpose(jnp.dot(block, matched[...], preferred_element_type=f32))
+        for j in range(step * CHUNK, (step + 1) * CHUNK):
             for half, ref in enumerate((own_ref, other_ref)):
                 chosen = ref[j, FEAT_AT : FEAT_AT + NACT, :].astype(f32)
-                at = (2 * piece + half) * TILE
+                at = (2 * (j - step * CHUNK) + half) * TILE
                 total = jnp.zeros((NPOL, TILE), f32)
                 for c in range(NACT):
                     total += out[c * NPOL : (c + 1) * NPOL, at : at + TILE] * chosen[c : c + 1]
                 image_ref[2 * j + jnp.where(core == half, 0, 1)] = total * factor
-        return carry
-
-    lax.fori_loop(0, PLANES // CHUNK, rows_of, 0)
-
-
-def third_kernel(place_ref, parts_ref, side_ref, rewards_ref, image_ref, own_ref, sums_ref):
+
+
+def third_kernel(parts_ref, side_ref, rewards_ref, image_ref, sums_ref):
     total = parts_ref[0]
     for i in range(1, LEFT):
         total += parts_ref[i]
-    side = side_ref[place_ref[1]]
+    side = side_ref[...]
     image = total + ridge * side
     image_ref[...] = image
-    own_ref[...] = side
     lane = lax.broadcasted_iota(i32, (NPOL, TILE), 1)
     row = lax.broadcasted_iota(i32, (NPOL, TILE), 0)
     spread = jnp.zeros((NPOL, TILE), f32)
@@ -222,15 +220,15 @@
 def on_device(contexts, logged_actions, policy_actions, rewards):
     core = lax.axis_index("core")
     column = lax.axis_index(COLUMN)
-    place = jnp.stack([core, column]).astype(i32)
+    place = jnp.stack([core, column, lax.axis_index(PLANE)]).astype(i32)
     sds = jax.ShapeDtypeStruct
     vmem = pl.BlockSpec(memory_space=pltpu.VMEM)
     smem = pl.BlockSpec(memory_space=pltpu.SMEM)
 
-    plane_send, column_send = pl.pallas_call(
+    plane_send, mine = pl.pallas_call(
         prepare,
         in_specs=[pl.BlockSpec(memory_space=pl.ANY)] * 3,
-        out_shape=(sds((PLANES, ROWS, D), bf16), sds((COLUMNS, RIGHT_ROWS, D), bf16)),
+        out_shape=(sds((PLANES, ROWS, D), bf16), sds((RIGHT_ROWS, D), bf16)),
         scratch_shapes=[
             pltpu.VMEM((TILE, D), bf16),
             pltpu.VMEM((1, TILE), i32),
@@ -239,9 +237,10 @@
         ],
         compiler_params=params(60 * MIB),
     )(contexts, logged_actions.reshape(1, TILE), policy_actions.T)
-    own = exchange(plane_send, PLANE)
+    ring = lambda shift: [(i, (i + shift) % COLUMNS) for i in range(COLUMNS)]
+    right = [lax.ppermute(mine, COLUMN, ring(shift)) for shift in range(1, COLUMNS)]
+    own, *right[:BESIDE] = lax.optimization_barrier((exchange(plane_send, PLANE), *right[:BESIDE]))
     other = lax.ppermute(own, "core", [(0, 1), (1, 0)])
-    right = exchange(column_send, COLUMN)
 
     width = COLUMNS * TILE
     policy = pl.pallas_call(
@@ -252,34 +251,33 @@
     )(own, other)
     kernel, first = pl.pallas_call(
         first_kernel,
-        in_specs=[smem] + [vmem] * 4,
+        in_specs=[smem] + [vmem] * (2 + COLUMNS),
         out_shape=(sds((LEFT * TILE, width), bf16), sds((COLUMNS, COLUMNS, NPOL, TILE), f32)),
-        scratch_shapes=[pltpu.VMEM((8, width), f32), pltpu.VMEM((TILE, width), f32)],
-        compiler_params=params(),
-    )(place, own, other, right, policy)
+        scratch_shapes=[pltpu.VMEM((8, width), f32), pltpu.VMEM((TILE, width), f32), pltpu.VMEM((width, D), bf16)],
+        compiler_params=params(),
+    )(place, own, other, policy, *right)
     parts = exchange(first, COLUMN)
     image_parts, side = pl.pallas_call(
         second_kernel,
-        in_specs=[smem] + [vmem] * 5,
-        out_shape=(sds((LEFT, NPOL, TILE), f32), sds((COLUMNS, NPOL, TILE), f32)),
-        scratch_shapes=[pltpu.VMEM((TILE, width), bf16)],
-        compiler_params=params(),
-    )(place, kernel, parts, right, own, other)
+        in_specs=[smem] + [vmem] * (3 + COLUMNS),
+        out_shape=(sds((LEFT, NPOL, TILE), f32), sds((NPOL, TILE), f32)),
+        scratch_shapes=[pltpu.VMEM((width, TILE), bf16)],
+        compiler_params=params(),
+    )(place, kernel, parts, own, other, *right)
     image_parts = exchange(image_parts, PLANE + ("core",))
 
     count = LEFT * COLUMNS
-    image, own_side, sums = pl.pallas_call(
+    image, sums = pl.pallas_call(
         third_kernel,
-        in_specs=[smem, vmem, vmem, vmem],
-        out_shape=(sds((NPOL, TILE), f32), sds((NPOL, TILE), f32), sds((count, TILE), f32)),
-        compiler_params=params(),
-    )(place, image_parts, side, rewards.reshape(1, TILE))
+                out_shape=(sds((NPOL, TILE), f32), sds((count, TILE), f32)),
+        compiler_params=params(),
+    )(image_parts, side, rewards.reshape(1, TILE))
     sums = exchange(sums.reshape(count, 1, TILE), EVERY).reshape(count, TILE)
     weights, residual, values = pl.pallas_call(
         last_kernel,
         out_shape=(sds((NPOL, TILE), f32), sds((NPOL, TILE), f32), sds((1, NPOL), f32)),
         compiler_params=params(),
-    )(sums, image, own_side)
+    )(sums, image, side)
     return weights.T, residual.T, values.reshape(NPOL)
 
 

time: 104 us -> 93.9 us (0.903)
  starting transfers between devices: 10.3 us -> 25 us
  blocking collectives: 63.6 us -> 49.5 us
  waiting for transfers between devices: 12.1 us -> 6.34 us
  Pallas kernels: 16.8 us -> 12 us
    ppermute x0 -> x7, starting transfers between devices: none -> 15.1 us  [on_device(): lax.ppermute(mine, COLUMN, ring(shift))]
    all_to_all x4 -> x3, blocking collectives: 63.6 us -> 49.5 us  [exchange(): return lax.all_to_all(value, axes, 0, 0)]
    all_to_all x1, waiting for transfers between devices: 12.1 us -> 0.01 us  [exchange(): return lax.all_to_all(value, axes, 0, 0)]
    ppermute x0 -> x7, waiting for transfers between devices: none -> 6.34 us  [on_device(): lax.ppermute(mine, COLUMN, ring(shift))]
    pallas_call x3, Pallas kernels: 13.3 us -> 8.61 us  [the longest x1 5.35 us: on_device(): pl.pallas_call(first_kernel, in_specs=[smem] + [vmem] * (2 + COLUMNS), ou...]
  transfers between devices with their start and end apart: 2 -> 9, of which waited for: 1 -> 5; matrix products, arithmetic and copies ran while one was open for 0% -> 0% of each run, Pallas kernels for 1% -> 1%
where the time goes in v3:
time: 93.9 us; the launch traced here: 93.6 us
  blocking collectives  49.5 us (53%)
  starting transfers between devices  25 us (27%)
  Pallas kernels  12 us (13%)
  waiting for transfers between devices  6.34 us (7%)
    all_to_all x3, blocking collectives, exchange(): return lax.all_to_all(value, axes, 0, 0)  49.5 us
    ppermute x7, starting transfers between devices, on_device(): lax.ppermute(mine, COLUMN, ring(shift))  15.1 us
    all_to_all x1, starting transfers between devices, exchange(): return lax.all_to_all(value, axes, 0, 0)  7.6 us
    ppermute x7, waiting for transfers between devices, on_device(): lax.ppermute(mine, COLUMN, ring(shift))  6.34 us
    pallas_call x1, Pallas kernels, on_device(): pl.pallas_call(first_kernel, in_specs=[smem] + [vmem] * (2 + COLUMNS), ou...  5.35 us
    pallas_call x1, Pallas kernels, on_device(): pl.pallas_call(second_kernel, in_specs=[smem] + [vmem] * (3 + COLUMNS), o...  3.13 us
    ppermute x1, starting transfers between devices, on_device(): other = lax.ppermute(own, 'core', [(0, 1), (1, 0)])  2.34 us
  transfers between devices with their start and end apart: 9, of which 5 were waited for; matrix products, arithmetic and copies ran while one was open for 0% of the time, Pallas kernels for 1%

profile of v3, /device:TPU:1, one launch (start us, length us, event | category | flops | bytes accessed | tf_op | source)
XLA Modules:
  0.0 93.6 jit_solution(2395775069710910802)
XLA Ops:
  0.6 1.8 %shard_map.67 = (bf16[16,160,128]{2,1,0:T(8,128)(2,1)}, bf16[144,128]{1,0:T(8,128)(2,1)}) custom-call(bf16[128,128]{1,0:T(8,128)(2,1)} %ctx_hbm.1, s32[1,128]{1,0:T(1,128)} %bitcast.17, s32[8,128]{1,0:T(8,128)} %bitcast.16), custom_call_target="tpu_custom_call" | custom-call | tf_op jit(solution)/shard_map/pallas_call | solution.py:228
  2.4 0.0 copy-start
  2.4 7.6 %all-to-all-start = ((bf16[16,160,128]{2,1,0:T(8,128)(2,1)}), bf16[16,160,128]{2,1,0:T(8,128)(2,1)S(1)}, u32[]{:S(2)}, u32[]{:S(2)}) async-start(bf16[16,160,128]{2,1,0:T(8,128)(2,1)} %get-tuple-element.20), calls=%async_computation | async-start | bytes 1310720 | tf_op jit(solution)/shard_map/all_to_all | solution.py:217
  10.0 6.5 %collective-permute-start.4 = (bf16[144,128]{1,0:T(8,128)(2,1)}, bf16[144,128]{1,0:T(8,128)(2,1)S(1)}, u32[]{:S(2)}, u32[]{:S(2)}) collective-permute-start(bf16[144,128]{1,0:T(8,128)(2,1)} %get-tuple-element.21), channel_id=1, source_target_pairs={{0,136},{8,144},{16,152},{24,0},{128,8},{136,16},{144,24},{152,128... | collective-permute-start | bytes 110600 | tf_op jit(solution)/shard_map/ppermute | solution.py:241
  16.6 0.5 collective-permute-start.3
  17.1 3.2 %collective-permute-start.2 = (bf16[144,128]{1,0:T(8,128)(2,1)}, bf16[144,128]{1,0:T(8,128)(2,1)S(1)}, u32[]{:S(2)}, u32[]{:S(2)}) collective-permute-start(bf16[144,128]{1,0:T(8,128)(2,1)} %get-tuple-element.21), channel_id=1, source_target_pairs={{0,24},{8,128},{16,136},{24,144},{128,152},{136,0},{144,8},{152,16... | collective-permute-start | bytes 110600 | tf_op jit(solution)/shard_map/ppermute | solution.py:241
  20.3 2.4 %collective-permute-start.1 = (bf16[144,128]{1,0:T(8,128)(2,1)}, bf16[144,128]{1,0:T(8,128)(2,1)S(1)}, u32[]{:S(2)}, u32[]{:S(2)}) collective-permute-start(bf16[144,128]{1,0:T(8,128)(2,1)} %get-tuple-element.21), channel_id=1, source_target_pairs={{0,16},{8,24},{16,128},{24,136},{128,144},{136,152},{144,0},{152,8... | collective-permute-start | bytes 110600 | tf_op jit(solution)/shard_map/ppermute | solution.py:241
  22.7 0.7 collective-permute-start
  23.4 0.0 collective-permute-done.4.refs_4_
  23.4 0.5 collective-permute-done.3.refs_3_
  23.9 0.0 collective-permute-done.2.refs_2_
  23.9 3.1 %collective-permute-done.1.refs_1_ = bf16[144,128]{1,0:T(8,128)(2,1)S(1)} collective-permute-done((bf16[144,128]{1,0:T(8,128)(2,1)}, bf16[144,128]{1,0:T(8,128)(2,1)S(1)}, u32[]{:S(2)}, u32[]{:S(2)}) %collective-permute-start.1) | collective-permute-done | bytes 36896 | tf_op jit(solution)/shard_map/ppermute | solution.py:241
  27.0 0.8 collective-permute-done.refs_0_
  27.8 0.0 all-to-all-done.own_ref
  27.8 2.3 %collective-permute-start.5 = (bf16[16,160,128]{2,1,0:T(8,128)(2,1)S(1)}, bf16[16,160,128]{2,1,0:T(8,128)(2,1)S(1)}, u32[]{:S(2)}, u32[]{:S(2)}) collective-permute-start(bf16[16,160,128]{2,1,0:T(8,128)(2,1)S(1)} %all-to-all-done.own_ref), channel_id=1, source_target_pairs={{0,1},{1,0},{2,3},{3,2},{4,5},{5,4},{6,7},{7,6},{8,9},{9,8},{10,11... | collective-permute-start | bytes 1966088 | tf_op jit(solution)/shard_map/ppermute | solution.py:243
  30.1 0.7 collective-permute-start.7
  30.9 1.0 %collective-permute-start.6 = (bf16[144,128]{1,0:T(8,128)(2,1)}, bf16[144,128]{1,0:T(8,128)(2,1)S(1)}, u32[]{:S(2)}, u32[]{:S(2)}) collective-permute-start(bf16[144,128]{1,0:T(8,128)(2,1)} %get-tuple-element.21), channel_id=1, source_target_pairs={{0,144},{8,152},{16,0},{24,8},{128,16},{136,24},{144,128},{152,136... | collective-permute-start | bytes 110600 | tf_op jit(solution)/shard_map/ppermute | solution.py:241
  31.9 0.1 pad_add_fusion.place_ref
  31.9 0.0 collective-permute-done.5.other_ref
  31.9 0.9 shard_map.68.policy_ref
  32.8 0.3 collective-permute-done.7.refs_6_
  33.2 1.6 %collective-permute-done.6.refs_5_ = bf16[144,128]{1,0:T(8,128)(2,1)S(1)} collective-permute-done((bf16[144,128]{1,0:T(8,128)(2,1)}, bf16[144,128]{1,0:T(8,128)(2,1)S(1)}, u32[]{:S(2)}, u32[]{:S(2)}) %collective-permute-start.6) | collective-permute-done | bytes 36896 | tf_op jit(solution)/shard_map/ppermute | solution.py:241
  34.8 5.3 %shard_map.69 = (bf16[4096,1024]{1,0:T(8,128)(2,1)S(1)}, f32[8,8,8,128]{3,2,1,0:T(8,128)S(1)}) custom-call(s32[3]{0:T(128)S(1)} %pad_add_fusion.place_ref, bf16[16,160,128]{2,1,0:T(8,128)(2,1)S(1)} %all-to-all-done.own_ref, bf16[16,160,128]{2,1,0:T(8,128)(2,1)S(1)} %collective-permute-done.5.other_ref, bf16[128,4096]{1,0:T(8,128)(2,1)S(1)} %shard_map.68.policy_ref, ...), custom_call_target="tpu_custom_call" | custom-call | tf_op jit(solution)/shard_map/pallas_call | solution.py:252
  40.2 13.6 %all_to_all.20.parts_ref = f32[8,8,8,128]{3,2,1,0:T(8,128)S(1)} all-to-all(f32[8,8,8,128]{3,2,1,0:T(8,128)S(1)} %get-tuple-element.29), channel_id=1, replica_groups=mesh['z_hi'=2,'x'=4,'z_lo'=4,'y'=4,'core'=2] {'z_hi','z_lo'}, dimensions={0} | all-to-all | bytes 524288 | tf_op jit(solution)/shard_map/all_to_all | solution.py:217
  53.8 3.1 %shard_map.70 = (f32[32,8,128]{2,1,0:T(8,128)S(1)}, f32[8,128]{1,0:T(8,128)S(1)}) custom-call(s32[3]{0:T(128)S(1)} %pad_add_fusion.place_ref, bf16[4096,1024]{1,0:T(8,128)(2,1)S(1)} %get-tuple-element.28.kernel_ref, f32[8,8,8,128]{3,2,1,0:T(8,128)S(1)} %all_to_all.20.parts_ref, bf16[16,160,128]{2,1,0:T(8,128)(2,1)S(1)} %all-to-all-done.own_ref, ...), custom_call_target="tpu_custom_call" | custom-call | tf_op jit(solution)/shard_map/pallas_call | solution.py:260
  56.9 17.9 %all_to_all.21.parts_ref = f32[32,8,128]{2,1,0:T(8,128)S(1)} all-to-all(f32[32,8,128]{2,1,0:T(8,128)S(1)} %get-tuple-element.30), channel_id=1, replica_groups=mesh['z_hi'=2,'x'=4,'z_lo'=4,'y'=4,'core'=2] {'x','y','core'}, dimensions={0} | all-to-all | bytes 262144 | tf_op jit(solution)/shard_map/all_to_all | solution.py:217
  74.8 0.0 copy-done
  74.8 0.1 shard_map.71
  75.0 17.9 %all_to_all.22 = f32[256,1,128]{2,1,0:T(1,128)S(1)} all-to-all(f32[256,1,128]{2,1,0:T(1,128)S(1)} %bitcast.14), channel_id=1, replica_groups=mesh['z_hi'=2,'x'=4,'z_lo'=4,'y'=4,'core'=2] {'z_hi','x','z_lo','y','core'}, dimensions={0} | all-to-all | bytes 262144 | tf_op jit(solution)/shard_map/all_to_all | solution.py:217
  92.9 0.7 shard_map.72
Async XLA Ops:
  2.4 72.4 %copy-start = (f32[128]{0:T(128)S(1)}, f32[128]{0:T(128)}, u32[]{:S(2)}) copy-start(f32[128]{0:T(128)} %param.7) | copy-start | bytes 1540
  2.4 25.4 %all-to-all-start = ((bf16[16,160,128]{2,1,0:T(8,128)(2,1)}), bf16[16,160,128]{2,1,0:T(8,128)(2,1)S(1)}, u32[]{:S(2)}, u32[]{:S(2)}) async-start(bf16[16,160,128]{2,1,0:T(8,128)(2,1)} %get-tuple-element.20), calls=%async_computation | async-start | bytes 1310720 | tf_op jit(solution)/shard_map/all_to_all | solution.py:217
  10.0 13.4 %collective-permute-start.4 = (bf16[144,128]{1,0:T(8,128)(2,1)}, bf16[144,128]{1,0:T(8,128)(2,1)S(1)}, u32[]{:S(2)}, u32[]{:S(2)}) collective-permute-start(bf16[144,128]{1,0:T(8,128)(2,1)} %get-tuple-element.21), channel_id=1, source_target_pairs={{0,136},{8,144},{16,152},{24,0},{128,8},{136,16},{144,24},{152,128... | collective-permute-start | bytes 110600 | tf_op jit(solution)/shard_map/ppermute | solution.py:241
  16.6 7.3 %collective-permute-start.3 = (bf16[144,128]{1,0:T(8,128)(2,1)}, bf16[144,128]{1,0:T(8,128)(2,1)S(1)}, u32[]{:S(2)}, u32[]{:S(2)}) collective-permute-start(bf16[144,128]{1,0:T(8,128)(2,1)} %get-tuple-element.21), channel_id=1, source_target_pairs={{0,128},{8,136},{16,144},{24,152},{128,0},{136,8},{144,16},{152,24... | collective-permute-start | bytes 110600 | tf_op jit(solution)/shard_map/ppermute | solution.py:241
  17.1 6.8 %collective-permute-start.2 = (bf16[144,128]{1,0:T(8,128)(2,1)}, bf16[144,128]{1,0:T(8,128)(2,1)S(1)}, u32[]{:S(2)}, u32[]{:S(2)}) collective-permute-start(bf16[144,128]{1,0:T(8,128)(2,1)} %get-tuple-element.21), channel_id=1, source_target_pairs={{0,24},{8,128},{16,136},{24,144},{128,152},{136,0},{144,8},{152,16... | collective-permute-start | bytes 110600 | tf_op jit(solution)/shard_map/ppermute | solution.py:241
  20.3 6.7 %collective-permute-start.1 = (bf16[144,128]{1,0:T(8,128)(2,1)}, bf16[144,128]{1,0:T(8,128)(2,1)S(1)}, u32[]{:S(2)}, u32[]{:S(2)}) collective-permute-start(bf16[144,128]{1,0:T(8,128)(2,1)} %get-tuple-element.21), channel_id=1, source_target_pairs={{0,16},{8,24},{16,128},{24,136},{128,144},{136,152},{144,0},{152,8... | collective-permute-start | bytes 110600 | tf_op jit(solution)/shard_map/ppermute | solution.py:241
  22.7 5.1 %collective-permute-start = (bf16[144,128]{1,0:T(8,128)(2,1)}, bf16[144,128]{1,0:T(8,128)(2,1)S(1)}, u32[]{:S(2)}, u32[]{:S(2)}) collective-permute-start(bf16[144,128]{1,0:T(8,128)(2,1)} %get-tuple-element.21), channel_id=1, source_target_pairs={{0,8},{8,16},{16,24},{24,128},{128,136},{136,144},{144,152},{152,0... | collective-permute-start | bytes 110600 | tf_op jit(solution)/shard_map/ppermute | solution.py:241
  27.8 4.1 %collective-permute-start.5 = (bf16[16,160,128]{2,1,0:T(8,128)(2,1)S(1)}, bf16[16,160,128]{2,1,0:T(8,128)(2,1)S(1)}, u32[]{:S(2)}, u32[]{:S(2)}) collective-permute-start(bf16[16,160,128]{2,1,0:T(8,128)(2,1)S(1)} %all-to-all-done.own_ref), channel_id=1, source_target_pairs={{0,1},{1,0},{2,3},{3,2},{4,5},{5,4},{6,7},{7,6},{8,9},{9,8},{10,11... | collective-permute-start | bytes 1966088 | tf_op jit(solution)/shard_map/ppermute | solution.py:243
  30.1 3.0 %collective-permute-start.7 = (bf16[144,128]{1,0:T(8,128)(2,1)}, bf16[144,128]{1,0:T(8,128)(2,1)S(1)}, u32[]{:S(2)}, u32[]{:S(2)}) collective-permute-start(bf16[144,128]{1,0:T(8,128)(2,1)} %get-tuple-element.21), channel_id=1, source_target_pairs={{0,152},{8,0},{16,8},{24,16},{128,24},{136,128},{144,136},{152,144... | collective-permute-start | bytes 110600 | tf_op jit(solution)/shard_map/ppermute | solution.py:241
  30.9 3.9 %collective-permute-start.6 = (bf16[144,128]{1,0:T(8,128)(2,1)}, bf16[144,128]{1,0:T(8,128)(2,1)S(1)}, u32[]{:S(2)}, u32[]{:S(2)}) collective-permute-start(bf16[144,128]{1,0:T(8,128)(2,1)} %get-tuple-element.21), channel_id=1, source_target_pairs={{0,144},{8,152},{16,0},{24,8},{128,16},{136,24},{144,128},{152,136... | collective-permute-start | bytes 110600 | tf_op jit(solution)/shard_map/ppermute | solution.py:241

commit v4 on v3

--- a/solution.py
+++ b/solution.py
@@ -94,18 +94,35 @@
     mine_ref[TILE:, :] = small[:NACT]
 
 
-def policy_kernel(own_ref, other_ref, policy_ref):
+def pieces(total):
+    high = total.astype(bf16).astype(f32)
+    rest = total - high
+    middle = rest.astype(bf16).astype(f32)
+    return high, middle, rest - middle
+
+
+def lanes():
+    return lax.broadcasted_iota(i32, (TILE, TILE), 1)
+
+
+def policy_kernel(own_ref, other_ref, policy_ref, extra_ref):
+    lane = lanes()
     for half, ref in enumerate((own_ref, other_ref)):
         for j in range(PLANES):
+            at = 2 * j + half
             codes = ref[j, CODE_AT:ROWS, :].astype(f32).astype(i32)
             acts = (codes[:NPOL] << 9) + codes[NPOL:] + 256
             feats = jnp.concatenate(features(acts), axis=0).astype(bf16)
-            policy_ref[:, (2 * j + half) * TILE : (2 * j + half + 1) * TILE] = feats
+            policy_ref[:, at * TILE : (at + 1) * TILE] = feats
+            wide = ref[j, :TILE, :].astype(f32)
+            high, middle, low = pieces(jnp.sum(wide * wide, axis=1, keepdims=True))
+            extra = jnp.where(lane == 0, high, jnp.where(lane == 1, middle, jnp.where(lane == 2, low, 1.0)))
+            extra_ref[at] = extra.astype(bf16)
 
 
 SCALE = math.log2(math.e) / D
 CHUNK = 8
-BESIDE = 5
+BESIDE = 3
 SPAN = 2 * CHUNK * TILE
 
 
@@ -113,39 +130,67 @@
     return lax.rem(place_ref[1] + (COLUMNS - shift), COLUMNS)
 
 
-def first_kernel(place_ref, own_ref, other_ref, policy_ref, *refs):
-    right_refs = (own_ref.at[place_ref[2]], *refs[: COLUMNS - 1])
-    kernel_ref, sums_ref, squares, acc, cols = refs[COLUMNS - 1 :]
+def block(left_refs, right_refs, kernel_ref, acc, cols):
+    own_ref, other_ref, policy_ref, extra_ref = left_refs
+    lane = lanes()
     for b, right_ref in enumerate(right_refs):
-        x = right_ref[:TILE, :]
-        cols[b * TILE : (b + 1) * TILE, :] = x
-        x = x.astype(f32)
-        total = jnp.sum(x * x, axis=1, keepdims=True) * SCALE
-        squares[:, b * TILE : (b + 1) * TILE] = jnp.transpose(jnp.broadcast_to(total, (TILE, TILE)))[:8]
-    acc[...] = jnp.zeros_like(acc)
+        here = slice(b * TILE, (b + 1) * TILE)
+        x = right_ref[:TILE, :].astype(f32)
+        high, middle, low = pieces(jnp.sum(x * x, axis=1, keepdims=True))
+        extra = jnp.where(lane < 3, -1.0, 0.0)
+        for at, piece in ((3, high), (4, middle), (5, low)):
+            extra = jnp.where(lane == at, -piece, extra)
+        cols[here, :D] = (2.0 * x).astype(bf16)
+        cols[here, D:] = extra.astype(bf16)
+    width = len(right_refs) * TILE
+    wide = 2 * TILE
     for step in range(PLANES // CHUNK):
-        tiles = [ref[j, :TILE, :] for j in range(step * CHUNK, (step + 1) * CHUNK) for ref in (own_ref, other_ref)]
-        rows = jnp.concatenate(tiles, axis=0)
-        wide = rows.astype(f32)
-        row_sq = jnp.sum(wide * wide, axis=1, keepdims=True) * SCALE
+        rows = jnp.concatenate(
+            [
+                jnp.concatenate([ref[j, :TILE, :], extra_ref[2 * j + half]], axis=1)
+                for j in range(step * CHUNK, (step + 1) * CHUNK)
+                for half, ref in enumerate((own_ref, other_ref))
+            ],
+            axis=0,
+        )
         whole = slice(step * SPAN, (step + 1) * SPAN)
-        for b in range(0, COLUMNS, 2):
-            span = slice(b * TILE, (b + 2) * TILE)
-            inner = lax.dot_general(rows, cols[span, :], (((1,), (1,)), ((), ())), preferred_element_type=f32)
-            expo = (2.0 * SCALE) * inner - row_sq - squares[0:1, span]
-            kernel_ref[whole, span] = jnp.exp2(expo).astype(bf16)
-        acc[...] += jnp.dot(policy_ref[:, whole], kernel_ref[whole, :], preferred_element_type=f32)
+        for at in range(0, width, wide):
+            span = slice(at, at + wide)
+            expo = lax.dot_general(rows, cols[span, :], (((1,), (1,)), ((), ())), preferred_element_type=f32)
+            kernel_ref[whole, span] = jnp.exp2(SCALE * expo).astype(bf16)
+        term = jnp.dot(policy_ref[:, whole], kernel_ref[whole, :], preferred_element_type=f32)
+        if step:
+            term += acc[...]
+        acc[...] = term
+    sums = []
     for b, right_ref in enumerate(right_refs):
         chosen = right_ref[FEAT_AT : FEAT_AT + NACT, :].astype(f32)
         total = jnp.zeros((NPOL, TILE), f32)
         for c in range(NACT):
             total += acc[c * NPOL : (c + 1) * NPOL, b * TILE : (b + 1) * TILE] * chosen[c : c + 1]
+        sums.append(total)
+    return sums
+
+
+def first_half(place_ref, own_ref, other_ref, policy_ref, extra_ref, *refs):
+    right_refs = (own_ref.at[place_ref[2]], *refs[:BESIDE])
+    kernel_ref, sums_ref, acc, cols = refs[BESIDE:]
+    for b, total in enumerate(block((own_ref, other_ref, policy_ref, extra_ref), right_refs, kernel_ref, acc, cols)):
+        sums_ref[b] = total
+
+
+def second_half(place_ref, own_ref, other_ref, policy_ref, extra_ref, done_ref, *refs):
+    right_refs = refs[: COLUMNS - 1 - BESIDE]
+    kernel_ref, sums_ref, acc, cols = refs[COLUMNS - 1 - BESIDE :]
+    totals = block((own_ref, other_ref, policy_ref, extra_ref), right_refs, kernel_ref, acc, cols)
+    totals = [done_ref[b] for b in range(BESIDE + 1)] + totals
+    for b, total in enumerate(totals):
         at = home(place_ref, b)
         for peer in range(COLUMNS):
             sums_ref[peer, at] = total
 
 
-def second_kernel(place_ref, kernel_ref, parts_ref, own_ref, other_ref, *refs):
+def second_kernel(place_ref, near_ref, far_ref, parts_ref, own_ref, other_ref, *refs):
     right_refs = (own_ref.at[place_ref[2]], *refs[: COLUMNS - 1])
     image_ref, side_ref, matched = refs[COLUMNS - 1 :]
     factor = NACT / (TILE * LEFT * COLUMNS)
@@ -162,9 +207,12 @@
         made = jnp.concatenate([chosen[c : c + 1] * low for c in range(NACT)], axis=0)
         matched[b * TILE : (b + 1) * TILE, :] = jnp.transpose(made).astype(bf16)
     core = place_ref[0]
+    cut = (BESIDE + 1) * TILE
     for step in range(PLANES // CHUNK):
-        block = kernel_ref[step * SPAN : (step + 1) * SPAN, :]
-        out = jnp.transpose(jnp.dot(block, matched[...], preferred_element_type=f32))
+        whole = slice(step * SPAN, (step + 1) * SPAN)
+        out = jnp.dot(near_ref[whole, :], matched[:cut, :], preferred_element_type=f32)
+        out += jnp.dot(far_ref[whole, :], matched[cut:, :], preferred_element_type=f32)
+        out = jnp.transpose(out)
         for j in range(step * CHUNK, (step + 1) * CHUNK):
             for half, ref in enumerate((own_ref, other_ref)):
                 chosen = ref[j, FEAT_AT : FEAT_AT + NACT, :].astype(f32)
@@ -242,28 +290,46 @@
     own, *right[:BESIDE] = lax.optimization_barrier((exchange(plane_send, PLANE), *right[:BESIDE]))
     other = lax.ppermute(own, "core", [(0, 1), (1, 0)])
 
-    width = COLUMNS * TILE
-    policy = pl.pallas_call(
+    policy, extra = pl.pallas_call(
         policy_kernel,
-        out_shape=sds((TILE, LEFT * TILE), bf16),
-        cost_estimate=pl.CostEstimate(flops=60_000_000, bytes_accessed=2_000_000, transcendentals=0),
+        out_shape=(sds((TILE, LEFT * TILE), bf16), sds((LEFT, TILE, TILE), bf16)),
+        cost_estimate=pl.CostEstimate(flops=60_000_000, bytes_accessed=3_000_000, transcendentals=0),
         compiler_params=params(),
     )(own, other)
-    kernel, first = pl.pallas_call(
-        first_kernel,
-        in_specs=[smem] + [vmem] * (2 + COLUMNS),
-        out_shape=(sds((LEFT * TILE, width), bf16), sds((COLUMNS, COLUMNS, NPOL, TILE), f32)),
-        scratch_shapes=[pltpu.VMEM((8, width), f32), pltpu.VMEM((TILE, width), f32), pltpu.VMEM((width, D), bf16)],
-        compiler_params=params(),
-    )(place, own, other, policy, *right)
+    left = (place, own, other, policy, extra)
+    rows = LEFT * TILE
+
+    def cost(width):
+        return pl.CostEstimate(
+            flops=2 * rows * width * (2 * D + TILE), bytes_accessed=2 * rows * (width + 4 * D), transcendentals=rows * width
+        )
+
+    near, far = (BESIDE + 1) * TILE, (COLUMNS - 1 - BESIDE) * TILE
+    scratch = lambda width: [pltpu.VMEM((TILE, width), f32), pltpu.VMEM((width, 2 * D), bf16)]
+    near_block, done = pl.pallas_call(
+        first_half,
+        in_specs=[smem] + [vmem] * (4 + BESIDE),
+        out_shape=(sds((rows, near), bf16), sds((BESIDE + 1, NPOL, TILE), f32)),
+        scratch_shapes=scratch(near),
+        cost_estimate=cost(near),
+        compiler_params=params(),
+    )(*left, *right[:BESIDE])
+    far_block, first = pl.pallas_call(
+        second_half,
+        in_specs=[smem] + [vmem] * (4 + COLUMNS - BESIDE),
+        out_shape=(sds((rows, far), bf16), sds((COLUMNS, COLUMNS, NPOL, TILE), f32)),
+        scratch_shapes=scratch(far),
+        cost_estimate=cost(far),
+        compiler_params=params(),
+    )(*left, done, *right[BESIDE:])
     parts = exchange(first, COLUMN)
     image_parts, side = pl.pallas_call(
         second_kernel,
-        in_specs=[smem] + [vmem] * (3 + COLUMNS),
+        in_specs=[smem] + [vmem] * (4 + COLUMNS),
         out_shape=(sds((LEFT, NPOL, TILE), f32), sds((NPOL, TILE), f32)),
-        scratch_shapes=[pltpu.VMEM((width, TILE), bf16)],
-        compiler_params=params(),
-    )(place, kernel, parts, own, other, *right)
+        scratch_shapes=[pltpu.VMEM((COLUMNS * TILE, TILE), bf16)],
+        compiler_params=params(),
+    )(place, near_block, far_block, parts, own, other, *right)
     image_parts = exchange(image_parts, PLANE + ("core",))
 
     count = LEFT * COLUMNS

time: 93.9 us -> 92.4 us (0.984)
  starting transfers between devices: 25 us -> 29.2 us
  blocking collectives: 49.5 us -> 45.5 us
  waiting for transfers between devices: 6.34 us -> 3.96 us
    ppermute x7, starting transfers between devices: 15.1 us -> 19.4 us  [on_device(): lax.ppermute(mine, COLUMN, ring(shift))]
    all_to_all x3, blocking collectives: 49.5 us -> 45.5 us  [exchange(): return lax.all_to_all(value, axes, 0, 0)]
    ppermute x7, waiting for transfers between devices: 6.34 us -> 3.95 us  [on_device(): lax.ppermute(mine, COLUMN, ring(shift))]
    pallas_call x3 -> x4, Pallas kernels: 9.38 us -> 9.95 us  [the longest x1 3.14 us: on_device(): pl.pallas_call(second_kernel, in_specs=[smem] + [vmem] * (4 + COLUMNS), o...]
  transfers between devices with their start and end apart: 9 -> 9, of which waited for: 5 -> 2; matrix products, arithmetic and copies ran while one was open for 0% -> 0% of each run, Pallas kernels for 1% -> 5%
where the time goes in v4:
time: 92.4 us; the launch traced here: 92 us
  blocking collectives  45.5 us (49%)
  starting transfers between devices  29.2 us (32%)
  Pallas kernels  12.6 us (14%)
  waiting for transfers between devices  3.96 us (4%)
    all_to_all x3, blocking collectives, exchange(): return lax.all_to_all(value, axes, 0, 0)  45.5 us
    ppermute x7, starting transfers between devices, on_device(): lax.ppermute(mine, COLUMN, ring(shift))  19.4 us
    all_to_all x1, starting transfers between devices, exchange(): return lax.all_to_all(value, axes, 0, 0)  7.6 us
    ppermute x7, waiting for transfers between devices, on_device(): lax.ppermute(mine, COLUMN, ring(shift))  3.95 us
    pallas_call x1, Pallas kernels, on_device(): pl.pallas_call(second_kernel, in_specs=[smem] + [vmem] * (4 + COLUMNS), o...  3.14 us
    pallas_call x1, Pallas kernels, on_device(): pl.pallas_call(second_half, in_specs=[smem] + [vmem] * (4 + COLUMNS - BES...  2.59 us
    pallas_call x1, Pallas kernels, on_device(): pl.pallas_call(first_half, in_specs=[smem] + [vmem] * (4 + BESIDE), out_s...  2.58 us
    ppermute x1, starting transfers between devices, on_device(): other = lax.ppermute(own, 'core', [(0, 1), (1, 0)])  2.21 us
  transfers between devices with their start and end apart: 9, of which 2 were waited for; matrix products, arithmetic and copies ran while one was open for 0% of the time, Pallas kernels for 5%

profile of v4, /device:TPU:1, one launch (start us, length us, event | category | flops | bytes accessed | tf_op | source)
XLA Modules:
  0.0 92.0 jit_solution(10654166741055811740)
XLA Ops:
  0.6 1.8 %shard_map.67 = (bf16[16,160,128]{2,1,0:T(8,128)(2,1)}, bf16[144,128]{1,0:T(8,128)(2,1)}) custom-call(bf16[128,128]{1,0:T(8,128)(2,1)} %ctx_hbm.1, s32[1,128]{1,0:T(1,128)} %bitcast.17, s32[8,128]{1,0:T(8,128)} %bitcast.16), custom_call_target="tpu_custom_call" | custom-call | tf_op jit(solution)/shard_map/pallas_call | solution.py:276
  2.4 7.6 %all-to-all-start = ((bf16[16,160,128]{2,1,0:T(8,128)(2,1)}), bf16[16,160,128]{2,1,0:T(8,128)(2,1)S(1)}, u32[]{:S(2)}, u32[]{:S(2)}) async-start(bf16[16,160,128]{2,1,0:T(8,128)(2,1)} %get-tuple-element.22), calls=%async_computation | async-start | bytes 1310720 | tf_op jit(solution)/shard_map/all_to_all | solution.py:265
  10.0 4.4 %collective-permute-start.2 = (bf16[144,128]{1,0:T(8,128)(2,1)}, bf16[144,128]{1,0:T(8,128)(2,1)S(1)}, u32[]{:S(2)}, u32[]{:S(2)}) collective-permute-start(bf16[144,128]{1,0:T(8,128)(2,1)} %get-tuple-element.23), channel_id=1, source_target_pairs={{0,24},{8,128},{16,136},{24,144},{128,152},{136,0},{144,8},{152,16... | collective-permute-start | bytes 110600 | tf_op jit(solution)/shard_map/ppermute | solution.py:289
  14.4 3.3 %collective-permute-start.1 = (bf16[144,128]{1,0:T(8,128)(2,1)}, bf16[144,128]{1,0:T(8,128)(2,1)S(1)}, u32[]{:S(2)}, u32[]{:S(2)}) collective-permute-start(bf16[144,128]{1,0:T(8,128)(2,1)} %get-tuple-element.23), channel_id=1, source_target_pairs={{0,16},{8,24},{16,128},{24,136},{128,144},{136,152},{144,0},{152,8... | collective-permute-start | bytes 110600 | tf_op jit(solution)/shard_map/ppermute | solution.py:289
  17.7 0.7 collective-permute-start
  18.5 0.0 collective-permute-done.2.refs_2_
  18.5 2.2 %collective-permute-done.1.refs_1_ = bf16[144,128]{1,0:T(8,128)(2,1)S(1)} collective-permute-done((bf16[144,128]{1,0:T(8,128)(2,1)}, bf16[144,128]{1,0:T(8,128)(2,1)S(1)}, u32[]{:S(2)}, u32[]{:S(2)}) %collective-permute-start.1) | collective-permute-done | bytes 36896 | tf_op jit(solution)/shard_map/ppermute | solution.py:289
  20.7 1.7 %collective-permute-done.refs_0_ = bf16[144,128]{1,0:T(8,128)(2,1)S(1)} collective-permute-done((bf16[144,128]{1,0:T(8,128)(2,1)}, bf16[144,128]{1,0:T(8,128)(2,1)S(1)}, u32[]{:S(2)}, u32[]{:S(2)}) %collective-permute-start) | collective-permute-done | bytes 36896 | tf_op jit(solution)/shard_map/ppermute | solution.py:289
  22.4 0.0 all-to-all-done.own_ref
  22.4 2.2 %collective-permute-start.3 = (bf16[16,160,128]{2,1,0:T(8,128)(2,1)S(1)}, bf16[16,160,128]{2,1,0:T(8,128)(2,1)S(1)}, u32[]{:S(2)}, u32[]{:S(2)}) collective-permute-start(bf16[16,160,128]{2,1,0:T(8,128)(2,1)S(1)} %all-to-all-done.own_ref), channel_id=1, source_target_pairs={{0,1},{1,0},{2,3},{3,2},{4,5},{5,4},{6,7},{7,6},{8,9},{9,8},{10,11... | collective-permute-start | bytes 1966088 | tf_op jit(solution)/shard_map/ppermute | solution.py:291
  24.6 4.8 %collective-permute-start.7 = (bf16[144,128]{1,0:T(8,128)(2,1)}, bf16[144,128]{1,0:T(8,128)(2,1)S(1)}, u32[]{:S(2)}, u32[]{:S(2)}) collective-permute-start(bf16[144,128]{1,0:T(8,128)(2,1)} %get-tuple-element.23), channel_id=1, source_target_pairs={{0,152},{8,0},{16,8},{24,16},{128,24},{136,128},{144,136},{152,144... | collective-permute-start | bytes 110600 | tf_op jit(solution)/shard_map/ppermute | solution.py:289
  29.4 1.2 %collective-permute-start.6 = (bf16[144,128]{1,0:T(8,128)(2,1)}, bf16[144,128]{1,0:T(8,128)(2,1)S(1)}, u32[]{:S(2)}, u32[]{:S(2)}) collective-permute-start(bf16[144,128]{1,0:T(8,128)(2,1)} %get-tuple-element.23), channel_id=1, source_target_pairs={{0,144},{8,152},{16,0},{24,8},{128,16},{136,24},{144,128},{152,136... | collective-permute-start | bytes 110600 | tf_op jit(solution)/shard_map/ppermute | solution.py:289
  30.6 0.4 collective-permute-start.5
  31.1 4.5 %collective-permute-start.4 = (bf16[144,128]{1,0:T(8,128)(2,1)}, bf16[144,128]{1,0:T(8,128)(2,1)S(1)}, u32[]{:S(2)}, u32[]{:S(2)}) collective-permute-start(bf16[144,128]{1,0:T(8,128)(2,1)} %get-tuple-element.23), channel_id=1, source_target_pairs={{0,128},{8,136},{16,144},{24,152},{128,0},{136,8},{144,16},{152,24... | collective-permute-start | bytes 110600 | tf_op jit(solution)/shard_map/ppermute | solution.py:289
  35.5 0.1 pad_add_fusion.place_ref
  35.6 0.0 collective-permute-done.3.other_ref
  35.6 1.6 %shard_map.68 = (bf16[128,4096]{1,0:T(8,128)(2,1)S(1)}, bf16[32,128,128]{2,1,0:T(8,128)(2,1)S(1)}) custom-call(bf16[16,160,128]{2,1,0:T(8,128)(2,1)S(1)} %all-to-all-done.own_ref, bf16[16,160,128]{2,1,0:T(8,128)(2,1)S(1)} %collective-permute-done.3.other_ref), custom_call_target="tpu_custom_call" | custom-call | flops 60000000 | bytes 3000000 | tf_op jit(solution)/shard_map/pallas_call | solution.py:293
  37.3 2.6 %shard_map.69 = (bf16[4096,512]{1,0:T(8,128)(2,1)S(1)}, f32[4,8,128]{2,1,0:T(8,128)S(1)}) custom-call(s32[3]{0:T(128)S(1)} %pad_add_fusion.place_ref, bf16[16,160,128]{2,1,0:T(8,128)(2,1)S(1)} %all-to-all-done.own_ref, bf16[16,160,128]{2,1,0:T(8,128)(2,1)S(1)} %collective-permute-done.3.other_ref, bf16[128,4096]{1,0:T(8,128)(2,1)S(1)} %get-tuple-element.25.policy_ref, ...), custom_call_target="tpu_custom_call" | custom-call | flops 1610612736 | bytes 8388608 | tf_op jit(solution)/shard_map/pallas_call | solution.py:309
  39.9 0.0 collective-permute-done.7.refs_3_.refs_6_
  39.9 0.0 collective-permute-done.6.refs_2_.refs_5_
  39.9 0.0 collective-permute-done.5.refs_1_.refs_4_
  39.9 0.0 collective-permute-done.4.refs_0_.refs_3_
  39.9 2.6 %shard_map.70 = (bf16[4096,512]{1,0:T(8,128)(2,1)S(1)}, f32[8,8,8,128]{3,2,1,0:T(8,128)S(1)}) custom-call(s32[3]{0:T(128)S(1)} %pad_add_fusion.place_ref, bf16[16,160,128]{2,1,0:T(8,128)(2,1)S(1)} %all-to-all-done.own_ref, bf16[16,160,128]{2,1,0:T(8,128)(2,1)S(1)} %collective-permute-done.3.other_ref, bf16[128,4096]{1,0:T(8,128)(2,1)S(1)} %get-tuple-element.25.policy_ref, ...), custom_call_target="tpu_custom_call" | custom-call | flops 1610612736 | bytes 8388608 | tf_op jit(solution)/shard_map/pallas_call | solution.py:317
  42.5 13.1 %all_to_all.20.parts_ref = f32[8,8,8,128]{3,2,1,0:T(8,128)S(1)} all-to-all(f32[8,8,8,128]{3,2,1,0:T(8,128)S(1)} %get-tuple-element.33), channel_id=1, replica_groups=mesh['z_hi'=2,'x'=4,'z_lo'=4,'y'=4,'core'=2] {'z_hi','z_lo'}, dimensions={0} | all-to-all | bytes 524288 | tf_op jit(solution)/shard_map/all_to_all | solution.py:265
  55.6 0.0 copy-start
  55.6 3.1 %shard_map.71 = (f32[32,8,128]{2,1,0:T(8,128)S(1)}, f32[8,128]{1,0:T(8,128)S(1)}) custom-call(s32[3]{0:T(128)S(1)} %pad_add_fusion.place_ref, bf16[4096,512]{1,0:T(8,128)(2,1)S(1)} %get-tuple-element.30.near_ref, bf16[4096,512]{1,0:T(8,128)(2,1)S(1)} %get-tuple-element.32.far_ref, f32[8,8,8,128]{3,2,1,0:T(8,128)S(1)} %all_to_all.20.parts_ref, ...), custom_call_target="tpu_custom_call" | custom-call | tf_op jit(solution)/shard_map/pallas_call | solution.py:326
  58.7 14.5 %all_to_all.21.parts_ref = f32[32,8,128]{2,1,0:T(8,128)S(1)} all-to-all(f32[32,8,128]{2,1,0:T(8,128)S(1)} %get-tuple-element.34), channel_id=1, replica_groups=mesh['z_hi'=2,'x'=4,'z_lo'=4,'y'=4,'core'=2] {'x','y','core'}, dimensions={0} | all-to-all | bytes 262144 | tf_op jit(solution)/shard_map/all_to_all | solution.py:265
  73.3 0.0 copy-done
  73.3 0.1 shard_map.72
  73.4 17.9 %all_to_all.22 = f32[256,1,128]{2,1,0:T(1,128)S(1)} all-to-all(f32[256,1,128]{2,1,0:T(1,128)S(1)} %bitcast.14), channel_id=1, replica_groups=mesh['z_hi'=2,'x'=4,'z_lo'=4,'y'=4,'core'=2] {'z_hi','x','z_lo','y','core'}, dimensions={0} | all-to-all | bytes 262144 | tf_op jit(solution)/shard_map/all_to_all | solution.py:265
  91.3 0.7 shard_map.73
Async XLA Ops:
  2.4 20.0 %all-to-all-start = ((bf16[16,160,128]{2,1,0:T(8,128)(2,1)}), bf16[16,160,128]{2,1,0:T(8,128)(2,1)S(1)}, u32[]{:S(2)}, u32[]{:S(2)}) async-start(bf16[16,160,128]{2,1,0:T(8,128)(2,1)} %get-tuple-element.22), calls=%async_computation | async-start | bytes 1310720 | tf_op jit(solution)/shard_map/all_to_all | solution.py:265
  10.0 8.5 %collective-permute-start.2 = (bf16[144,128]{1,0:T(8,128)(2,1)}, bf16[144,128]{1,0:T(8,128)(2,1)S(1)}, u32[]{:S(2)}, u32[]{:S(2)}) collective-permute-start(bf16[144,128]{1,0:T(8,128)(2,1)} %get-tuple-element.23), channel_id=1, source_target_pairs={{0,24},{8,128},{16,136},{24,144},{128,152},{136,0},{144,8},{152,16... | collective-permute-start | bytes 110600 | tf_op jit(solution)/shard_map/ppermute | solution.py:289
  14.4 6.3 %collective-permute-start.1 = (bf16[144,128]{1,0:T(8,128)(2,1)}, bf16[144,128]{1,0:T(8,128)(2,1)S(1)}, u32[]{:S(2)}, u32[]{:S(2)}) collective-permute-start(bf16[144,128]{1,0:T(8,128)(2,1)} %get-tuple-element.23), channel_id=1, source_target_pairs={{0,16},{8,24},{16,128},{24,136},{128,144},{136,152},{144,0},{152,8... | collective-permute-start | bytes 110600 | tf_op jit(solution)/shard_map/ppermute | solution.py:289
  17.7 4.7 %collective-permute-start = (bf16[144,128]{1,0:T(8,128)(2,1)}, bf16[144,128]{1,0:T(8,128)(2,1)S(1)}, u32[]{:S(2)}, u32[]{:S(2)}) collective-permute-start(bf16[144,128]{1,0:T(8,128)(2,1)} %get-tuple-element.23), channel_id=1, source_target_pairs={{0,8},{8,16},{16,24},{24,128},{128,136},{136,144},{144,152},{152,0... | collective-permute-start | bytes 110600 | tf_op jit(solution)/shard_map/ppermute | solution.py:289
  22.4 13.2 %collective-permute-start.3 = (bf16[16,160,128]{2,1,0:T(8,128)(2,1)S(1)}, bf16[16,160,128]{2,1,0:T(8,128)(2,1)S(1)}, u32[]{:S(2)}, u32[]{:S(2)}) collective-permute-start(bf16[16,160,128]{2,1,0:T(8,128)(2,1)S(1)} %all-to-all-done.own_ref), channel_id=1, source_target_pairs={{0,1},{1,0},{2,3},{3,2},{4,5},{5,4},{6,7},{7,6},{8,9},{9,8},{10,11... | collective-permute-start | bytes 1966088 | tf_op jit(solution)/shard_map/ppermute | solution.py:291
  24.6 15.2 %collective-permute-start.7 = (bf16[144,128]{1,0:T(8,128)(2,1)}, bf16[144,128]{1,0:T(8,128)(2,1)S(1)}, u32[]{:S(2)}, u32[]{:S(2)}) collective-permute-start(bf16[144,128]{1,0:T(8,128)(2,1)} %get-tuple-element.23), channel_id=1, source_target_pairs={{0,152},{8,0},{16,8},{24,16},{128,24},{136,128},{144,136},{152,144... | collective-permute-start | bytes 110600 | tf_op jit(solution)/shard_map/ppermute | solution.py:289
  29.4 10.4 %collective-permute-start.6 = (bf16[144,128]{1,0:T(8,128)(2,1)}, bf16[144,128]{1,0:T(8,128)(2,1)S(1)}, u32[]{:S(2)}, u32[]{:S(2)}) collective-permute-start(bf16[144,128]{1,0:T(8,128)(2,1)} %get-tuple-element.23), channel_id=1, source_target_pairs={{0,144},{8,152},{16,0},{24,8},{128,16},{136,24},{144,128},{152,136... | collective-permute-start | bytes 110600 | tf_op jit(solution)/shard_map/ppermute | solution.py:289
  30.6 9.3 %collective-permute-start.5 = (bf16[144,128]{1,0:T(8,128)(2,1)}, bf16[144,128]{1,0:T(8,128)(2,1)S(1)}, u32[]{:S(2)}, u32[]{:S(2)}) collective-permute-start(bf16[144,128]{1,0:T(8,128)(2,1)} %get-tuple-element.23), channel_id=1, source_target_pairs={{0,136},{8,144},{16,152},{24,0},{128,8},{136,16},{144,24},{152,128... | collective-permute-start | bytes 110600 | tf_op jit(solution)/shard_map/ppermute | solution.py:289
  31.1 8.8 %collective-permute-start.4 = (bf16[144,128]{1,0:T(8,128)(2,1)}, bf16[144,128]{1,0:T(8,128)(2,1)S(1)}, u32[]{:S(2)}, u32[]{:S(2)}) collective-permute-start(bf16[144,128]{1,0:T(8,128)(2,1)} %get-tuple-element.23), channel_id=1, source_target_pairs={{0,128},{8,136},{16,144},{24,152},{128,0},{136,8},{144,16},{152,24... | collective-permute-start | bytes 110600 | tf_op jit(solution)/shard_map/ppermute | solution.py:289
  55.6 17.7 %copy-start = (f32[128]{0:T(128)S(1)}, f32[128]{0:T(128)}, u32[]{:S(2)}) copy-start(f32[128]{0:T(128)} %param.7) | copy-start | bytes 1540

commit v5 on v4

--- a/solution.py
+++ b/solution.py
@@ -122,12 +122,18 @@
 
 SCALE = math.log2(math.e) / D
 CHUNK = 8
-BESIDE = 3
+BESIDE = 1
+NEAR = 2 + 2 * BESIDE
 SPAN = 2 * CHUNK * TILE
 
 
-def home(place_ref, shift):
-    return lax.rem(place_ref[1] + (COLUMNS - shift), COLUMNS)
+def home(place_ref, at):
+    upper, lower = place_ref[1] >> 2, place_ref[1] & 3
+    return (((upper + at % 2) & 1) << 2) + ((lower + 4 - at // 2) & 3)
+
+
+def pairs(own_ref, place_ref, partner_ref, moved):
+    return [own_ref.at[place_ref[2]], partner_ref] + [ref.at[i] for ref in moved for i in range(2)]
 
 
 def block(left_refs, right_refs, kernel_ref, acc, cols):
@@ -173,17 +179,17 @@
 
 
 def first_half(place_ref, own_ref, other_ref, policy_ref, extra_ref, *refs):
-    right_refs = (own_ref.at[place_ref[2]], *refs[:BESIDE])
-    kernel_ref, sums_ref, acc, cols = refs[BESIDE:]
+    right_refs = pairs(own_ref, place_ref, refs[0], refs[1 : 1 + BESIDE])
+    kernel_ref, sums_ref, acc, cols = refs[1 + BESIDE :]
     for b, total in enumerate(block((own_ref, other_ref, policy_ref, extra_ref), right_refs, kernel_ref, acc, cols)):
         sums_ref[b] = total
 
 
 def second_half(place_ref, own_ref, other_ref, policy_ref, extra_ref, done_ref, *refs):
-    right_refs = refs[: COLUMNS - 1 - BESIDE]
-    kernel_ref, sums_ref, acc, cols = refs[COLUMNS - 1 - BESIDE :]
+    right_refs = [ref.at[i] for ref in refs[: 3 - BESIDE] for i in range(2)]
+    kernel_ref, sums_ref, acc, cols = refs[3 - BESIDE :]
     totals = block((own_ref, other_ref, policy_ref, extra_ref), right_refs, kernel_ref, acc, cols)
-    totals = [done_ref[b] for b in range(BESIDE + 1)] + totals
+    totals = [done_ref[b] for b in range(NEAR)] + totals
     for b, total in enumerate(totals):
         at = home(place_ref, b)
         for peer in range(COLUMNS):
@@ -191,8 +197,8 @@
 
 
 def second_kernel(place_ref, near_ref, far_ref, parts_ref, own_ref, other_ref, *refs):
-    right_refs = (own_ref.at[place_ref[2]], *refs[: COLUMNS - 1])
-    image_ref, side_ref, matched = refs[COLUMNS - 1 :]
+    right_refs = pairs(own_ref, place_ref, refs[0], refs[1:4])
+    image_ref, side_ref, matched = refs[4:]
     factor = NACT / (TILE * LEFT * COLUMNS)
     for b, right_ref in enumerate(right_refs):
         at = home(place_ref, b)
@@ -207,7 +213,7 @@
         made = jnp.concatenate([chosen[c : c + 1] * low for c in range(NACT)], axis=0)
         matched[b * TILE : (b + 1) * TILE, :] = jnp.transpose(made).astype(bf16)
     core = place_ref[0]
-    cut = (BESIDE + 1) * TILE
+    cut = NEAR * TILE
     for step in range(PLANES // CHUNK):
         whole = slice(step * SPAN, (step + 1) * SPAN)
         out = jnp.dot(near_ref[whole, :], matched[:cut, :], preferred_element_type=f32)
@@ -285,9 +291,10 @@
         ],
         compiler_params=params(60 * MIB),
     )(contexts, logged_actions.reshape(1, TILE), policy_actions.T)
-    ring = lambda shift: [(i, (i + shift) % COLUMNS) for i in range(COLUMNS)]
-    right = [lax.ppermute(mine, COLUMN, ring(shift)) for shift in range(1, COLUMNS)]
-    own, *right[:BESIDE] = lax.optimization_barrier((exchange(plane_send, PLANE), *right[:BESIDE]))
+    partner = lax.ppermute(mine, "z_hi", [(0, 1), (1, 0)])
+    pair = jnp.stack([mine, partner])
+    moved = [lax.ppermute(pair, "z_lo", [(i, (i + shift) % 4) for i in range(4)]) for shift in range(1, 4)]
+    own, partner, *moved[:BESIDE] = lax.optimization_barrier((exchange(plane_send, PLANE), partner, *moved[:BESIDE]))
     other = lax.ppermute(own, "core", [(0, 1), (1, 0)])
 
     policy, extra = pl.pallas_call(
@@ -304,32 +311,32 @@
             flops=2 * rows * width * (2 * D + TILE), bytes_accessed=2 * rows * (width + 4 * D), transcendentals=rows * width
         )
 
-    near, far = (BESIDE + 1) * TILE, (COLUMNS - 1 - BESIDE) * TILE
+    near, far = NEAR * TILE, (COLUMNS - NEAR) * TILE
     scratch = lambda width: [pltpu.VMEM((TILE, width), f32), pltpu.VMEM((width, 2 * D), bf16)]
     near_block, done = pl.pallas_call(
         first_half,
-        in_specs=[smem] + [vmem] * (4 + BESIDE),
-        out_shape=(sds((rows, near), bf16), sds((BESIDE + 1, NPOL, TILE), f32)),
+        in_specs=[smem] + [vmem] * (5 + BESIDE),
+        out_shape=(sds((rows, near), bf16), sds((NEAR, NPOL, TILE), f32)),
         scratch_shapes=scratch(near),
         cost_estimate=cost(near),
         compiler_params=params(),
-    )(*left, *right[:BESIDE])
+    )(*left, partner, *moved[:BESIDE])
     far_block, first = pl.pallas_call(
         second_half,
-        in_specs=[smem] + [vmem] * (4 + COLUMNS - BESIDE),
+        in_specs=[smem] + [vmem] * (8 - BESIDE),
         out_shape=(sds((rows, far), bf16), sds((COLUMNS, COLUMNS, NPOL, TILE), f32)),
         scratch_shapes=scratch(far),
         cost_estimate=cost(far),
         compiler_params=params(),
-    )(*left, done, *right[BESIDE:])
+    )(*left, done, *moved[BESIDE:])
     parts = exchange(first, COLUMN)
     image_parts, side = pl.pallas_call(
         second_kernel,
-        in_specs=[smem] + [vmem] * (4 + COLUMNS),
+        in_specs=[smem] + [vmem] * 9,
         out_shape=(sds((LEFT, NPOL, TILE), f32), sds((NPOL, TILE), f32)),
         scratch_shapes=[pltpu.VMEM((COLUMNS * TILE, TILE), bf16)],
         compiler_params=params(),
-    )(place, near_block, far_block, parts, own, other, *right)
+    )(place, near_block, far_block, parts, own, other, partner, *moved)
     image_parts = exchange(image_parts, PLANE + ("core",))
 
     count = LEFT * COLUMNS

time: 92.4 us -> 93.1 us (level)
  starting transfers between devices: 29.2 us -> 19.6 us
  blocking collectives: 45.5 us -> 50.7 us
  waiting for transfers between devices: 3.96 us -> 8.2 us
    ppermute x7 -> x4, starting transfers between devices: 19.4 us -> 8.99 us  [the longest x1 7 us: on_device(): partner = lax.ppermute(mine, 'z_hi', [(0, 1), (1, 0)])]
    all_to_all x3, blocking collectives: 45.5 us -> 50.7 us  [exchange(): return lax.all_to_all(value, axes, 0, 0)]
    ppermute x7 -> x4, waiting for transfers between devices: 3.95 us -> 7.8 us  [the longest x3 6.25 us: on_device(): lax.ppermute(pair, 'z_lo', [(i, (i + shift) % 4) for i in range(4)])]
  transfers between devices with their start and end apart: 9 -> 6, of which waited for: 2 -> 4; matrix products, arithmetic and copies ran while one was open for 0% -> 1% of each run, Pallas kernels for 5% -> 5%
where the time goes in v5:
time: 93.1 us; the launch traced here: 92.7 us
  blocking collectives  50.7 us (54%)
  starting transfers between devices  19.6 us (21%)
  Pallas kernels  12.7 us (14%)
  waiting for transfers between devices  8.2 us (9%)
    all_to_all x3, blocking collectives, exchange(): return lax.all_to_all(value, axes, 0, 0)  50.7 us
    all_to_all x1, starting transfers between devices, exchange(): return lax.all_to_all(value, axes, 0, 0)  7.6 us
    ppermute x1, starting transfers between devices, on_device(): partner = lax.ppermute(mine, 'z_hi', [(0, 1), (1, 0)])  7 us
    ppermute x3, waiting for transfers between devices, on_device(): lax.ppermute(pair, 'z_lo', [(i, (i + shift) % 4) for i in range(4)])  6.25 us
    pallas_call x1, Pallas kernels, on_device(): pl.pallas_call(second_kernel, in_specs=[smem] + [vmem] * 9, out_shape=(sd...  3.21 us
    ppermute x1, starting transfers between devices, on_device(): other = lax.ppermute(own, 'core', [(0, 1), (1, 0)])  3.02 us
    pallas_call x1, Pallas kernels, on_device(): pl.pallas_call(second_half, in_specs=[smem] + [vmem] * (8 - BESIDE), out_...  2.6 us
    pallas_call x1, Pallas kernels, on_device(): pl.pallas_call(first_half, in_specs=[smem] + [vmem] * (5 + BESIDE), out_s...  2.59 us
  transfers between devices with their start and end apart: 6, of which 4 were waited for; matrix products, arithmetic and copies ran while one was open for 1% of the time, Pallas kernels for 5%

profile of v5, /device:TPU:1, one launch (start us, length us, event | category | flops | bytes accessed | tf_op | source)
XLA Modules:
  0.0 92.7 jit_solution(11336546627383264302)
XLA Ops:
  0.6 1.8 %shard_map.67 = (bf16[16,160,128]{2,1,0:T(8,128)(2,1)}, bf16[144,128]{1,0:T(8,128)(2,1)}) custom-call(bf16[128,128]{1,0:T(8,128)(2,1)} %ctx_hbm.1, s32[1,128]{1,0:T(1,128)} %bitcast.21, s32[8,128]{1,0:T(8,128)} %bitcast.20), custom_call_target="tpu_custom_call" | custom-call | tf_op jit(solution)/shard_map/pallas_call | solution.py:282
  2.4 7.6 %all-to-all-start = ((bf16[16,160,128]{2,1,0:T(8,128)(2,1)}), bf16[16,160,128]{2,1,0:T(8,128)(2,1)S(1)}, u32[]{:S(2)}, u32[]{:S(2)}) async-start(bf16[16,160,128]{2,1,0:T(8,128)(2,1)} %get-tuple-element.21), calls=%async_computation | async-start | bytes 1310720 | tf_op jit(solution)/shard_map/all_to_all | solution.py:271
  10.0 7.0 %collective-permute-start = (bf16[144,128]{1,0:T(8,128)(2,1)}, bf16[144,128]{1,0:T(8,128)(2,1)S(1)}, u32[]{:S(2)}, u32[]{:S(2)}) collective-permute-start(bf16[144,128]{1,0:T(8,128)(2,1)} %get-tuple-element.22), channel_id=1, source_target_pairs={{0,128},{128,0},{1,129},{129,1},{2,130},{130,2},{3,131},{131,3},{4... | collective-permute-start | bytes 110600 | tf_op jit(solution)/shard_map/ppermute | solution.py:294
  17.0 1.6 %collective-permute-done.refs_0_ = bf16[144,128]{1,0:T(8,128)(2,1)S(1)} collective-permute-done((bf16[144,128]{1,0:T(8,128)(2,1)}, bf16[144,128]{1,0:T(8,128)(2,1)S(1)}, u32[]{:S(2)}, u32[]{:S(2)}) %collective-permute-start) | collective-permute-done | bytes 36896 | tf_op jit(solution)/shard_map/ppermute | solution.py:294
  18.6 0.8 pad_maximum_fusion
  19.3 0.7 collective-permute-start.1
  20.1 4.3 %collective-permute-done.1.refs_1_ = bf16[2,144,128]{2,1,0:T(8,128)(2,1)S(1)} collective-permute-done((bf16[2,144,128]{2,1,0:T(8,128)(2,1)S(1)}, bf16[2,144,128]{2,1,0:T(8,128)(2,1)S(1)}, u32[]{:S(2)}, u32[]{:S(2)}) %collective-permute-start.1) | collective-permute-done | bytes 73760 | tf_op jit(solution)/shard_map/ppermute | solution.py:296
  24.3 0.0 all-to-all-done.own_ref
  24.3 3.0 %collective-permute-start.2 = (bf16[16,160,128]{2,1,0:T(8,128)(2,1)S(1)}, bf16[16,160,128]{2,1,0:T(8,128)(2,1)S(1)}, u32[]{:S(2)}, u32[]{:S(2)}) collective-permute-start(bf16[16,160,128]{2,1,0:T(8,128)(2,1)S(1)} %all-to-all-done.own_ref), channel_id=1, source_target_pairs={{0,1},{1,0},{2,3},{3,2},{4,5},{5,4},{6,7},{7,6},{8,9},{9,8},{10,11... | collective-permute-start | bytes 1966088 | tf_op jit(solution)/shard_map/ppermute | solution.py:298
  27.4 0.1 pad_add_fusion.place_ref
  27.4 1.3 %collective-permute-start.4 = (bf16[2,144,128]{2,1,0:T(8,128)(2,1)S(1)}, bf16[2,144,128]{2,1,0:T(8,128)(2,1)S(1)}, u32[]{:S(2)}, u32[]{:S(2)}) collective-permute-start(bf16[2,144,128]{2,1,0:T(8,128)(2,1)S(1)} %pad_maximum_fusion), channel_id=1, source_target_pairs={{0,24},{8,0},{16,8},{24,16},{1,25},{9,1},{17,9},{25,17},{2,26},{10... | collective-permute-start | bytes 221192 | tf_op jit(solution)/shard_map/ppermute | solution.py:296
  28.7 0.0 collective-permute-start.3
  28.7 0.4 collective-permute-done.2.other_ref
  29.1 1.6 %shard_map.68 = (bf16[128,4096]{1,0:T(8,128)(2,1)S(1)}, bf16[32,128,128]{2,1,0:T(8,128)(2,1)S(1)}) custom-call(bf16[16,160,128]{2,1,0:T(8,128)(2,1)S(1)} %all-to-all-done.own_ref, bf16[16,160,128]{2,1,0:T(8,128)(2,1)S(1)} %collective-permute-done.2.other_ref), custom_call_target="tpu_custom_call" | custom-call | flops 60000000 | bytes 3000000 | tf_op jit(solution)/shard_map/pallas_call | solution.py:300
  30.7 2.6 %shard_map.69 = (bf16[4096,512]{1,0:T(8,128)(2,1)S(1)}, f32[4,8,128]{2,1,0:T(8,128)S(1)}) custom-call(s32[3]{0:T(128)S(1)} %pad_add_fusion.place_ref, bf16[16,160,128]{2,1,0:T(8,128)(2,1)S(1)} %all-to-all-done.own_ref, bf16[16,160,128]{2,1,0:T(8,128)(2,1)S(1)} %collective-permute-done.2.other_ref, bf16[128,4096]{1,0:T(8,128)(2,1)S(1)} %get-tuple-element.24.policy_ref, ...), custom_call_target="tpu_custom_call" | custom-call | flops 1610612736 | bytes 8388608 | tf_op jit(solution)/shard_map/pallas_call | solution.py:316
  33.3 0.0 collective-permute-done.4.refs_1_.refs_3_
  33.4 2.0 %collective-permute-done.3.refs_0_.refs_2_ = bf16[2,144,128]{2,1,0:T(8,128)(2,1)S(1)} collective-permute-done((bf16[2,144,128]{2,1,0:T(8,128)(2,1)S(1)}, bf16[2,144,128]{2,1,0:T(8,128)(2,1)S(1)}, u32[]{:S(2)}, u32[]{:S(2)}) %collective-permute-start.3) | collective-permute-done | bytes 73760 | tf_op jit(solution)/shard_map/ppermute | solution.py:296
  35.3 2.6 %shard_map.70 = (bf16[4096,512]{1,0:T(8,128)(2,1)S(1)}, f32[8,8,8,128]{3,2,1,0:T(8,128)S(1)}) custom-call(s32[3]{0:T(128)S(1)} %pad_add_fusion.place_ref, bf16[16,160,128]{2,1,0:T(8,128)(2,1)S(1)} %all-to-all-done.own_ref, bf16[16,160,128]{2,1,0:T(8,128)(2,1)S(1)} %collective-permute-done.2.other_ref, bf16[128,4096]{1,0:T(8,128)(2,1)S(1)} %get-tuple-element.24.policy_ref, ...), custom_call_target="tpu_custom_call" | custom-call | flops 1610612736 | bytes 8388608 | tf_op jit(solution)/shard_map/pallas_call | solution.py:324
  37.9 15.5 %all_to_all.20.parts_ref = f32[8,8,8,128]{3,2,1,0:T(8,128)S(1)} all-to-all(f32[8,8,8,128]{3,2,1,0:T(8,128)S(1)} %get-tuple-element.31), channel_id=1, replica_groups=mesh['z_hi'=2,'x'=4,'z_lo'=4,'y'=4,'core'=2] {'z_hi','z_lo'}, dimensions={0} | all-to-all | bytes 524288 | tf_op jit(solution)/shard_map/all_to_all | solution.py:271
  53.4 0.0 copy-start
  53.4 3.2 %shard_map.71 = (f32[32,8,128]{2,1,0:T(8,128)S(1)}, f32[8,128]{1,0:T(8,128)S(1)}) custom-call(s32[3]{0:T(128)S(1)} %pad_add_fusion.place_ref, bf16[4096,512]{1,0:T(8,128)(2,1)S(1)} %get-tuple-element.28.near_ref, bf16[4096,512]{1,0:T(8,128)(2,1)S(1)} %get-tuple-element.30.far_ref, f32[8,8,8,128]{3,2,1,0:T(8,128)S(1)} %all_to_all.20.parts_ref, ...), custom_call_target="tpu_custom_call" | custom-call | tf_op jit(solution)/shard_map/pallas_call | solution.py:333
  56.6 17.3 %all_to_all.21.parts_ref = f32[32,8,128]{2,1,0:T(8,128)S(1)} all-to-all(f32[32,8,128]{2,1,0:T(8,128)S(1)} %get-tuple-element.32), channel_id=1, replica_groups=mesh['z_hi'=2,'x'=4,'z_lo'=4,'y'=4,'core'=2] {'x','y','core'}, dimensions={0} | all-to-all | bytes 262144 | tf_op jit(solution)/shard_map/all_to_all | solution.py:271
  74.0 0.0 copy-done
  74.0 0.1 shard_map.72
  74.1 17.9 %all_to_all.22 = f32[256,1,128]{2,1,0:T(1,128)S(1)} all-to-all(f32[256,1,128]{2,1,0:T(1,128)S(1)} %bitcast.17), channel_id=1, replica_groups=mesh['z_hi'=2,'x'=4,'z_lo'=4,'y'=4,'core'=2] {'z_hi','x','z_lo','y','core'}, dimensions={0} | all-to-all | bytes 262144 | tf_op jit(solution)/shard_map/all_to_all | solution.py:271
  92.0 0.7 shard_map.73
Async XLA Ops:
  2.4 21.9 %all-to-all-start = ((bf16[16,160,128]{2,1,0:T(8,128)(2,1)}), bf16[16,160,128]{2,1,0:T(8,128)(2,1)S(1)}, u32[]{:S(2)}, u32[]{:S(2)}) async-start(bf16[16,160,128]{2,1,0:T(8,128)(2,1)} %get-tuple-element.21), calls=%async_computation | async-start | bytes 1310720 | tf_op jit(solution)/shard_map/all_to_all | solution.py:271
  10.0 8.6 %collective-permute-start = (bf16[144,128]{1,0:T(8,128)(2,1)}, bf16[144,128]{1,0:T(8,128)(2,1)S(1)}, u32[]{:S(2)}, u32[]{:S(2)}) collective-permute-start(bf16[144,128]{1,0:T(8,128)(2,1)} %get-tuple-element.22), channel_id=1, source_target_pairs={{0,128},{128,0},{1,129},{129,1},{2,130},{130,2},{3,131},{131,3},{4... | collective-permute-start | bytes 110600 | tf_op jit(solution)/shard_map/ppermute | solution.py:294
  19.3 5.0 %collective-permute-start.1 = (bf16[2,144,128]{2,1,0:T(8,128)(2,1)S(1)}, bf16[2,144,128]{2,1,0:T(8,128)(2,1)S(1)}, u32[]{:S(2)}, u32[]{:S(2)}) collective-permute-start(bf16[2,144,128]{2,1,0:T(8,128)(2,1)S(1)} %pad_maximum_fusion), channel_id=1, source_target_pairs={{0,8},{8,16},{16,24},{24,0},{1,9},{9,17},{17,25},{25,1},{2,10},{10... | collective-permute-start | bytes 221192 | tf_op jit(solution)/shard_map/ppermute | solution.py:296
  24.3 4.7 %collective-permute-start.2 = (bf16[16,160,128]{2,1,0:T(8,128)(2,1)S(1)}, bf16[16,160,128]{2,1,0:T(8,128)(2,1)S(1)}, u32[]{:S(2)}, u32[]{:S(2)}) collective-permute-start(bf16[16,160,128]{2,1,0:T(8,128)(2,1)S(1)} %all-to-all-done.own_ref), channel_id=1, source_target_pairs={{0,1},{1,0},{2,3},{3,2},{4,5},{5,4},{6,7},{7,6},{8,9},{9,8},{10,11... | collective-permute-start | bytes 1966088 | tf_op jit(solution)/shard_map/ppermute | solution.py:298
  27.4 5.9 %collective-permute-start.4 = (bf16[2,144,128]{2,1,0:T(8,128)(2,1)S(1)}, bf16[2,144,128]{2,1,0:T(8,128)(2,1)S(1)}, u32[]{:S(2)}, u32[]{:S(2)}) collective-permute-start(bf16[2,144,128]{2,1,0:T(8,128)(2,1)S(1)} %pad_maximum_fusion), channel_id=1, source_target_pairs={{0,24},{8,0},{16,8},{24,16},{1,25},{9,1},{17,9},{25,17},{2,26},{10... | collective-permute-start | bytes 221192 | tf_op jit(solution)/shard_map/ppermute | solution.py:296
  28.7 6.6 %collective-permute-start.3 = (bf16[2,144,128]{2,1,0:T(8,128)(2,1)S(1)}, bf16[2,144,128]{2,1,0:T(8,128)(2,1)S(1)}, u32[]{:S(2)}, u32[]{:S(2)}) collective-permute-start(bf16[2,144,128]{2,1,0:T(8,128)(2,1)S(1)} %pad_maximum_fusion), channel_id=1, source_target_pairs={{0,16},{8,24},{16,0},{24,8},{1,17},{9,25},{17,1},{25,9},{2,18},{10... | collective-permute-start | bytes 221192 | tf_op jit(solution)/shard_map/ppermute | solution.py:296
  53.4 20.5 %copy-start = (f32[128]{0:T(128)S(1)}, f32[128]{0:T(128)}, u32[]{:S(2)}) copy-start(f32[128]{0:T(128)} %param.7) | copy-start | bytes 1540

commit v6 on v4

--- a/solution.py
+++ b/solution.py
@@ -80,12 +80,13 @@
     ]
     for move in moves:
         move.start()
-    for move in moves:
+    for move in moves[1:]:
         move.wait()
     logged = jnp.concatenate(features(logged_ref[...]), axis=0)
     acts = policy_ref[...]
     codes = jnp.concatenate([acts >> 9, (acts & 511) - 256], axis=0).astype(f32)
     small = jnp.concatenate([logged, codes], axis=0).astype(bf16)
+    moves[0].wait()
     ctx = ctx_ref[...]
     for i in range(PLANES):
         plane_ref[i, :TILE, :] = ctx
@@ -122,7 +123,8 @@
 
 SCALE = math.log2(math.e) / D
 CHUNK = 8
-BESIDE = 3
+NEAR = 4
+BESIDE = 4
 SPAN = 2 * CHUNK * TILE
 
 
@@ -173,17 +175,17 @@
 
 
 def first_half(place_ref, own_ref, other_ref, policy_ref, extra_ref, *refs):
-    right_refs = (own_ref.at[place_ref[2]], *refs[:BESIDE])
-    kernel_ref, sums_ref, acc, cols = refs[BESIDE:]
+    right_refs = (own_ref.at[place_ref[2]], *refs[: NEAR - 1])
+    kernel_ref, sums_ref, acc, cols = refs[NEAR - 1 :]
     for b, total in enumerate(block((own_ref, other_ref, policy_ref, extra_ref), right_refs, kernel_ref, acc, cols)):
         sums_ref[b] = total
 
 
 def second_half(place_ref, own_ref, other_ref, policy_ref, extra_ref, done_ref, *refs):
-    right_refs = refs[: COLUMNS - 1 - BESIDE]
-    kernel_ref, sums_ref, acc, cols = refs[COLUMNS - 1 - BESIDE :]
+    right_refs = refs[: COLUMNS - NEAR]
+    kernel_ref, sums_ref, acc, cols = refs[COLUMNS - NEAR :]
     totals = block((own_ref, other_ref, policy_ref, extra_ref), right_refs, kernel_ref, acc, cols)
-    totals = [done_ref[b] for b in range(BESIDE + 1)] + totals
+    totals = [done_ref[b] for b in range(NEAR)] + totals
     for b, total in enumerate(totals):
         at = home(place_ref, b)
         for peer in range(COLUMNS):
@@ -207,7 +209,7 @@
         made = jnp.concatenate([chosen[c : c + 1] * low for c in range(NACT)], axis=0)
         matched[b * TILE : (b + 1) * TILE, :] = jnp.transpose(made).astype(bf16)
     core = place_ref[0]
-    cut = (BESIDE + 1) * TILE
+    cut = NEAR * TILE
     for step in range(PLANES // CHUNK):
         whole = slice(step * SPAN, (step + 1) * SPAN)
         out = jnp.dot(near_ref[whole, :], matched[:cut, :], preferred_element_type=f32)
@@ -304,24 +306,24 @@
             flops=2 * rows * width * (2 * D + TILE), bytes_accessed=2 * rows * (width + 4 * D), transcendentals=rows * width
         )
 
-    near, far = (BESIDE + 1) * TILE, (COLUMNS - 1 - BESIDE) * TILE
+    near, far = NEAR * TILE, (COLUMNS - NEAR) * TILE
     scratch = lambda width: [pltpu.VMEM((TILE, width), f32), pltpu.VMEM((width, 2 * D), bf16)]
     near_block, done = pl.pallas_call(
         first_half,
-        in_specs=[smem] + [vmem] * (4 + BESIDE),
-        out_shape=(sds((rows, near), bf16), sds((BESIDE + 1, NPOL, TILE), f32)),
+        in_specs=[smem] + [vmem] * (3 + NEAR),
+        out_shape=(sds((rows, near), bf16), sds((NEAR, NPOL, TILE), f32)),
         scratch_shapes=scratch(near),
         cost_estimate=cost(near),
         compiler_params=params(),
-    )(*left, *right[:BESIDE])
+    )(*left, *right[: NEAR - 1])
     far_block, first = pl.pallas_call(
         second_half,
-        in_specs=[smem] + [vmem] * (4 + COLUMNS - BESIDE),
+        in_specs=[smem] + [vmem] * (5 + COLUMNS - NEAR),
         out_shape=(sds((rows, far), bf16), sds((COLUMNS, COLUMNS, NPOL, TILE), f32)),
         scratch_shapes=scratch(far),
         cost_estimate=cost(far),
         compiler_params=params(),
-    )(*left, done, *right[BESIDE:])
+    )(*left, done, *right[NEAR - 1 :])
     parts = exchange(first, COLUMN)
     image_parts, side = pl.pallas_call(
         second_kernel,

time: 92.4 us -> 91.9 us (level)
  starting transfers between devices: 29.2 us -> 23.5 us
  blocking collectives: 45.5 us -> 49.2 us
  waiting for transfers between devices: 3.96 us -> 5.5 us
    ppermute x7, starting transfers between devices: 19.4 us -> 13.1 us  [on_device(): lax.ppermute(mine, COLUMN, ring(shift))]
    all_to_all x3, blocking collectives: 45.5 us -> 49.2 us  [exchange(): return lax.all_to_all(value, axes, 0, 0)]
    ppermute x7, waiting for transfers between devices: 3.95 us -> 5.49 us  [on_device(): lax.ppermute(mine, COLUMN, ring(shift))]
  transfers between devices with their start and end apart: 9 -> 9, of which waited for: 2 -> 3; matrix products, arithmetic and copies ran while one was open for 0% -> 0% of each run, Pallas kernels for 5% -> 5%
where the time goes in v6:
time: 91.9 us; the launch traced here: 91.6 us
  blocking collectives  49.2 us (54%)
  starting transfers between devices  23.5 us (26%)
  Pallas kernels  12.7 us (14%)
  waiting for transfers between devices  5.5 us (6%)
    all_to_all x3, blocking collectives, exchange(): return lax.all_to_all(value, axes, 0, 0)  49.2 us
    ppermute x7, starting transfers between devices, on_device(): lax.ppermute(mine, COLUMN, ring(shift))  13.1 us
    all_to_all x1, starting transfers between devices, exchange(): return lax.all_to_all(value, axes, 0, 0)  7.6 us
    ppermute x7, waiting for transfers between devices, on_device(): lax.ppermute(mine, COLUMN, ring(shift))  5.49 us
    pallas_call x1, Pallas kernels, on_device(): pl.pallas_call(second_kernel, in_specs=[smem] + [vmem] * (4 + COLUMNS), o...  3.21 us
    ppermute x1, starting transfers between devices, on_device(): other = lax.ppermute(own, 'core', [(0, 1), (1, 0)])  2.75 us
    pallas_call x1, Pallas kernels, on_device(): pl.pallas_call(second_half, in_specs=[smem] + [vmem] * (5 + COLUMNS - NEA...  2.6 us
    pallas_call x1, Pallas kernels, on_device(): pl.pallas_call(first_half, in_specs=[smem] + [vmem] * (3 + NEAR), out_sha...  2.59 us
  transfers between devices with their start and end apart: 9, of which 3 were waited for; matrix products, arithmetic and copies ran while one was open for 0% of the time, Pallas kernels for 5%

profile of v6, /device:TPU:1, one launch (start us, length us, event | category | flops | bytes accessed | tf_op | source)
XLA Modules:
  0.0 91.6 jit_solution(13627869545757771621)
XLA Ops:
  0.6 1.8 %shard_map.67 = (bf16[16,160,128]{2,1,0:T(8,128)(2,1)}, bf16[144,128]{1,0:T(8,128)(2,1)}) custom-call(bf16[128,128]{1,0:T(8,128)(2,1)} %ctx_hbm.1, s32[1,128]{1,0:T(1,128)} %bitcast.17, s32[8,128]{1,0:T(8,128)} %bitcast.16), custom_call_target="tpu_custom_call" | custom-call | tf_op jit(solution)/shard_map/pallas_call | solution.py:278
  2.4 7.6 %all-to-all-start = ((bf16[16,160,128]{2,1,0:T(8,128)(2,1)}), bf16[16,160,128]{2,1,0:T(8,128)(2,1)S(1)}, u32[]{:S(2)}, u32[]{:S(2)}) async-start(bf16[16,160,128]{2,1,0:T(8,128)(2,1)} %get-tuple-element.23), calls=%async_computation | async-start | bytes 1310720 | tf_op jit(solution)/shard_map/all_to_all | solution.py:267
  10.0 7.0 %collective-permute-start.3 = (bf16[144,128]{1,0:T(8,128)(2,1)}, bf16[144,128]{1,0:T(8,128)(2,1)S(1)}, u32[]{:S(2)}, u32[]{:S(2)}) collective-permute-start(bf16[144,128]{1,0:T(8,128)(2,1)} %get-tuple-element.24), channel_id=1, source_target_pairs={{0,128},{8,136},{16,144},{24,152},{128,0},{136,8},{144,16},{152,24... | collective-permute-start | bytes 110600 | tf_op jit(solution)/shard_map/ppermute | solution.py:291
  17.0 1.6 %collective-permute-start.2 = (bf16[144,128]{1,0:T(8,128)(2,1)}, bf16[144,128]{1,0:T(8,128)(2,1)S(1)}, u32[]{:S(2)}, u32[]{:S(2)}) collective-permute-start(bf16[144,128]{1,0:T(8,128)(2,1)} %get-tuple-element.24), channel_id=1, source_target_pairs={{0,24},{8,128},{16,136},{24,144},{128,152},{136,0},{144,8},{152,16... | collective-permute-start | bytes 110600 | tf_op jit(solution)/shard_map/ppermute | solution.py:291
  18.6 0.0 collective-permute-start.1
  18.6 0.3 collective-permute-start
  18.9 0.0 collective-permute-done.3.refs_0_.refs_3_
  18.9 4.6 %collective-permute-done.2.refs_2_ = bf16[144,128]{1,0:T(8,128)(2,1)S(1)} collective-permute-done((bf16[144,128]{1,0:T(8,128)(2,1)}, bf16[144,128]{1,0:T(8,128)(2,1)S(1)}, u32[]{:S(2)}, u32[]{:S(2)}) %collective-permute-start.2) | collective-permute-done | bytes 36896 | tf_op jit(solution)/shard_map/ppermute | solution.py:291
  23.6 0.6 collective-permute-done.1.refs_1_
  24.2 0.2 collective-permute-done.refs_0_
  24.4 0.0 all-to-all-done.own_ref
  24.4 2.8 %collective-permute-start.4 = (bf16[16,160,128]{2,1,0:T(8,128)(2,1)S(1)}, bf16[16,160,128]{2,1,0:T(8,128)(2,1)S(1)}, u32[]{:S(2)}, u32[]{:S(2)}) collective-permute-start(bf16[16,160,128]{2,1,0:T(8,128)(2,1)S(1)} %all-to-all-done.own_ref), channel_id=1, source_target_pairs={{0,1},{1,0},{2,3},{3,2},{4,5},{5,4},{6,7},{7,6},{8,9},{9,8},{10,11... | collective-permute-start | bytes 1966088 | tf_op jit(solution)/shard_map/ppermute | solution.py:293
  27.2 2.3 %collective-permute-start.7 = (bf16[144,128]{1,0:T(8,128)(2,1)}, bf16[144,128]{1,0:T(8,128)(2,1)S(1)}, u32[]{:S(2)}, u32[]{:S(2)}) collective-permute-start(bf16[144,128]{1,0:T(8,128)(2,1)} %get-tuple-element.24), channel_id=1, source_target_pairs={{0,152},{8,0},{16,8},{24,16},{128,24},{136,128},{144,136},{152,144... | collective-permute-start | bytes 110600 | tf_op jit(solution)/shard_map/ppermute | solution.py:291
  29.4 1.2 %collective-permute-start.6 = (bf16[144,128]{1,0:T(8,128)(2,1)}, bf16[144,128]{1,0:T(8,128)(2,1)S(1)}, u32[]{:S(2)}, u32[]{:S(2)}) collective-permute-start(bf16[144,128]{1,0:T(8,128)(2,1)} %get-tuple-element.24), channel_id=1, source_target_pairs={{0,144},{8,152},{16,0},{24,8},{128,16},{136,24},{144,128},{152,136... | collective-permute-start | bytes 110600 | tf_op jit(solution)/shard_map/ppermute | solution.py:291
  30.6 0.8 collective-permute-start.5
  31.4 0.1 pad_add_fusion.place_ref
  31.4 0.0 collective-permute-done.4.other_ref
  31.4 1.6 %shard_map.68 = (bf16[128,4096]{1,0:T(8,128)(2,1)S(1)}, bf16[32,128,128]{2,1,0:T(8,128)(2,1)S(1)}) custom-call(bf16[16,160,128]{2,1,0:T(8,128)(2,1)S(1)} %all-to-all-done.own_ref, bf16[16,160,128]{2,1,0:T(8,128)(2,1)S(1)} %collective-permute-done.4.other_ref), custom_call_target="tpu_custom_call" | custom-call | flops 60000000 | bytes 3000000 | tf_op jit(solution)/shard_map/pallas_call | solution.py:295
  33.1 2.6 %shard_map.69 = (bf16[4096,512]{1,0:T(8,128)(2,1)S(1)}, f32[4,8,128]{2,1,0:T(8,128)S(1)}) custom-call(s32[3]{0:T(128)S(1)} %pad_add_fusion.place_ref, bf16[16,160,128]{2,1,0:T(8,128)(2,1)S(1)} %all-to-all-done.own_ref, bf16[16,160,128]{2,1,0:T(8,128)(2,1)S(1)} %collective-permute-done.4.other_ref, bf16[128,4096]{1,0:T(8,128)(2,1)S(1)} %get-tuple-element.26.policy_ref, ...), custom_call_target="tpu_custom_call" | custom-call | flops 1610612736 | bytes 8388608 | tf_op jit(solution)/shard_map/pallas_call | solution.py:311
  35.7 0.0 collective-permute-done.7.refs_3_.refs_6_
  35.7 0.0 collective-permute-done.6.refs_2_.refs_5_
  35.7 0.0 collective-permute-done.5.refs_1_.refs_4_
  35.7 2.6 %shard_map.70 = (bf16[4096,512]{1,0:T(8,128)(2,1)S(1)}, f32[8,8,8,128]{3,2,1,0:T(8,128)S(1)}) custom-call(s32[3]{0:T(128)S(1)} %pad_add_fusion.place_ref, bf16[16,160,128]{2,1,0:T(8,128)(2,1)S(1)} %all-to-all-done.own_ref, bf16[16,160,128]{2,1,0:T(8,128)(2,1)S(1)} %collective-permute-done.4.other_ref, bf16[128,4096]{1,0:T(8,128)(2,1)S(1)} %get-tuple-element.26.policy_ref, ...), custom_call_target="tpu_custom_call" | custom-call | flops 1610612736 | bytes 8388608 | tf_op jit(solution)/shard_map/pallas_call | solution.py:319
  38.3 15.4 %all_to_all.20.parts_ref = f32[8,8,8,128]{3,2,1,0:T(8,128)S(1)} all-to-all(f32[8,8,8,128]{3,2,1,0:T(8,128)S(1)} %get-tuple-element.35), channel_id=1, replica_groups=mesh['z_hi'=2,'x'=4,'z_lo'=4,'y'=4,'core'=2] {'z_hi','z_lo'}, dimensions={0} | all-to-all | bytes 524288 | tf_op jit(solution)/shard_map/all_to_all | solution.py:267
  53.8 0.0 copy-start
  53.8 3.2 %shard_map.71 = (f32[32,8,128]{2,1,0:T(8,128)S(1)}, f32[8,128]{1,0:T(8,128)S(1)}) custom-call(s32[3]{0:T(128)S(1)} %pad_add_fusion.place_ref, bf16[4096,512]{1,0:T(8,128)(2,1)S(1)} %get-tuple-element.31.near_ref, bf16[4096,512]{1,0:T(8,128)(2,1)S(1)} %get-tuple-element.34.far_ref, f32[8,8,8,128]{3,2,1,0:T(8,128)S(1)} %all_to_all.20.parts_ref, ...), custom_call_target="tpu_custom_call" | custom-call | tf_op jit(solution)/shard_map/pallas_call | solution.py:328
  57.0 15.8 %all_to_all.21.parts_ref = f32[32,8,128]{2,1,0:T(8,128)S(1)} all-to-all(f32[32,8,128]{2,1,0:T(8,128)S(1)} %get-tuple-element.36), channel_id=1, replica_groups=mesh['z_hi'=2,'x'=4,'z_lo'=4,'y'=4,'core'=2] {'x','y','core'}, dimensions={0} | all-to-all | bytes 262144 | tf_op jit(solution)/shard_map/all_to_all | solution.py:267
  72.8 0.0 copy-done
  72.8 0.1 shard_map.72
  72.9 17.9 %all_to_all.22 = f32[256,1,128]{2,1,0:T(1,128)S(1)} all-to-all(f32[256,1,128]{2,1,0:T(1,128)S(1)} %bitcast.14), channel_id=1, replica_groups=mesh['z_hi'=2,'x'=4,'z_lo'=4,'y'=4,'core'=2] {'z_hi','x','z_lo','y','core'}, dimensions={0} | all-to-all | bytes 262144 | tf_op jit(solution)/shard_map/all_to_all | solution.py:267
  90.9 0.7 shard_map.73
Async XLA Ops:
  2.4 22.0 %all-to-all-start = ((bf16[16,160,128]{2,1,0:T(8,128)(2,1)}), bf16[16,160,128]{2,1,0:T(8,128)(2,1)S(1)}, u32[]{:S(2)}, u32[]{:S(2)}) async-start(bf16[16,160,128]{2,1,0:T(8,128)(2,1)} %get-tuple-element.23), calls=%async_computation | async-start | bytes 1310720 | tf_op jit(solution)/shard_map/all_to_all | solution.py:267
  10.0 8.9 %collective-permute-start.3 = (bf16[144,128]{1,0:T(8,128)(2,1)}, bf16[144,128]{1,0:T(8,128)(2,1)S(1)}, u32[]{:S(2)}, u32[]{:S(2)}) collective-permute-start(bf16[144,128]{1,0:T(8,128)(2,1)} %get-tuple-element.24), channel_id=1, source_target_pairs={{0,128},{8,136},{16,144},{24,152},{128,0},{136,8},{144,16},{152,24... | collective-permute-start | bytes 110600 | tf_op jit(solution)/shard_map/ppermute | solution.py:291
  17.0 6.6 %collective-permute-start.2 = (bf16[144,128]{1,0:T(8,128)(2,1)}, bf16[144,128]{1,0:T(8,128)(2,1)S(1)}, u32[]{:S(2)}, u32[]{:S(2)}) collective-permute-start(bf16[144,128]{1,0:T(8,128)(2,1)} %get-tuple-element.24), channel_id=1, source_target_pairs={{0,24},{8,128},{16,136},{24,144},{128,152},{136,0},{144,8},{152,16... | collective-permute-start | bytes 110600 | tf_op jit(solution)/shard_map/ppermute | solution.py:291
  18.6 5.5 %collective-permute-start.1 = (bf16[144,128]{1,0:T(8,128)(2,1)}, bf16[144,128]{1,0:T(8,128)(2,1)S(1)}, u32[]{:S(2)}, u32[]{:S(2)}) collective-permute-start(bf16[144,128]{1,0:T(8,128)(2,1)} %get-tuple-element.24), channel_id=1, source_target_pairs={{0,16},{8,24},{16,128},{24,136},{128,144},{136,152},{144,0},{152,8... | collective-permute-start | bytes 110600 | tf_op jit(solution)/shard_map/ppermute | solution.py:291
  18.6 5.8 %collective-permute-start = (bf16[144,128]{1,0:T(8,128)(2,1)}, bf16[144,128]{1,0:T(8,128)(2,1)S(1)}, u32[]{:S(2)}, u32[]{:S(2)}) collective-permute-start(bf16[144,128]{1,0:T(8,128)(2,1)} %get-tuple-element.24), channel_id=1, source_target_pairs={{0,8},{8,16},{16,24},{24,128},{128,136},{136,144},{144,152},{152,0... | collective-permute-start | bytes 110600 | tf_op jit(solution)/shard_map/ppermute | solution.py:291
  24.4 7.0 %collective-permute-start.4 = (bf16[16,160,128]{2,1,0:T(8,128)(2,1)S(1)}, bf16[16,160,128]{2,1,0:T(8,128)(2,1)S(1)}, u32[]{:S(2)}, u32[]{:S(2)}) collective-permute-start(bf16[16,160,128]{2,1,0:T(8,128)(2,1)S(1)} %all-to-all-done.own_ref), channel_id=1, source_target_pairs={{0,1},{1,0},{2,3},{3,2},{4,5},{5,4},{6,7},{7,6},{8,9},{9,8},{10,11... | collective-permute-start | bytes 1966088 | tf_op jit(solution)/shard_map/ppermute | solution.py:293
  27.2 8.5 %collective-permute-start.7 = (bf16[144,128]{1,0:T(8,128)(2,1)}, bf16[144,128]{1,0:T(8,128)(2,1)S(1)}, u32[]{:S(2)}, u32[]{:S(2)}) collective-permute-start(bf16[144,128]{1,0:T(8,128)(2,1)} %get-tuple-element.24), channel_id=1, source_target_pairs={{0,152},{8,0},{16,8},{24,16},{128,24},{136,128},{144,136},{152,144... | collective-permute-start | bytes 110600 | tf_op jit(solution)/shard_map/ppermute | solution.py:291
  29.4 6.3 %collective-permute-start.6 = (bf16[144,128]{1,0:T(8,128)(2,1)}, bf16[144,128]{1,0:T(8,128)(2,1)S(1)}, u32[]{:S(2)}, u32[]{:S(2)}) collective-permute-start(bf16[144,128]{1,0:T(8,128)(2,1)} %get-tuple-element.24), channel_id=1, source_target_pairs={{0,144},{8,152},{16,0},{24,8},{128,16},{136,24},{144,128},{152,136... | collective-permute-start | bytes 110600 | tf_op jit(solution)/shard_map/ppermute | solution.py:291
  30.6 5.1 %collective-permute-start.5 = (bf16[144,128]{1,0:T(8,128)(2,1)}, bf16[144,128]{1,0:T(8,128)(2,1)S(1)}, u32[]{:S(2)}, u32[]{:S(2)}) collective-permute-start(bf16[144,128]{1,0:T(8,128)(2,1)} %get-tuple-element.24), channel_id=1, source_target_pairs={{0,136},{8,144},{16,152},{24,0},{128,8},{136,16},{144,24},{152,128... | collective-permute-start | bytes 110600 | tf_op jit(solution)/shard_map/ppermute | solution.py:291
  53.8 19.0 %copy-start = (f32[128]{0:T(128)S(1)}, f32[128]{0:T(128)}, u32[]{:S(2)}) copy-start(f32[128]{0:T(128)} %param.7) | copy-start | bytes 1540

commit v7 on v6

--- a/solution.py
+++ b/solution.py
@@ -188,8 +188,11 @@
     totals = [done_ref[b] for b in range(NEAR)] + totals
     for b, total in enumerate(totals):
         at = home(place_ref, b)
+        high, middle, low = (piece.astype(bf16) for piece in pieces(total))
         for peer in range(COLUMNS):
-            sums_ref[peer, at] = total
+            sums_ref[peer, at] = high
+        sums_ref[at, COLUMNS] = middle
+        sums_ref[at, COLUMNS + 1] = low
 
 
 def second_kernel(place_ref, near_ref, far_ref, parts_ref, own_ref, other_ref, *refs):
@@ -198,9 +201,13 @@
     factor = NACT / (TILE * LEFT * COLUMNS)
     for b, right_ref in enumerate(right_refs):
         at = home(place_ref, b)
-        total = parts_ref[0, at]
-        for peer in range(1, COLUMNS):
-            total += parts_ref[peer, at]
+        total = jnp.zeros((NPOL, TILE), f32)
+        for peer in range(COLUMNS):
+            part = parts_ref[peer, at].astype(f32)
+            if b == 0:
+                part += parts_ref[peer, COLUMNS].astype(f32)
+                part += parts_ref[peer, COLUMNS + 1].astype(f32)
+            total += part
         total = total * factor
         if b == 0:
             side_ref[...] = total
@@ -319,7 +326,7 @@
     far_block, first = pl.pallas_call(
         second_half,
         in_specs=[smem] + [vmem] * (5 + COLUMNS - NEAR),
-        out_shape=(sds((rows, far), bf16), sds((COLUMNS, COLUMNS, NPOL, TILE), f32)),
+        out_shape=(sds((rows, far), bf16), sds((COLUMNS, COLUMNS + 2, NPOL, TILE), bf16)),
         scratch_shapes=scratch(far),
         cost_estimate=cost(far),
         compiler_params=params(),

time: 91.9 us -> 89.9 us (0.978)
  blocking collectives: 49.2 us -> 47.1 us
    all_to_all x3, blocking collectives: 49.2 us -> 47.1 us  [exchange(): return lax.all_to_all(value, axes, 0, 0)]
where the time goes in v7:
time: 89.9 us; the launch traced here: 89.5 us
  blocking collectives  47.1 us (52%)
  starting transfers between devices  23.5 us (26%)
  Pallas kernels  12.7 us (14%)
  waiting for transfers between devices  5.5 us (6%)
    all_to_all x3, blocking collectives, exchange(): return lax.all_to_all(value, axes, 0, 0)  47.1 us
    ppermute x7, starting transfers between devices, on_device(): lax.ppermute(mine, COLUMN, ring(shift))  13.1 us
    all_to_all x1, starting transfers between devices, exchange(): return lax.all_to_all(value, axes, 0, 0)  7.6 us
    ppermute x7, waiting for transfers between devices, on_device(): lax.ppermute(mine, COLUMN, ring(shift))  5.49 us
    pallas_call x1, Pallas kernels, on_device(): pl.pallas_call(second_kernel, in_specs=[smem] + [vmem] * (4 + COLUMNS), o...  3.22 us
    ppermute x1, starting transfers between devices, on_device(): other = lax.ppermute(own, 'core', [(0, 1), (1, 0)])  2.75 us
    pallas_call x1, Pallas kernels, on_device(): pl.pallas_call(second_half, in_specs=[smem] + [vmem] * (5 + COLUMNS - NEA...  2.61 us
    pallas_call x1, Pallas kernels, on_device(): pl.pallas_call(first_half, in_specs=[smem] + [vmem] * (3 + NEAR), out_sha...  2.59 us
  transfers between devices with their start and end apart: 9, of which 3 were waited for; matrix products, arithmetic and copies ran while one was open for 0% of the time, Pallas kernels for 5%

profile of v7, /device:TPU:1, one launch (start us, length us, event | category | flops | bytes accessed | tf_op | source)
XLA Modules:
  0.0 89.5 jit_solution(15672103478750479050)
XLA Ops:
  0.6 1.8 %shard_map.67 = (bf16[16,160,128]{2,1,0:T(8,128)(2,1)}, bf16[144,128]{1,0:T(8,128)(2,1)}) custom-call(bf16[128,128]{1,0:T(8,128)(2,1)} %ctx_hbm.1, s32[1,128]{1,0:T(1,128)} %bitcast.17, s32[8,128]{1,0:T(8,128)} %bitcast.16), custom_call_target="tpu_custom_call" | custom-call | tf_op jit(solution)/shard_map/pallas_call | solution.py:285
  2.4 7.6 %all-to-all-start = ((bf16[16,160,128]{2,1,0:T(8,128)(2,1)}), bf16[16,160,128]{2,1,0:T(8,128)(2,1)S(1)}, u32[]{:S(2)}, u32[]{:S(2)}) async-start(bf16[16,160,128]{2,1,0:T(8,128)(2,1)} %get-tuple-element.23), calls=%async_computation | async-start | bytes 1310720 | tf_op jit(solution)/shard_map/all_to_all | solution.py:274
  10.0 7.0 %collective-permute-start.3 = (bf16[144,128]{1,0:T(8,128)(2,1)}, bf16[144,128]{1,0:T(8,128)(2,1)S(1)}, u32[]{:S(2)}, u32[]{:S(2)}) collective-permute-start(bf16[144,128]{1,0:T(8,128)(2,1)} %get-tuple-element.24), channel_id=1, source_target_pairs={{0,128},{8,136},{16,144},{24,152},{128,0},{136,8},{144,16},{152,24... | collective-permute-start | bytes 110600 | tf_op jit(solution)/shard_map/ppermute | solution.py:298
  17.0 1.6 %collective-permute-start.2 = (bf16[144,128]{1,0:T(8,128)(2,1)}, bf16[144,128]{1,0:T(8,128)(2,1)S(1)}, u32[]{:S(2)}, u32[]{:S(2)}) collective-permute-start(bf16[144,128]{1,0:T(8,128)(2,1)} %get-tuple-element.24), channel_id=1, source_target_pairs={{0,24},{8,128},{16,136},{24,144},{128,152},{136,0},{144,8},{152,16... | collective-permute-start | bytes 110600 | tf_op jit(solution)/shard_map/ppermute | solution.py:298
  18.6 0.0 collective-permute-start.1
  18.6 0.3 collective-permute-start
  18.9 0.0 collective-permute-done.3.refs_0_.refs_3_
  18.9 4.6 %collective-permute-done.2.refs_2_ = bf16[144,128]{1,0:T(8,128)(2,1)S(1)} collective-permute-done((bf16[144,128]{1,0:T(8,128)(2,1)}, bf16[144,128]{1,0:T(8,128)(2,1)S(1)}, u32[]{:S(2)}, u32[]{:S(2)}) %collective-permute-start.2) | collective-permute-done | bytes 36896 | tf_op jit(solution)/shard_map/ppermute | solution.py:298
  23.6 0.6 collective-permute-done.1.refs_1_
  24.2 0.2 collective-permute-done.refs_0_
  24.4 0.0 all-to-all-done.own_ref
  24.4 2.8 %collective-permute-start.4 = (bf16[16,160,128]{2,1,0:T(8,128)(2,1)S(1)}, bf16[16,160,128]{2,1,0:T(8,128)(2,1)S(1)}, u32[]{:S(2)}, u32[]{:S(2)}) collective-permute-start(bf16[16,160,128]{2,1,0:T(8,128)(2,1)S(1)} %all-to-all-done.own_ref), channel_id=1, source_target_pairs={{0,1},{1,0},{2,3},{3,2},{4,5},{5,4},{6,7},{7,6},{8,9},{9,8},{10,11... | collective-permute-start | bytes 1966088 | tf_op jit(solution)/shard_map/ppermute | solution.py:300
  27.2 2.3 %collective-permute-start.7 = (bf16[144,128]{1,0:T(8,128)(2,1)}, bf16[144,128]{1,0:T(8,128)(2,1)S(1)}, u32[]{:S(2)}, u32[]{:S(2)}) collective-permute-start(bf16[144,128]{1,0:T(8,128)(2,1)} %get-tuple-element.24), channel_id=1, source_target_pairs={{0,152},{8,0},{16,8},{24,16},{128,24},{136,128},{144,136},{152,144... | collective-permute-start | bytes 110600 | tf_op jit(solution)/shard_map/ppermute | solution.py:298
  29.4 1.2 %collective-permute-start.6 = (bf16[144,128]{1,0:T(8,128)(2,1)}, bf16[144,128]{1,0:T(8,128)(2,1)S(1)}, u32[]{:S(2)}, u32[]{:S(2)}) collective-permute-start(bf16[144,128]{1,0:T(8,128)(2,1)} %get-tuple-element.24), channel_id=1, source_target_pairs={{0,144},{8,152},{16,0},{24,8},{128,16},{136,24},{144,128},{152,136... | collective-permute-start | bytes 110600 | tf_op jit(solution)/shard_map/ppermute | solution.py:298
  30.6 0.8 collective-permute-start.5
  31.4 0.1 pad_add_fusion.place_ref
  31.4 0.0 collective-permute-done.4.other_ref
  31.4 1.6 %shard_map.68 = (bf16[128,4096]{1,0:T(8,128)(2,1)S(1)}, bf16[32,128,128]{2,1,0:T(8,128)(2,1)S(1)}) custom-call(bf16[16,160,128]{2,1,0:T(8,128)(2,1)S(1)} %all-to-all-done.own_ref, bf16[16,160,128]{2,1,0:T(8,128)(2,1)S(1)} %collective-permute-done.4.other_ref), custom_call_target="tpu_custom_call" | custom-call | flops 60000000 | bytes 3000000 | tf_op jit(solution)/shard_map/pallas_call | solution.py:302
  33.1 2.6 %shard_map.69 = (bf16[4096,512]{1,0:T(8,128)(2,1)S(1)}, f32[4,8,128]{2,1,0:T(8,128)S(1)}) custom-call(s32[3]{0:T(128)S(1)} %pad_add_fusion.place_ref, bf16[16,160,128]{2,1,0:T(8,128)(2,1)S(1)} %all-to-all-done.own_ref, bf16[16,160,128]{2,1,0:T(8,128)(2,1)S(1)} %collective-permute-done.4.other_ref, bf16[128,4096]{1,0:T(8,128)(2,1)S(1)} %get-tuple-element.26.policy_ref, ...), custom_call_target="tpu_custom_call" | custom-call | flops 1610612736 | bytes 8388608 | tf_op jit(solution)/shard_map/pallas_call | solution.py:318
  35.7 0.0 collective-permute-done.7.refs_3_.refs_6_
  35.7 0.0 collective-permute-done.6.refs_2_.refs_5_
  35.7 0.0 collective-permute-done.5.refs_1_.refs_4_
  35.7 2.6 %shard_map.70 = (bf16[4096,512]{1,0:T(8,128)(2,1)S(1)}, bf16[8,10,8,128]{3,2,1,0:T(8,128)(2,1)S(1)}) custom-call(s32[3]{0:T(128)S(1)} %pad_add_fusion.place_ref, bf16[16,160,128]{2,1,0:T(8,128)(2,1)S(1)} %all-to-all-done.own_ref, bf16[16,160,128]{2,1,0:T(8,128)(2,1)S(1)} %collective-permute-done.4.other_ref, ...), custom_call_target="tpu_custom_call" | custom-call | flops 1610612736 | bytes 8388608 | tf_op jit(solution)/shard_map/pallas_call | solution.py:326
  38.3 13.3 %all_to_all.20.parts_ref = bf16[8,10,8,128]{3,2,1,0:T(8,128)(2,1)S(1)} all-to-all(bf16[8,10,8,128]{3,2,1,0:T(8,128)(2,1)S(1)} %get-tuple-element.35), channel_id=1, replica_groups=mesh['z_hi'=2,'x'=4,'z_lo'=4,'y'=4,'core'=2] {'z_hi','z_lo'}, dimensions={0} | all-to-all | bytes 327680 | tf_op jit(solution)/shard_map/all_to_all | solution.py:274
  51.7 0.0 copy-start
  51.7 3.2 %shard_map.71 = (f32[32,8,128]{2,1,0:T(8,128)S(1)}, f32[8,128]{1,0:T(8,128)S(1)}) custom-call(s32[3]{0:T(128)S(1)} %pad_add_fusion.place_ref, bf16[4096,512]{1,0:T(8,128)(2,1)S(1)} %get-tuple-element.31.near_ref, bf16[4096,512]{1,0:T(8,128)(2,1)S(1)} %get-tuple-element.34.far_ref, bf16[8,10,8,128]{3,2,1,0:T(8,128)(2,1)S(1)} %all_to_all.20.parts_ref, ...), custom_call_target="tpu_custom_call" | custom-call | tf_op jit(solution)/shard_map/pallas_call | solution.py:335
  54.9 15.8 %all_to_all.21.parts_ref = f32[32,8,128]{2,1,0:T(8,128)S(1)} all-to-all(f32[32,8,128]{2,1,0:T(8,128)S(1)} %get-tuple-element.36), channel_id=1, replica_groups=mesh['z_hi'=2,'x'=4,'z_lo'=4,'y'=4,'core'=2] {'x','y','core'}, dimensions={0} | all-to-all | bytes 262144 | tf_op jit(solution)/shard_map/all_to_all | solution.py:274
  70.7 0.0 copy-done
  70.7 0.1 shard_map.72
  70.9 17.9 %all_to_all.22 = f32[256,1,128]{2,1,0:T(1,128)S(1)} all-to-all(f32[256,1,128]{2,1,0:T(1,128)S(1)} %bitcast.14), channel_id=1, replica_groups=mesh['z_hi'=2,'x'=4,'z_lo'=4,'y'=4,'core'=2] {'z_hi','x','z_lo','y','core'}, dimensions={0} | all-to-all | bytes 262144 | tf_op jit(solution)/shard_map/all_to_all | solution.py:274
  88.8 0.7 shard_map.73
Async XLA Ops:
  2.4 22.0 %all-to-all-start = ((bf16[16,160,128]{2,1,0:T(8,128)(2,1)}), bf16[16,160,128]{2,1,0:T(8,128)(2,1)S(1)}, u32[]{:S(2)}, u32[]{:S(2)}) async-start(bf16[16,160,128]{2,1,0:T(8,128)(2,1)} %get-tuple-element.23), calls=%async_computation | async-start | bytes 1310720 | tf_op jit(solution)/shard_map/all_to_all | solution.py:274
  10.0 8.9 %collective-permute-start.3 = (bf16[144,128]{1,0:T(8,128)(2,1)}, bf16[144,128]{1,0:T(8,128)(2,1)S(1)}, u32[]{:S(2)}, u32[]{:S(2)}) collective-permute-start(bf16[144,128]{1,0:T(8,128)(2,1)} %get-tuple-element.24), channel_id=1, source_target_pairs={{0,128},{8,136},{16,144},{24,152},{128,0},{136,8},{144,16},{152,24... | collective-permute-start | bytes 110600 | tf_op jit(solution)/shard_map/ppermute | solution.py:298
  17.0 6.6 %collective-permute-start.2 = (bf16[144,128]{1,0:T(8,128)(2,1)}, bf16[144,128]{1,0:T(8,128)(2,1)S(1)}, u32[]{:S(2)}, u32[]{:S(2)}) collective-permute-start(bf16[144,128]{1,0:T(8,128)(2,1)} %get-tuple-element.24), channel_id=1, source_target_pairs={{0,24},{8,128},{16,136},{24,144},{128,152},{136,0},{144,8},{152,16... | collective-permute-start | bytes 110600 | tf_op jit(solution)/shard_map/ppermute | solution.py:298
  18.6 5.5 %collective-permute-start.1 = (bf16[144,128]{1,0:T(8,128)(2,1)}, bf16[144,128]{1,0:T(8,128)(2,1)S(1)}, u32[]{:S(2)}, u32[]{:S(2)}) collective-permute-start(bf16[144,128]{1,0:T(8,128)(2,1)} %get-tuple-element.24), channel_id=1, source_target_pairs={{0,16},{8,24},{16,128},{24,136},{128,144},{136,152},{144,0},{152,8... | collective-permute-start | bytes 110600 | tf_op jit(solution)/shard_map/ppermute | solution.py:298
  18.6 5.8 %collective-permute-start = (bf16[144,128]{1,0:T(8,128)(2,1)}, bf16[144,128]{1,0:T(8,128)(2,1)S(1)}, u32[]{:S(2)}, u32[]{:S(2)}) collective-permute-start(bf16[144,128]{1,0:T(8,128)(2,1)} %get-tuple-element.24), channel_id=1, source_target_pairs={{0,8},{8,16},{16,24},{24,128},{128,136},{136,144},{144,152},{152,0... | collective-permute-start | bytes 110600 | tf_op jit(solution)/shard_map/ppermute | solution.py:298
  24.4 7.0 %collective-permute-start.4 = (bf16[16,160,128]{2,1,0:T(8,128)(2,1)S(1)}, bf16[16,160,128]{2,1,0:T(8,128)(2,1)S(1)}, u32[]{:S(2)}, u32[]{:S(2)}) collective-permute-start(bf16[16,160,128]{2,1,0:T(8,128)(2,1)S(1)} %all-to-all-done.own_ref), channel_id=1, source_target_pairs={{0,1},{1,0},{2,3},{3,2},{4,5},{5,4},{6,7},{7,6},{8,9},{9,8},{10,11... | collective-permute-start | bytes 1966088 | tf_op jit(solution)/shard_map/ppermute | solution.py:300
  27.2 8.5 %collective-permute-start.7 = (bf16[144,128]{1,0:T(8,128)(2,1)}, bf16[144,128]{1,0:T(8,128)(2,1)S(1)}, u32[]{:S(2)}, u32[]{:S(2)}) collective-permute-start(bf16[144,128]{1,0:T(8,128)(2,1)} %get-tuple-element.24), channel_id=1, source_target_pairs={{0,152},{8,0},{16,8},{24,16},{128,24},{136,128},{144,136},{152,144... | collective-permute-start | bytes 110600 | tf_op jit(solution)/shard_map/ppermute | solution.py:298
  29.4 6.3 %collective-permute-start.6 = (bf16[144,128]{1,0:T(8,128)(2,1)}, bf16[144,128]{1,0:T(8,128)(2,1)S(1)}, u32[]{:S(2)}, u32[]{:S(2)}) collective-permute-start(bf16[144,128]{1,0:T(8,128)(2,1)} %get-tuple-element.24), channel_id=1, source_target_pairs={{0,144},{8,152},{16,0},{24,8},{128,16},{136,24},{144,128},{152,136... | collective-permute-start | bytes 110600 | tf_op jit(solution)/shard_map/ppermute | solution.py:298
  30.6 5.1 %collective-permute-start.5 = (bf16[144,128]{1,0:T(8,128)(2,1)}, bf16[144,128]{1,0:T(8,128)(2,1)S(1)}, u32[]{:S(2)}, u32[]{:S(2)}) collective-permute-start(bf16[144,128]{1,0:T(8,128)(2,1)} %get-tuple-element.24), channel_id=1, source_target_pairs={{0,136},{8,144},{16,152},{24,0},{128,8},{136,16},{144,24},{152,128... | collective-permute-start | bytes 110600 | tf_op jit(solution)/shard_map/ppermute | solution.py:298
  51.7 19.1 %copy-start = (f32[128]{0:T(128)S(1)}, f32[128]{0:T(128)}, u32[]{:S(2)}) copy-start(f32[128]{0:T(128)} %param.7) | copy-start | bytes 1540

commit v8 on v6

--- a/solution.py
+++ b/solution.py
@@ -122,7 +122,7 @@
 
 
 SCALE = math.log2(math.e) / D
-CHUNK = 8
+CHUNK = 4
 NEAR = 4
 BESIDE = 4
 SPAN = 2 * CHUNK * TILE
@@ -144,23 +144,21 @@
             extra = jnp.where(lane == at, -piece, extra)
         cols[here, :D] = (2.0 * x).astype(bf16)
         cols[here, D:] = extra.astype(bf16)
-    width = len(right_refs) * TILE
-    wide = 2 * TILE
     for step in range(PLANES // CHUNK):
-        rows = jnp.concatenate(
-            [
-                jnp.concatenate([ref[j, :TILE, :], extra_ref[2 * j + half]], axis=1)
-                for j in range(step * CHUNK, (step + 1) * CHUNK)
-                for half, ref in enumerate((own_ref, other_ref))
-            ],
-            axis=0,
+        for j in range(step * CHUNK, (step + 1) * CHUNK):
+            rows = jnp.concatenate(
+                [
+                    jnp.concatenate([ref[j, :TILE, :], extra_ref[2 * j + half]], axis=1)
+                    for half, ref in enumerate((own_ref, other_ref))
+                ],
+                axis=0,
+            )
+            expo = lax.dot_general(cols[...], rows, (((1,), (1,)), ((), ())), preferred_element_type=f32)
+            kernel_ref[:, 2 * j * TILE : 2 * (j + 1) * TILE] = jnp.exp2(SCALE * expo).astype(bf16)
+        whole = slice(step * SPAN, (step + 1) * SPAN)
+        term = lax.dot_general(
+            policy_ref[:, whole], kernel_ref[:, whole], (((1,), (1,)), ((), ())), preferred_element_type=f32
         )
-        whole = slice(step * SPAN, (step + 1) * SPAN)
-        for at in range(0, width, wide):
-            span = slice(at, at + wide)
-            expo = lax.dot_general(rows, cols[span, :], (((1,), (1,)), ((), ())), preferred_element_type=f32)
-            kernel_ref[whole, span] = jnp.exp2(SCALE * expo).astype(bf16)
-        term = jnp.dot(policy_ref[:, whole], kernel_ref[whole, :], preferred_element_type=f32)
         if step:
             term += acc[...]
         acc[...] = term
@@ -207,14 +205,13 @@
         low = total.astype(bf16).astype(f32)
         chosen = right_ref[FEAT_AT : FEAT_AT + NACT, :].astype(f32)
         made = jnp.concatenate([chosen[c : c + 1] * low for c in range(NACT)], axis=0)
-        matched[b * TILE : (b + 1) * TILE, :] = jnp.transpose(made).astype(bf16)
+        matched[:, b * TILE : (b + 1) * TILE] = made.astype(bf16)
     core = place_ref[0]
     cut = NEAR * TILE
     for step in range(PLANES // CHUNK):
         whole = slice(step * SPAN, (step + 1) * SPAN)
-        out = jnp.dot(near_ref[whole, :], matched[:cut, :], preferred_element_type=f32)
-        out += jnp.dot(far_ref[whole, :], matched[cut:, :], preferred_element_type=f32)
-        out = jnp.transpose(out)
+        out = jnp.dot(matched[:, :cut], near_ref[:, whole], preferred_element_type=f32)
+        out += jnp.dot(matched[:, cut:], far_ref[:, whole], preferred_element_type=f32)
         for j in range(step * CHUNK, (step + 1) * CHUNK):
             for half, ref in enumerate((own_ref, other_ref)):
                 chosen = ref[j, FEAT_AT : FEAT_AT + NACT, :].astype(f32)
@@ -311,7 +308,7 @@
     near_block, done = pl.pallas_call(
         first_half,
         in_specs=[smem] + [vmem] * (3 + NEAR),
-        out_shape=(sds((rows, near), bf16), sds((NEAR, NPOL, TILE), f32)),
+        out_shape=(sds((near, rows), bf16), sds((NEAR, NPOL, TILE), f32)),
         scratch_shapes=scratch(near),
         cost_estimate=cost(near),
         compiler_params=params(),
@@ -319,7 +316,7 @@
     far_block, first = pl.pallas_call(
         second_half,
         in_specs=[smem] + [vmem] * (5 + COLUMNS - NEAR),
-        out_shape=(sds((rows, far), bf16), sds((COLUMNS, COLUMNS, NPOL, TILE), f32)),
+        out_shape=(sds((far, rows), bf16), sds((COLUMNS, COLUMNS, NPOL, TILE), f32)),
         scratch_shapes=scratch(far),
         cost_estimate=cost(far),
         compiler_params=params(),
@@ -329,7 +326,7 @@
         second_kernel,
         in_specs=[smem] + [vmem] * (4 + COLUMNS),
         out_shape=(sds((LEFT, NPOL, TILE), f32), sds((NPOL, TILE), f32)),
-        scratch_shapes=[pltpu.VMEM((COLUMNS * TILE, TILE), bf16)],
+        scratch_shapes=[pltpu.VMEM((TILE, COLUMNS * TILE), bf16)],
         compiler_params=params(),
     )(place, near_block, far_block, parts, own, other, *right)
     image_parts = exchange(image_parts, PLANE + ("core",))

time: 91.9 us -> 91.7 us (level)
    pallas_call x1, Pallas kernels: 3.21 us -> 1.84 us  [on_device(): pl.pallas_call(second_kernel, in_specs=[smem] + [vmem] * (4 + COLUMNS), o...]
where the time goes in v8:
time: 91.7 us; the launch traced here: 91.3 us
  blocking collectives  49.2 us (54%)
  starting transfers between devices  23.5 us (26%)
  Pallas kernels  12.4 us (14%)
  waiting for transfers between devices  5.5 us (6%)
    all_to_all x3, blocking collectives, exchange(): return lax.all_to_all(value, axes, 0, 0)  49.2 us
    ppermute x7, starting transfers between devices, on_device(): lax.ppermute(mine, COLUMN, ring(shift))  13.1 us
    all_to_all x1, starting transfers between devices, exchange(): return lax.all_to_all(value, axes, 0, 0)  7.6 us
    ppermute x7, waiting for transfers between devices, on_device(): lax.ppermute(mine, COLUMN, ring(shift))  5.49 us
    pallas_call x1, Pallas kernels, on_device(): pl.pallas_call(second_half, in_specs=[smem] + [vmem] * (5 + COLUMNS - NEA...  3.17 us
    pallas_call x1, Pallas kernels, on_device(): pl.pallas_call(first_half, in_specs=[smem] + [vmem] * (3 + NEAR), out_sha...  3.16 us
    ppermute x1, starting transfers between devices, on_device(): other = lax.ppermute(own, 'core', [(0, 1), (1, 0)])  2.75 us
    pallas_call x1, Pallas kernels, on_device(): pl.pallas_call(second_kernel, in_specs=[smem] + [vmem] * (4 + COLUMNS), o...  1.84 us
  transfers between devices with their start and end apart: 9, of which 3 were waited for; matrix products, arithmetic and copies ran while one was open for 0% of the time, Pallas kernels for 5%

profile of v8, /device:TPU:1, one launch (start us, length us, event | category | flops | bytes accessed | tf_op | source)
XLA Modules:
  0.0 91.3 jit_solution(15099818093751571039)
XLA Ops:
  0.6 1.8 %shard_map.67 = (bf16[16,160,128]{2,1,0:T(8,128)(2,1)}, bf16[144,128]{1,0:T(8,128)(2,1)}) custom-call(bf16[128,128]{1,0:T(8,128)(2,1)} %ctx_hbm.1, s32[1,128]{1,0:T(1,128)} %bitcast.17, s32[8,128]{1,0:T(8,128)} %bitcast.16), custom_call_target="tpu_custom_call" | custom-call | tf_op jit(solution)/shard_map/pallas_call | solution.py:275
  2.4 7.6 %all-to-all-start = ((bf16[16,160,128]{2,1,0:T(8,128)(2,1)}), bf16[16,160,128]{2,1,0:T(8,128)(2,1)S(1)}, u32[]{:S(2)}, u32[]{:S(2)}) async-start(bf16[16,160,128]{2,1,0:T(8,128)(2,1)} %get-tuple-element.23), calls=%async_computation | async-start | bytes 1310720 | tf_op jit(solution)/shard_map/all_to_all | solution.py:264
  10.0 7.0 %collective-permute-start.3 = (bf16[144,128]{1,0:T(8,128)(2,1)}, bf16[144,128]{1,0:T(8,128)(2,1)S(1)}, u32[]{:S(2)}, u32[]{:S(2)}) collective-permute-start(bf16[144,128]{1,0:T(8,128)(2,1)} %get-tuple-element.24), channel_id=1, source_target_pairs={{0,128},{8,136},{16,144},{24,152},{128,0},{136,8},{144,16},{152,24... | collective-permute-start | bytes 110600 | tf_op jit(solution)/shard_map/ppermute | solution.py:288
  17.0 1.6 %collective-permute-start.2 = (bf16[144,128]{1,0:T(8,128)(2,1)}, bf16[144,128]{1,0:T(8,128)(2,1)S(1)}, u32[]{:S(2)}, u32[]{:S(2)}) collective-permute-start(bf16[144,128]{1,0:T(8,128)(2,1)} %get-tuple-element.24), channel_id=1, source_target_pairs={{0,24},{8,128},{16,136},{24,144},{128,152},{136,0},{144,8},{152,16... | collective-permute-start | bytes 110600 | tf_op jit(solution)/shard_map/ppermute | solution.py:288
  18.6 0.0 collective-permute-start.1
  18.6 0.3 collective-permute-start
  18.9 0.0 collective-permute-done.3.refs_0_.refs_3_
  18.9 4.6 %collective-permute-done.2.refs_2_ = bf16[144,128]{1,0:T(8,128)(2,1)S(1)} collective-permute-done((bf16[144,128]{1,0:T(8,128)(2,1)}, bf16[144,128]{1,0:T(8,128)(2,1)S(1)}, u32[]{:S(2)}, u32[]{:S(2)}) %collective-permute-start.2) | collective-permute-done | bytes 36896 | tf_op jit(solution)/shard_map/ppermute | solution.py:288
  23.6 0.6 collective-permute-done.1.refs_1_
  24.2 0.2 collective-permute-done.refs_0_
  24.4 0.0 all-to-all-done.own_ref
  24.4 2.8 %collective-permute-start.4 = (bf16[16,160,128]{2,1,0:T(8,128)(2,1)S(1)}, bf16[16,160,128]{2,1,0:T(8,128)(2,1)S(1)}, u32[]{:S(2)}, u32[]{:S(2)}) collective-permute-start(bf16[16,160,128]{2,1,0:T(8,128)(2,1)S(1)} %all-to-all-done.own_ref), channel_id=1, source_target_pairs={{0,1},{1,0},{2,3},{3,2},{4,5},{5,4},{6,7},{7,6},{8,9},{9,8},{10,11... | collective-permute-start | bytes 1966088 | tf_op jit(solution)/shard_map/ppermute | solution.py:290
  27.2 2.3 %collective-permute-start.7 = (bf16[144,128]{1,0:T(8,128)(2,1)}, bf16[144,128]{1,0:T(8,128)(2,1)S(1)}, u32[]{:S(2)}, u32[]{:S(2)}) collective-permute-start(bf16[144,128]{1,0:T(8,128)(2,1)} %get-tuple-element.24), channel_id=1, source_target_pairs={{0,152},{8,0},{16,8},{24,16},{128,24},{136,128},{144,136},{152,144... | collective-permute-start | bytes 110600 | tf_op jit(solution)/shard_map/ppermute | solution.py:288
  29.4 1.2 %collective-permute-start.6 = (bf16[144,128]{1,0:T(8,128)(2,1)}, bf16[144,128]{1,0:T(8,128)(2,1)S(1)}, u32[]{:S(2)}, u32[]{:S(2)}) collective-permute-start(bf16[144,128]{1,0:T(8,128)(2,1)} %get-tuple-element.24), channel_id=1, source_target_pairs={{0,144},{8,152},{16,0},{24,8},{128,16},{136,24},{144,128},{152,136... | collective-permute-start | bytes 110600 | tf_op jit(solution)/shard_map/ppermute | solution.py:288
  30.6 0.8 collective-permute-start.5
  31.4 0.1 pad_add_fusion.place_ref
  31.4 0.0 collective-permute-done.4.other_ref
  31.4 1.6 %shard_map.68 = (bf16[128,4096]{1,0:T(8,128)(2,1)S(1)}, bf16[32,128,128]{2,1,0:T(8,128)(2,1)S(1)}) custom-call(bf16[16,160,128]{2,1,0:T(8,128)(2,1)S(1)} %all-to-all-done.own_ref, bf16[16,160,128]{2,1,0:T(8,128)(2,1)S(1)} %collective-permute-done.4.other_ref), custom_call_target="tpu_custom_call" | custom-call | flops 60000000 | bytes 3000000 | tf_op jit(solution)/shard_map/pallas_call | solution.py:292
  33.1 3.2 %shard_map.69 = (bf16[512,4096]{1,0:T(8,128)(2,1)S(1)}, f32[4,8,128]{2,1,0:T(8,128)S(1)}) custom-call(s32[3]{0:T(128)S(1)} %pad_add_fusion.place_ref, bf16[16,160,128]{2,1,0:T(8,128)(2,1)S(1)} %all-to-all-done.own_ref, bf16[16,160,128]{2,1,0:T(8,128)(2,1)S(1)} %collective-permute-done.4.other_ref, bf16[128,4096]{1,0:T(8,128)(2,1)S(1)} %get-tuple-element.26.policy_ref, ...), custom_call_target="tpu_custom_call" | custom-call | flops 1610612736 | bytes 8388608 | tf_op jit(solution)/shard_map/pallas_call | solution.py:308
  36.3 0.0 collective-permute-done.7.refs_3_.refs_6_
  36.3 0.0 collective-permute-done.6.refs_2_.refs_5_
  36.3 0.0 collective-permute-done.5.refs_1_.refs_4_
  36.3 3.2 %shard_map.70 = (bf16[512,4096]{1,0:T(8,128)(2,1)S(1)}, f32[8,8,8,128]{3,2,1,0:T(8,128)S(1)}) custom-call(s32[3]{0:T(128)S(1)} %pad_add_fusion.place_ref, bf16[16,160,128]{2,1,0:T(8,128)(2,1)S(1)} %all-to-all-done.own_ref, bf16[16,160,128]{2,1,0:T(8,128)(2,1)S(1)} %collective-permute-done.4.other_ref, bf16[128,4096]{1,0:T(8,128)(2,1)S(1)} %get-tuple-element.26.policy_ref, ...), custom_call_target="tpu_custom_call" | custom-call | flops 1610612736 | bytes 8388608 | tf_op jit(solution)/shard_map/pallas_call | solution.py:316
  39.5 15.4 %all_to_all.20.parts_ref = f32[8,8,8,128]{3,2,1,0:T(8,128)S(1)} all-to-all(f32[8,8,8,128]{3,2,1,0:T(8,128)S(1)} %get-tuple-element.35), channel_id=1, replica_groups=mesh['z_hi'=2,'x'=4,'z_lo'=4,'y'=4,'core'=2] {'z_hi','z_lo'}, dimensions={0} | all-to-all | bytes 524288 | tf_op jit(solution)/shard_map/all_to_all | solution.py:264
  54.9 0.0 copy-start
  54.9 1.8 %shard_map.71 = (f32[32,8,128]{2,1,0:T(8,128)S(1)}, f32[8,128]{1,0:T(8,128)S(1)}) custom-call(s32[3]{0:T(128)S(1)} %pad_add_fusion.place_ref, bf16[512,4096]{1,0:T(8,128)(2,1)S(1)} %get-tuple-element.31.near_ref, bf16[512,4096]{1,0:T(8,128)(2,1)S(1)} %get-tuple-element.34.far_ref, f32[8,8,8,128]{3,2,1,0:T(8,128)S(1)} %all_to_all.20.parts_ref, ...), custom_call_target="tpu_custom_call" | custom-call | tf_op jit(solution)/shard_map/pallas_call | solution.py:325
  56.8 15.8 %all_to_all.21.parts_ref = f32[32,8,128]{2,1,0:T(8,128)S(1)} all-to-all(f32[32,8,128]{2,1,0:T(8,128)S(1)} %get-tuple-element.36), channel_id=1, replica_groups=mesh['z_hi'=2,'x'=4,'z_lo'=4,'y'=4,'core'=2] {'x','y','core'}, dimensions={0} | all-to-all | bytes 262144 | tf_op jit(solution)/shard_map/all_to_all | solution.py:264
  72.6 0.0 copy-done
  72.6 0.1 shard_map.72
  72.7 17.9 %all_to_all.22 = f32[256,1,128]{2,1,0:T(1,128)S(1)} all-to-all(f32[256,1,128]{2,1,0:T(1,128)S(1)} %bitcast.14), channel_id=1, replica_groups=mesh['z_hi'=2,'x'=4,'z_lo'=4,'y'=4,'core'=2] {'z_hi','x','z_lo','y','core'}, dimensions={0} | all-to-all | bytes 262144 | tf_op jit(solution)/shard_map/all_to_all | solution.py:264
  90.6 0.7 shard_map.73
Async XLA Ops:
  2.4 22.0 %all-to-all-start = ((bf16[16,160,128]{2,1,0:T(8,128)(2,1)}), bf16[16,160,128]{2,1,0:T(8,128)(2,1)S(1)}, u32[]{:S(2)}, u32[]{:S(2)}) async-start(bf16[16,160,128]{2,1,0:T(8,128)(2,1)} %get-tuple-element.23), calls=%async_computation | async-start | bytes 1310720 | tf_op jit(solution)/shard_map/all_to_all | solution.py:264
  10.0 8.9 %collective-permute-start.3 = (bf16[144,128]{1,0:T(8,128)(2,1)}, bf16[144,128]{1,0:T(8,128)(2,1)S(1)}, u32[]{:S(2)}, u32[]{:S(2)}) collective-permute-start(bf16[144,128]{1,0:T(8,128)(2,1)} %get-tuple-element.24), channel_id=1, source_target_pairs={{0,128},{8,136},{16,144},{24,152},{128,0},{136,8},{144,16},{152,24... | collective-permute-start | bytes 110600 | tf_op jit(solution)/shard_map/ppermute | solution.py:288
  17.0 6.6 %collective-permute-start.2 = (bf16[144,128]{1,0:T(8,128)(2,1)}, bf16[144,128]{1,0:T(8,128)(2,1)S(1)}, u32[]{:S(2)}, u32[]{:S(2)}) collective-permute-start(bf16[144,128]{1,0:T(8,128)(2,1)} %get-tuple-element.24), channel_id=1, source_target_pairs={{0,24},{8,128},{16,136},{24,144},{128,152},{136,0},{144,8},{152,16... | collective-permute-start | bytes 110600 | tf_op jit(solution)/shard_map/ppermute | solution.py:288
  18.6 5.5 %collective-permute-start.1 = (bf16[144,128]{1,0:T(8,128)(2,1)}, bf16[144,128]{1,0:T(8,128)(2,1)S(1)}, u32[]{:S(2)}, u32[]{:S(2)}) collective-permute-start(bf16[144,128]{1,0:T(8,128)(2,1)} %get-tuple-element.24), channel_id=1, source_target_pairs={{0,16},{8,24},{16,128},{24,136},{128,144},{136,152},{144,0},{152,8... | collective-permute-start | bytes 110600 | tf_op jit(solution)/shard_map/ppermute | solution.py:288
  18.6 5.8 %collective-permute-start = (bf16[144,128]{1,0:T(8,128)(2,1)}, bf16[144,128]{1,0:T(8,128)(2,1)S(1)}, u32[]{:S(2)}, u32[]{:S(2)}) collective-permute-start(bf16[144,128]{1,0:T(8,128)(2,1)} %get-tuple-element.24), channel_id=1, source_target_pairs={{0,8},{8,16},{16,24},{24,128},{128,136},{136,144},{144,152},{152,0... | collective-permute-start | bytes 110600 | tf_op jit(solution)/shard_map/ppermute | solution.py:288
  24.4 7.0 %collective-permute-start.4 = (bf16[16,160,128]{2,1,0:T(8,128)(2,1)S(1)}, bf16[16,160,128]{2,1,0:T(8,128)(2,1)S(1)}, u32[]{:S(2)}, u32[]{:S(2)}) collective-permute-start(bf16[16,160,128]{2,1,0:T(8,128)(2,1)S(1)} %all-to-all-done.own_ref), channel_id=1, source_target_pairs={{0,1},{1,0},{2,3},{3,2},{4,5},{5,4},{6,7},{7,6},{8,9},{9,8},{10,11... | collective-permute-start | bytes 1966088 | tf_op jit(solution)/shard_map/ppermute | solution.py:290
  27.2 9.1 %collective-permute-start.7 = (bf16[144,128]{1,0:T(8,128)(2,1)}, bf16[144,128]{1,0:T(8,128)(2,1)S(1)}, u32[]{:S(2)}, u32[]{:S(2)}) collective-permute-start(bf16[144,128]{1,0:T(8,128)(2,1)} %get-tuple-element.24), channel_id=1, source_target_pairs={{0,152},{8,0},{16,8},{24,16},{128,24},{136,128},{144,136},{152,144... | collective-permute-start | bytes 110600 | tf_op jit(solution)/shard_map/ppermute | solution.py:288
  29.4 6.9 %collective-permute-start.6 = (bf16[144,128]{1,0:T(8,128)(2,1)}, bf16[144,128]{1,0:T(8,128)(2,1)S(1)}, u32[]{:S(2)}, u32[]{:S(2)}) collective-permute-start(bf16[144,128]{1,0:T(8,128)(2,1)} %get-tuple-element.24), channel_id=1, source_target_pairs={{0,144},{8,152},{16,0},{24,8},{128,16},{136,24},{144,128},{152,136... | collective-permute-start | bytes 110600 | tf_op jit(solution)/shard_map/ppermute | solution.py:288
  30.6 5.7 %collective-permute-start.5 = (bf16[144,128]{1,0:T(8,128)(2,1)}, bf16[144,128]{1,0:T(8,128)(2,1)S(1)}, u32[]{:S(2)}, u32[]{:S(2)}) collective-permute-start(bf16[144,128]{1,0:T(8,128)(2,1)} %get-tuple-element.24), channel_id=1, source_target_pairs={{0,136},{8,144},{16,152},{24,0},{128,8},{136,16},{144,24},{152,128... | collective-permute-start | bytes 110600 | tf_op jit(solution)/shard_map/ppermute | solution.py:288
  54.9 17.7 %copy-start = (f32[128]{0:T(128)S(1)}, f32[128]{0:T(128)}, u32[]{:S(2)}) copy-start(f32[128]{0:T(128)} %param.7) | copy-start | bytes 1540

commit v9 on v8

--- a/solution.py
+++ b/solution.py
@@ -71,7 +71,7 @@
     return out
 
 
-def prepare(ctx_hbm, logged_hbm, policy_hbm, plane_ref, mine_ref, ctx_ref, logged_ref, policy_ref, sems):
+def prepare(ctx_hbm, logged_hbm, policy_hbm, plane_hbm, mine_hbm, ctx_ref, small_ref, logged_ref, policy_ref, sems, outs):
     moves = [
         pltpu.make_async_copy(source, target, sems.at[i])
         for i, (source, target) in enumerate(
@@ -85,14 +85,16 @@
     logged = jnp.concatenate(features(logged_ref[...]), axis=0)
     acts = policy_ref[...]
     codes = jnp.concatenate([acts >> 9, (acts & 511) - 256], axis=0).astype(f32)
-    small = jnp.concatenate([logged, codes], axis=0).astype(bf16)
+    small_ref[...] = jnp.concatenate([logged, codes], axis=0).astype(bf16)
     moves[0].wait()
-    ctx = ctx_ref[...]
-    for i in range(PLANES):
-        plane_ref[i, :TILE, :] = ctx
-        plane_ref[i, TILE:, :] = small
-    mine_ref[:TILE, :] = ctx
-    mine_ref[TILE:, :] = small[:NACT]
+    pairs = [(ctx_ref, plane_hbm.at[i, :TILE]) for i in range(PLANES)]
+    pairs += [(small_ref, plane_hbm.at[i, TILE:]) for i in range(PLANES)]
+    pairs += [(ctx_ref, mine_hbm.at[:TILE]), (small_ref.at[:NACT], mine_hbm.at[TILE:])]
+    sends = [pltpu.make_async_copy(source, target, outs.at[i]) for i, (source, target) in enumerate(pairs)]
+    for send in sends:
+        send.start()
+    for send in sends:
+        send.wait()
 
 
 def pieces(total):
@@ -275,12 +277,15 @@
     plane_send, mine = pl.pallas_call(
         prepare,
         in_specs=[pl.BlockSpec(memory_space=pl.ANY)] * 3,
+        out_specs=(pl.BlockSpec(memory_space=pl.ANY),) * 2,
         out_shape=(sds((PLANES, ROWS, D), bf16), sds((RIGHT_ROWS, D), bf16)),
         scratch_shapes=[
             pltpu.VMEM((TILE, D), bf16),
+            pltpu.VMEM((ROWS - TILE, D), bf16),
             pltpu.VMEM((1, TILE), i32),
             pltpu.VMEM((NPOL, TILE), i32),
             pltpu.SemaphoreType.DMA((3,)),
+            pltpu.SemaphoreType.DMA((2 * PLANES + 2,)),
         ],
         compiler_params=params(60 * MIB),
     )(contexts, logged_actions.reshape(1, TILE), policy_actions.T)

time: 91.7 us -> 91.9 us (level)
  no operation moved by 1% of the time
where the time goes in v9:
time: 91.9 us; the launch traced here: 91.6 us
  blocking collectives  49.2 us (54%)
  starting transfers between devices  23.5 us (26%)
  Pallas kernels  12.7 us (14%)
  waiting for transfers between devices  5.5 us (6%)
    all_to_all x3, blocking collectives, exchange(): return lax.all_to_all(value, axes, 0, 0)  49.2 us
    ppermute x7, starting transfers between devices, on_device(): lax.ppermute(mine, COLUMN, ring(shift))  13.1 us
    all_to_all x1, starting transfers between devices, exchange(): return lax.all_to_all(value, axes, 0, 0)  7.6 us
    ppermute x7, waiting for transfers between devices, on_device(): lax.ppermute(mine, COLUMN, ring(shift))  5.49 us
    pallas_call x1, Pallas kernels, on_device(): pl.pallas_call(second_half, in_specs=[smem] + [vmem] * (5 + COLUMNS - NEA...  3.17 us
    pallas_call x1, Pallas kernels, on_device(): pl.pallas_call(first_half, in_specs=[smem] + [vmem] * (3 + NEAR), out_sha...  3.17 us
    ppermute x1, starting transfers between devices, on_device(): other = lax.ppermute(own, 'core', [(0, 1), (1, 0)])  2.75 us
    pallas_call x1, Pallas kernels, on_device(): pl.pallas_call(prepare, in_specs=[pl.BlockSpec(memory_space=pl.ANY)] * 3,...  1.99 us
  transfers between devices with their start and end apart: 9, of which 3 were waited for; matrix products, arithmetic and copies ran while one was open for 0% of the time, Pallas kernels for 5%

profile of v9, /device:TPU:1, one launch (start us, length us, event | category | flops | bytes accessed | tf_op | source)
XLA Modules:
  0.0 91.6 jit_solution(783714616872798334)
XLA Ops:
  0.6 2.0 %shard_map.67 = (bf16[16,160,128]{2,1,0:T(8,128)(2,1)}, bf16[144,128]{1,0:T(8,128)(2,1)}) custom-call(bf16[128,128]{1,0:T(8,128)(2,1)} %ctx_hbm.1, s32[1,128]{1,0:T(1,128)} %bitcast.17, s32[8,128]{1,0:T(8,128)} %bitcast.16), custom_call_target="tpu_custom_call" | custom-call | tf_op jit(solution)/shard_map/pallas_call | solution.py:277
  2.6 7.6 %all-to-all-start = ((bf16[16,160,128]{2,1,0:T(8,128)(2,1)}), bf16[16,160,128]{2,1,0:T(8,128)(2,1)S(1)}, u32[]{:S(2)}, u32[]{:S(2)}) async-start(bf16[16,160,128]{2,1,0:T(8,128)(2,1)} %get-tuple-element.23), calls=%async_computation | async-start | bytes 1310720 | tf_op jit(solution)/shard_map/all_to_all | solution.py:266
  10.2 7.0 %collective-permute-start.3 = (bf16[144,128]{1,0:T(8,128)(2,1)}, bf16[144,128]{1,0:T(8,128)(2,1)S(1)}, u32[]{:S(2)}, u32[]{:S(2)}) collective-permute-start(bf16[144,128]{1,0:T(8,128)(2,1)} %get-tuple-element.24), channel_id=1, source_target_pairs={{0,128},{8,136},{16,144},{24,152},{128,0},{136,8},{144,16},{152,24... | collective-permute-start | bytes 110600 | tf_op jit(solution)/shard_map/ppermute | solution.py:293
  17.2 1.6 %collective-permute-start.2 = (bf16[144,128]{1,0:T(8,128)(2,1)}, bf16[144,128]{1,0:T(8,128)(2,1)S(1)}, u32[]{:S(2)}, u32[]{:S(2)}) collective-permute-start(bf16[144,128]{1,0:T(8,128)(2,1)} %get-tuple-element.24), channel_id=1, source_target_pairs={{0,24},{8,128},{16,136},{24,144},{128,152},{136,0},{144,8},{152,16... | collective-permute-start | bytes 110600 | tf_op jit(solution)/shard_map/ppermute | solution.py:293
  18.9 0.0 collective-permute-start.1
  18.9 0.3 collective-permute-start
  19.2 0.0 collective-permute-done.3.refs_0_.refs_3_
  19.2 4.6 %collective-permute-done.2.refs_2_ = bf16[144,128]{1,0:T(8,128)(2,1)S(1)} collective-permute-done((bf16[144,128]{1,0:T(8,128)(2,1)}, bf16[144,128]{1,0:T(8,128)(2,1)S(1)}, u32[]{:S(2)}, u32[]{:S(2)}) %collective-permute-start.2) | collective-permute-done | bytes 36896 | tf_op jit(solution)/shard_map/ppermute | solution.py:293
  23.8 0.6 collective-permute-done.1.refs_1_
  24.4 0.2 collective-permute-done.refs_0_
  24.7 0.0 all-to-all-done.own_ref
  24.7 2.8 %collective-permute-start.4 = (bf16[16,160,128]{2,1,0:T(8,128)(2,1)S(1)}, bf16[16,160,128]{2,1,0:T(8,128)(2,1)S(1)}, u32[]{:S(2)}, u32[]{:S(2)}) collective-permute-start(bf16[16,160,128]{2,1,0:T(8,128)(2,1)S(1)} %all-to-all-done.own_ref), channel_id=1, source_target_pairs={{0,1},{1,0},{2,3},{3,2},{4,5},{5,4},{6,7},{7,6},{8,9},{9,8},{10,11... | collective-permute-start | bytes 1966088 | tf_op jit(solution)/shard_map/ppermute | solution.py:295
  27.4 2.3 %collective-permute-start.7 = (bf16[144,128]{1,0:T(8,128)(2,1)}, bf16[144,128]{1,0:T(8,128)(2,1)S(1)}, u32[]{:S(2)}, u32[]{:S(2)}) collective-permute-start(bf16[144,128]{1,0:T(8,128)(2,1)} %get-tuple-element.24), channel_id=1, source_target_pairs={{0,152},{8,0},{16,8},{24,16},{128,24},{136,128},{144,136},{152,144... | collective-permute-start | bytes 110600 | tf_op jit(solution)/shard_map/ppermute | solution.py:293
  29.7 1.2 %collective-permute-start.6 = (bf16[144,128]{1,0:T(8,128)(2,1)}, bf16[144,128]{1,0:T(8,128)(2,1)S(1)}, u32[]{:S(2)}, u32[]{:S(2)}) collective-permute-start(bf16[144,128]{1,0:T(8,128)(2,1)} %get-tuple-element.24), channel_id=1, source_target_pairs={{0,144},{8,152},{16,0},{24,8},{128,16},{136,24},{144,128},{152,136... | collective-permute-start | bytes 110600 | tf_op jit(solution)/shard_map/ppermute | solution.py:293
  30.8 0.8 collective-permute-start.5
  31.6 0.1 pad_add_fusion.place_ref
  31.7 0.0 collective-permute-done.4.other_ref
  31.7 1.6 %shard_map.68 = (bf16[128,4096]{1,0:T(8,128)(2,1)S(1)}, bf16[32,128,128]{2,1,0:T(8,128)(2,1)S(1)}) custom-call(bf16[16,160,128]{2,1,0:T(8,128)(2,1)S(1)} %all-to-all-done.own_ref, bf16[16,160,128]{2,1,0:T(8,128)(2,1)S(1)} %collective-permute-done.4.other_ref), custom_call_target="tpu_custom_call" | custom-call | flops 60000000 | bytes 3000000 | tf_op jit(solution)/shard_map/pallas_call | solution.py:297
  33.3 3.2 %shard_map.69 = (bf16[512,4096]{1,0:T(8,128)(2,1)S(1)}, f32[4,8,128]{2,1,0:T(8,128)S(1)}) custom-call(s32[3]{0:T(128)S(1)} %pad_add_fusion.place_ref, bf16[16,160,128]{2,1,0:T(8,128)(2,1)S(1)} %all-to-all-done.own_ref, bf16[16,160,128]{2,1,0:T(8,128)(2,1)S(1)} %collective-permute-done.4.other_ref, bf16[128,4096]{1,0:T(8,128)(2,1)S(1)} %get-tuple-element.26.policy_ref, ...), custom_call_target="tpu_custom_call" | custom-call | flops 1610612736 | bytes 8388608 | tf_op jit(solution)/shard_map/pallas_call | solution.py:313
  36.5 0.0 collective-permute-done.7.refs_3_.refs_6_
  36.5 0.0 collective-permute-done.6.refs_2_.refs_5_
  36.5 0.0 collective-permute-done.5.refs_1_.refs_4_
  36.5 3.2 %shard_map.70 = (bf16[512,4096]{1,0:T(8,128)(2,1)S(1)}, f32[8,8,8,128]{3,2,1,0:T(8,128)S(1)}) custom-call(s32[3]{0:T(128)S(1)} %pad_add_fusion.place_ref, bf16[16,160,128]{2,1,0:T(8,128)(2,1)S(1)} %all-to-all-done.own_ref, bf16[16,160,128]{2,1,0:T(8,128)(2,1)S(1)} %collective-permute-done.4.other_ref, bf16[128,4096]{1,0:T(8,128)(2,1)S(1)} %get-tuple-element.26.policy_ref, ...), custom_call_target="tpu_custom_call" | custom-call | flops 1610612736 | bytes 8388608 | tf_op jit(solution)/shard_map/pallas_call | solution.py:321
  39.7 15.4 %all_to_all.20.parts_ref = f32[8,8,8,128]{3,2,1,0:T(8,128)S(1)} all-to-all(f32[8,8,8,128]{3,2,1,0:T(8,128)S(1)} %get-tuple-element.35), channel_id=1, replica_groups=mesh['z_hi'=2,'x'=4,'z_lo'=4,'y'=4,'core'=2] {'z_hi','z_lo'}, dimensions={0} | all-to-all | bytes 524288 | tf_op jit(solution)/shard_map/all_to_all | solution.py:266
  55.2 0.0 copy-start
  55.2 1.8 %shard_map.71 = (f32[32,8,128]{2,1,0:T(8,128)S(1)}, f32[8,128]{1,0:T(8,128)S(1)}) custom-call(s32[3]{0:T(128)S(1)} %pad_add_fusion.place_ref, bf16[512,4096]{1,0:T(8,128)(2,1)S(1)} %get-tuple-element.31.near_ref, bf16[512,4096]{1,0:T(8,128)(2,1)S(1)} %get-tuple-element.34.far_ref, f32[8,8,8,128]{3,2,1,0:T(8,128)S(1)} %all_to_all.20.parts_ref, ...), custom_call_target="tpu_custom_call" | custom-call | tf_op jit(solution)/shard_map/pallas_call | solution.py:330
  57.0 15.8 %all_to_all.21.parts_ref = f32[32,8,128]{2,1,0:T(8,128)S(1)} all-to-all(f32[32,8,128]{2,1,0:T(8,128)S(1)} %get-tuple-element.36), channel_id=1, replica_groups=mesh['z_hi'=2,'x'=4,'z_lo'=4,'y'=4,'core'=2] {'x','y','core'}, dimensions={0} | all-to-all | bytes 262144 | tf_op jit(solution)/shard_map/all_to_all | solution.py:266
  72.8 0.0 copy-done
  72.8 0.1 shard_map.72
  72.9 17.9 %all_to_all.22 = f32[256,1,128]{2,1,0:T(1,128)S(1)} all-to-all(f32[256,1,128]{2,1,0:T(1,128)S(1)} %bitcast.14), channel_id=1, replica_groups=mesh['z_hi'=2,'x'=4,'z_lo'=4,'y'=4,'core'=2] {'z_hi','x','z_lo','y','core'}, dimensions={0} | all-to-all | bytes 262144 | tf_op jit(solution)/shard_map/all_to_all | solution.py:266
  90.9 0.7 shard_map.73
Async XLA Ops:
  2.6 22.0 %all-to-all-start = ((bf16[16,160,128]{2,1,0:T(8,128)(2,1)}), bf16[16,160,128]{2,1,0:T(8,128)(2,1)S(1)}, u32[]{:S(2)}, u32[]{:S(2)}) async-start(bf16[16,160,128]{2,1,0:T(8,128)(2,1)} %get-tuple-element.23), calls=%async_computation | async-start | bytes 1310720 | tf_op jit(solution)/shard_map/all_to_all | solution.py:266
  10.2 8.9 %collective-permute-start.3 = (bf16[144,128]{1,0:T(8,128)(2,1)}, bf16[144,128]{1,0:T(8,128)(2,1)S(1)}, u32[]{:S(2)}, u32[]{:S(2)}) collective-permute-start(bf16[144,128]{1,0:T(8,128)(2,1)} %get-tuple-element.24), channel_id=1, source_target_pairs={{0,128},{8,136},{16,144},{24,152},{128,0},{136,8},{144,16},{152,24... | collective-permute-start | bytes 110600 | tf_op jit(solution)/shard_map/ppermute | solution.py:293
  17.2 6.6 %collective-permute-start.2 = (bf16[144,128]{1,0:T(8,128)(2,1)}, bf16[144,128]{1,0:T(8,128)(2,1)S(1)}, u32[]{:S(2)}, u32[]{:S(2)}) collective-permute-start(bf16[144,128]{1,0:T(8,128)(2,1)} %get-tuple-element.24), channel_id=1, source_target_pairs={{0,24},{8,128},{16,136},{24,144},{128,152},{136,0},{144,8},{152,16... | collective-permute-start | bytes 110600 | tf_op jit(solution)/shard_map/ppermute | solution.py:293
  18.9 5.5 %collective-permute-start.1 = (bf16[144,128]{1,0:T(8,128)(2,1)}, bf16[144,128]{1,0:T(8,128)(2,1)S(1)}, u32[]{:S(2)}, u32[]{:S(2)}) collective-permute-start(bf16[144,128]{1,0:T(8,128)(2,1)} %get-tuple-element.24), channel_id=1, source_target_pairs={{0,16},{8,24},{16,128},{24,136},{128,144},{136,152},{144,0},{152,8... | collective-permute-start | bytes 110600 | tf_op jit(solution)/shard_map/ppermute | solution.py:293
  18.9 5.8 %collective-permute-start = (bf16[144,128]{1,0:T(8,128)(2,1)}, bf16[144,128]{1,0:T(8,128)(2,1)S(1)}, u32[]{:S(2)}, u32[]{:S(2)}) collective-permute-start(bf16[144,128]{1,0:T(8,128)(2,1)} %get-tuple-element.24), channel_id=1, source_target_pairs={{0,8},{8,16},{16,24},{24,128},{128,136},{136,144},{144,152},{152,0... | collective-permute-start | bytes 110600 | tf_op jit(solution)/shard_map/ppermute | solution.py:293
  24.7 7.0 %collective-permute-start.4 = (bf16[16,160,128]{2,1,0:T(8,128)(2,1)S(1)}, bf16[16,160,128]{2,1,0:T(8,128)(2,1)S(1)}, u32[]{:S(2)}, u32[]{:S(2)}) collective-permute-start(bf16[16,160,128]{2,1,0:T(8,128)(2,1)S(1)} %all-to-all-done.own_ref), channel_id=1, source_target_pairs={{0,1},{1,0},{2,3},{3,2},{4,5},{5,4},{6,7},{7,6},{8,9},{9,8},{10,11... | collective-permute-start | bytes 1966088 | tf_op jit(solution)/shard_map/ppermute | solution.py:295
  27.4 9.1 %collective-permute-start.7 = (bf16[144,128]{1,0:T(8,128)(2,1)}, bf16[144,128]{1,0:T(8,128)(2,1)S(1)}, u32[]{:S(2)}, u32[]{:S(2)}) collective-permute-start(bf16[144,128]{1,0:T(8,128)(2,1)} %get-tuple-element.24), channel_id=1, source_target_pairs={{0,152},{8,0},{16,8},{24,16},{128,24},{136,128},{144,136},{152,144... | collective-permute-start | bytes 110600 | tf_op jit(solution)/shard_map/ppermute | solution.py:293
  29.7 6.9 %collective-permute-start.6 = (bf16[144,128]{1,0:T(8,128)(2,1)}, bf16[144,128]{1,0:T(8,128)(2,1)S(1)}, u32[]{:S(2)}, u32[]{:S(2)}) collective-permute-start(bf16[144,128]{1,0:T(8,128)(2,1)} %get-tuple-element.24), channel_id=1, source_target_pairs={{0,144},{8,152},{16,0},{24,8},{128,16},{136,24},{144,128},{152,136... | collective-permute-start | bytes 110600 | tf_op jit(solution)/shard_map/ppermute | solution.py:293
  30.8 5.7 %collective-permute-start.5 = (bf16[144,128]{1,0:T(8,128)(2,1)}, bf16[144,128]{1,0:T(8,128)(2,1)S(1)}, u32[]{:S(2)}, u32[]{:S(2)}) collective-permute-start(bf16[144,128]{1,0:T(8,128)(2,1)} %get-tuple-element.24), channel_id=1, source_target_pairs={{0,136},{8,144},{16,152},{24,0},{128,8},{136,16},{144,24},{152,128... | collective-permute-start | bytes 110600 | tf_op jit(solution)/shard_map/ppermute | solution.py:293
  55.2 17.7 %copy-start = (f32[128]{0:T(128)S(1)}, f32[128]{0:T(128)}, u32[]{:S(2)}) copy-start(f32[128]{0:T(128)} %param.7) | copy-start | bytes 1540
